TPU v7x, 128 devices: a whole 4x4x4 slice. The times are simulated.
128 devices in a mesh: grp: 4 (over z_lo, core), feat: 32 (over x, y, z_hi).
Axes of the slice: x: 4, y: 4, z: 4 (z_hi: 2, z_lo: 2; z = z_hi * 2 + z_lo), core: 2. Of those that a mesh axis runs over, the one named last changes fastest.
Arguments:
- resid: bfloat16 [4, 512, 4096], P('grp', 'feat'), may hold values from -600 to 600
- norm_gain: float32 [4, 4096], P('grp'), may hold values from 0.25 to 1.75
- w_gate: bfloat16 [4, 4096, 14336], P('grp', None, 'feat'), may hold values from -0.09375 to 0.09375
- w_up: bfloat16 [4, 4096, 14336], P('grp', None, 'feat'), may hold values from -0.09375 to 0.09375
- w_down: bfloat16 [4, 14336, 4096], P('grp', 'feat'), may hold values from -0.046875 to 0.046875
- w_enc: bfloat16 [4, 4096, 16384], P('grp', None, 'feat'), may hold values from -0.09375 to 0.09375
- b_enc: float32 [4, 16384], P('grp', 'feat'), may hold values from -0.8 to 0.2
- w_dec: bfloat16 [4, 16384, 8192], P('grp', 'feat'), may hold values from -0.046875 to 0.046875
- carry_in: float32 [512, 4096], P('feat'), may hold values from -3 to 3
Outputs:
- errors: float32 [4, 512, 4096], P('grp', 'feat')
- forward: float32 [4, 512, 4096], P('grp', 'feat')
All inputs are finite; a program needn't handle non-finite values.
Results may differ from a plain program's by a relative error of at most 0.0044.
Values may be sent and summed in bfloat16 or wider, within the bound.
No kernel may reach another device: no remote copies, remote signals or barrier semaphores. Data moves between devices by JAX's collectives and lax.ppermute only.
A program may use at most 128 MiB of HBM per device.

v0:
```python
import jax
import jax.numpy as jnp
from jax import lax
from jax.sharding import Mesh
from jax.sharding import PartitionSpec as P

FEAT = ("feat_0", "feat_1", "feat_2")


def own_rows(total, axes):
    for axis in axes:
        total = lax.psum_scatter(total, axis, scatter_dimension=0, tiled=True)
    return total


def passed_along(value, axis, steps):
    count = lax.axis_size(axis)
    initial, last = (max(0, -steps), min(count, count - steps))
    return lax.ppermute(value, axis, [(source, source + steps) for source in range(initial, last)])


def body(resid, norm_gain, w_gate, w_up, w_down, w_enc, b_enc, w_dec, carry_in):
    stream = resid[0].astype(jnp.float32)
    inv_rms = lax.rsqrt(jnp.mean(stream * stream, axis=1, keepdims=True) + 1e-05)
    normed = (stream * inv_rms * norm_gain[0]).astype(jnp.bfloat16)
    gate_cols = w_gate[0]
    up_cols = w_up[0]
    enc_cols = w_enc[0]
    enc_bias = b_enc[0]
    hidden_width = gate_cols.shape[1]
    tile_rows = lax.all_gather(normed, FEAT, axis=0, tiled=True)
    gate_sum = jnp.dot(tile_rows, gate_cols, preferred_element_type=jnp.float32)
    up_sum = jnp.dot(tile_rows, up_cols, preferred_element_type=jnp.float32)
    hidden_part = (jax.nn.silu(gate_sum) * up_sum).astype(jnp.bfloat16)
    pre_act = jnp.dot(tile_rows, enc_cols, preferred_element_type=jnp.float32) + enc_bias
    feature_part = jax.nn.relu(pre_act).astype(jnp.bfloat16)
    joined = jnp.concatenate([hidden_part, feature_part], axis=1)
    hidden = joined[:, :hidden_width]
    features = joined[:, hidden_width:]
    down_rows = w_down[0]
    dec_rows = w_dec[0]
    model_width = down_rows.shape[1]
    dec_part = jnp.dot(features, dec_rows, preferred_element_type=jnp.float32)
    mlp_part = jnp.dot(hidden, down_rows, preferred_element_type=jnp.float32)
    decoded = own_rows(
        jnp.concatenate([dec_part[:, :model_width] - mlp_part, dec_part[:, model_width:]], axis=1),
        FEAT,
    )
    own_error = decoded[:, :model_width]
    to_next = decoded[:, model_width:]
    passed = passed_along(to_next, "grp", 1)
    incoming = jnp.where(lax.axis_index("grp") == 0, carry_in, passed)
    err_rows = own_error + incoming
    return (err_rows[None], to_next[None])


def solution(mesh):
    finer = Mesh(
        mesh.devices.reshape(mesh.shape["grp"], 4, 4, 2), ("grp", "feat_0", "feat_1", "feat_2")
    )
    return jax.shard_map(
        body,
        mesh=finer,
        in_specs=(
            P("grp", FEAT, None),
            P("grp", None),
            P("grp", None, FEAT),
            P("grp", None, FEAT),
            P("grp", FEAT, None),
            P("grp", None, FEAT),
            P("grp", FEAT),
            P("grp", FEAT, None),
            P(FEAT, None),
        ),
        out_specs=(P("grp", FEAT, None), P("grp", FEAT, None)),
        check_vma=False,
    )
```

profile of v0, /device:TPU:1, one launch (start us, length us, event | category | flops | bytes accessed | tf_op | source)
XLA Modules:
  0.0 386.6 jit_solution(16722595887475284601)
XLA Ops:
  7.2 0.0 all-gather.2.cloned.1.call-start
  7.2 1.1 fusion.24
  8.3 1.7 fusion.26
  9.9 0.0 all-gather.2.cloned.1.call-update
  10.0 0.0 reduce-scatter.4.cloned.1.call-start
  10.0 85.7 %all-gather.2.cloned.1.call-done = bf16[512,4096]{1,0:T(8,128)(2,1)} async-done(((bf16[16,4096]{1,0:T(8,128)(2,1)}), bf16[512,4096]{1,0:T(8,128)(2,1)}) %all-gather.2.cloned.1.call-update) | async-done | bytes 4194320 | tf_op jit(solution)/shard_map/all_gather | solution.py:31
  95.7 5.8 %fusion.18 = bf16[512,512]{1,0:T(8,128)(2,1)S(1)} fusion(bf16[512,4096]{1,0:T(8,128)(2,1)} %all-gather.2.cloned.1.call-done, bf16[1,4096,512]{2,1,0:T(8,128)(2,1)} %param.14, f32[512]{0:T(512)} %bitcast.49), kind=kOutput, calls=%fused_computation.14 | convolution fusion | flops 2148270080 | bytes 8914944 | tf_op jit(solution)/shard_map/dot_general | solution.py:35
  101.5 7.1 %fusion = f32[512,8192]{1,0:T(8,128)S(1)} fusion(bf16[512,512]{1,0:T(8,128)(2,1)S(1)} %fusion.18, bf16[1,512,8192]{2,1,0:T(8,128)(2,1)} %param.16), kind=kOutput, calls=%fused_computation.2 | convolution fusion | flops 4294967296 | bytes 25690112 | tf_op jit(solution)/shard_map/dot_general | solution.py:43
  108.6 0.0 copy-start
  108.6 0.0 copy-start.1
  108.6 4.4 %slice.17 = f32[512,4096]{1,0:T(8,128)} slice(f32[512,8192]{1,0:T(8,128)S(1)} %fusion), slice={[0:512], [4096:8192]} | slice | bytes 16777216 | tf_op jit(solution)/shard_map/slice | solution.py:46
  113.0 5.2 %copy-done = f32[512,8192]{1,0:T(8,128)} copy-done((f32[512,8192]{1,0:T(8,128)}, f32[512,8192]{1,0:T(8,128)S(1)}, u32[]{:S(2)}) %copy-start) | copy-done | bytes 16777240
  118.2 0.0 copy-done.1
  118.2 4.3 %fusion.7 = f32[512,448]{0,1:T(8,128)S(1)} fusion(bf16[512,4096]{1,0:T(8,128)(2,1)S(1)} %copy-done.1, bf16[1,4096,448]{1,2,0:T(8,128)(2,1)} %param.11), kind=kOutput, calls=%fused_computation.9 | convolution fusion | flops 1879048192 | bytes 8781824 | tf_op jit(solution)/shard_map/dot_general | solution.py:32
  122.5 14.4 %slice_subtract_fusion = f32[512,4096]{1,0:T(8,128)} fusion(f32[512,8192]{1,0:T(8,128)} %copy-done, bf16[1,448,4096]{2,1,0:T(8,128)(2,1)} %param.13, bf16[512,4096]{1,0:T(8,128)(2,1)} %all-gather.2.cloned.1.call-done, bf16[1,4096,448]{1,2,0:T(8,128)(2,1)} %param.12, f32[512,448]{0,1:T(8,128)S(1)} %fusion.7), kind=kOutput, calls=%fused_computation.1 | convolution fusion | flops 3761569792 | bytes 29229056 | tf_op jit(solution)/shard_map/dot_general | solution.py:44
  136.9 11.5 %pad_maximum_fusion = f32[512,8192]{1,0:T(8,128)} fusion(f32[512,4096]{1,0:T(8,128)} %slice.17, f32[512,4096]{1,0:T(8,128)} %slice_subtract_fusion), kind=kLoop, calls=%fused_computation | loop fusion | flops 4194304 | bytes 33554432 | tf_op jit(solution)/shard_map/concatenate | solution.py:46
  148.5 0.0 reduce-scatter.4.cloned.1.call-update
  148.5 0.0 copy-start.2
  148.5 0.0 reduce-scatter.6.cloned.1.call-start
  148.6 146.4 %reduce-scatter.4.cloned.1.call-done = f32[128,8192]{1,0:T(8,128)} async-done(((f32[512,8192]{1,0:T(8,128)}), f32[128,8192]{1,0:T(8,128)}) %reduce-scatter.4.cloned.1.call-update) | async-done | bytes 4194320 | tf_op jit(solution)/shard_map/reduce_scatter | solution.py:12
  295.0 0.0 reduce-scatter.6.cloned.1.call-update
  295.0 0.0 reduce-scatter.8.cloned.1.call-start
  295.0 49.1 %reduce-scatter.6.cloned.1.call-done = f32[32,8192]{1,0:T(8,128)} async-done(((f32[128,8192]{1,0:T(8,128)}), f32[32,8192]{1,0:T(8,128)}) %reduce-scatter.6.cloned.1.call-update) | async-done | bytes 1048592 | tf_op jit(solution)/shard_map/reduce_scatter | solution.py:12
  344.1 0.0 reduce-scatter.8.cloned.1.call-update
  344.1 26.4 %reduce-scatter.8.cloned.1.call-done = f32[16,8192]{1,0:T(8,128)} async-done(((f32[32,8192]{1,0:T(8,128)}), f32[16,8192]{1,0:T(8,128)}) %reduce-scatter.8.cloned.1.call-update) | async-done | bytes 524304 | tf_op jit(solution)/shard_map/reduce_scatter | solution.py:12
  370.5 1.7 slice_bitcast_fusion
  372.2 2.9 collective-permute-start
  375.1 3.3 collective-permute-done
  378.4 0.0 copy-done.2
  378.4 1.7 fusion.27
  (1 shorter events, 0.0 us)
Async XLA Ops:
  7.2 88.6 %all-gather.2.cloned.1.call-start = ((), (), s32[]{:S(2)}) async-start(), calls=%async_computation.3 | async-start | bytes 4325376 | tf_op jit(solution)/shard_map/all_gather | solution.py:31
  10.0 285.0 %reduce-scatter.4.cloned.1.call-start = ((), (), s32[]{:S(2)}) async-start(), calls=%async_computation.4 | async-start | bytes 20971520 | tf_op jit(solution)/shard_map/reduce_scatter | solution.py:12
  108.6 9.6 %copy-start = (f32[512,8192]{1,0:T(8,128)}, f32[512,8192]{1,0:T(8,128)S(1)}, u32[]{:S(2)}) copy-start(f32[512,8192]{1,0:T(8,128)S(1)} %fusion) | copy-start | bytes 50331652
  108.6 9.6 %copy-start.1 = (bf16[512,4096]{1,0:T(8,128)(2,1)S(1)}, bf16[512,4096]{1,0:T(8,128)(2,1)}, u32[]{:S(2)}) copy-start(bf16[512,4096]{1,0:T(8,128)(2,1)} %all-gather.2.cloned.1.call-done) | copy-start | bytes 12582916
  148.5 229.9 %copy-start.2 = (f32[16,4096]{1,0:T(8,128)S(1)}, f32[16,4096]{1,0:T(8,128)}, u32[]{:S(2)}) copy-start(f32[16,4096]{1,0:T(8,128)} %param.17) | copy-start | bytes 786436
  148.5 195.6 %reduce-scatter.6.cloned.1.call-start = ((), (), s32[]{:S(2)}) async-start(), calls=%async_computation.5 | async-start | bytes 5242880 | tf_op jit(solution)/shard_map/reduce_scatter | solution.py:12
  295.0 75.5 %reduce-scatter.8.cloned.1.call-start = ((), (), s32[]{:S(2)}) async-start(), calls=%async_computation.6 | async-start | bytes 1572864 | tf_op jit(solution)/shard_map/reduce_scatter | solution.py:12
  372.2 6.2 %collective-permute-start = (f32[16,4096]{1,0:T(8,128)S(1)}, f32[16,4096]{1,0:T(8,128)S(1)}, u32[]{:S(2)}, u32[]{:S(2)}) collective-permute-start(f32[16,4096]{1,0:T(8,128)S(1)} %get-tuple-element.3), channel_id=1, source_target_pairs={{0,32},{32,64},{64,96},{1,33},{33,65},{65,97},{2,34},{34,66},{66,9... | collective-permute-start | bytes 786440 | tf_op jit(solution)/shard_map/ppermute | solution.py:19
Sparse Core Ops, SparseCore 0:
  11.6 84.1 all-gather.1
  148.6 146.3 reduce-scatter.3
  297.5 46.5 reduce-scatter.5
  346.3 24.1 reduce-scatter.7
where the time goes:
time: 387 us
  waiting for transfers between devices  311 us (80%)
  matrix products  31.6 us (8%)
  other arithmetic  16 us (4%)
  between operations  13.8 us (4%)
  local copies, waits for them, and re-layouts  11.3 us (3%)
    reduce_scatter x3, waiting for transfers between devices, own_rows(): total = lax.psum_scatter(total, axis, scatter_dimension=0, tiled=True)  222 us
    all_gather x1, waiting for transfers between devices, body(): tile_rows = lax.all_gather(normed, FEAT, axis=0, tiled=True)  85.7 us
    dot_general x1, matrix products, body(): mlp_part = jnp.dot(hidden, down_rows, preferred_element_type=jnp.float32)  14.4 us
    concatenate x1, other arithmetic, body(): jnp.concatenate([dec_part[:, :model_width] - mlp_part, dec_part[:, model_...  11.5 us
  transfers between devices with their start and end apart: 5, of which 5 were waited for; matrix products, arithmetic and copies ran while one was open for 0% of the time, Pallas kernels for 0%

commit v1 on v0

v1 whole, which is shorter than its diff:
```python
import functools

import jax
import jax.numpy as jnp
from jax import lax
from jax.experimental import pallas as pl
from jax.experimental.pallas import tpu as pltpu
from jax.sharding import Mesh
from jax.sharding import PartitionSpec as P

FX, FY, FZ = "feat_0", "feat_1", "feat_2"
FEAT = (FX, FY, FZ)
BF = jnp.bfloat16
F32 = jnp.float32
VMEM = pl.BlockSpec(memory_space=pltpu.VMEM)
HBM = pl.BlockSpec(memory_space=pl.ANY)
CHEAP = pl.CostEstimate(flops=1, bytes_accessed=1, transcendentals=0)


def fetch(value, axis, ahead):
    count = lax.axis_size(axis)
    return lax.ppermute(value, axis, [((i + ahead) % count, i) for i in range(count)])


def tie(*values):
    return lax.optimization_barrier(values)


def dot(a, b):
    return jnp.dot(a, b, preferred_element_type=F32)


def dot_t(a, b):
    return lax.dot_general(a, b, (((1,), (1,)), ((), ())), preferred_element_type=F32)


def ring_gather(block, axis):
    return [block] + [fetch(block, axis, r) for r in (1, 2, 3)]


def block_orders(rows):
    own = lambda x, y: (y * 4 + x) * rows
    oth = lambda x, y: (16 + x * 4 + y) * rows
    x_first = [f(x, y) for x in range(4) for y in range(4) for f in (own, oth)]
    y_first = [f(x, y) for y in range(4) for x in range(4) for f in (own, oth)]
    return x_first, y_first


def place(act, rows, out_x, out_y):
    x_first, y_first = block_orders(rows)
    for out, order in ((out_x, x_first), (out_y, y_first)):
        for at, start in enumerate(order):
            out[at * rows:(at + 1) * rows, :] = act[start:start + rows, :]


def chunked(src, dst, sems, base, count):
    size = dst.shape[0] // count
    return [
        pltpu.make_async_copy(
            src.at[pl.ds(i * size, size), :], dst.at[pl.ds(i * size, size), :], sems.at[base + i])
        for i in range(count)
    ]


def write_parts(products, outs):
    for side in range(2):
        up, down, one, three, own = outs[side * 5:side * 5 + 5]
        far = products(2, side).astype(BF)
        mid = far.shape[0] // 2
        up[...] = far[:mid]
        down[...] = far[mid:]
        one[...] = products(1, side)
        three[...] = products(3, side)
        own[...] = products(0, side)


def part_shapes(block, half):
    far = jax.ShapeDtypeStruct((block // 2, half), BF)
    near = jax.ShapeDtypeStruct((block, half), F32)
    return [far, far, near, near, near] * 2


def fwd_kernel(rows, *refs):
    pieces, (enc, bias, dec), outs = refs[:8], refs[8:11], refs[11:21]
    feat_x, feat_y = refs[21:23]
    enc_v, dec_v, act, sems = refs[23:]
    width = enc_v.shape[0]
    copies = chunked(enc, enc_v, sems, 0, 4)
    dec_copy = pltpu.make_async_copy(dec.at[:, pl.ds(width, width)], dec_v, sems.at[4])
    for copy in copies:
        copy.start()
    dec_copy.start()
    step = width // 4
    total = None
    for i, copy in enumerate(copies):
        copy.wait()
        tokens = jnp.concatenate([p[:, i * step:(i + 1) * step] for p in pieces], axis=0)
        part = dot(tokens, enc_v[i * step:(i + 1) * step, :])
        total = part if total is None else total + part
    act[...] = jnp.maximum(total + bias[...], 0.0).astype(BF)
    place(act, rows, feat_x, feat_y)
    dec_copy.wait()
    half = width // 2
    block = 8 * rows

    def products(r, side):
        feat = (feat_x, feat_y)[side]
        return dot(feat[r * block:(r + 1) * block, :], dec_v[:, side * half:(side + 1) * half])

    write_parts(products, outs)


def err_kernel(rows, *refs):
    pieces, (feat_x, feat_y, gate, up, down, dec), outs = refs[:8], refs[8:14], refs[14:24]
    gate_v, up_v, down_v, dec_v, act, hid_x, hid_y, sems = refs[24:]
    width = gate_v.shape[1]
    hidden = gate_v.shape[0]
    copies = [
        pltpu.make_async_copy(gate, gate_v, sems.at[0]),
        pltpu.make_async_copy(up, up_v, sems.at[1]),
        pltpu.make_async_copy(down, down_v, sems.at[2]),
        pltpu.make_async_copy(dec.at[:, pl.ds(0, width)], dec_v, sems.at[3]),
    ]
    for copy in copies:
        copy.start()
    copies[0].wait()
    tokens = jnp.concatenate([p[...] for p in pieces], axis=0)
    gates = dot_t(tokens, gate_v[...])
    copies[1].wait()
    ups = dot_t(tokens, up_v[...])
    act[...] = (gates / (1.0 + jnp.exp(-gates)) * ups).astype(BF)
    place(act, rows, hid_x, hid_y)
    copies[2].wait()
    copies[3].wait()
    half = width // 2
    block = 8 * rows

    def products(r, side):
        feat, hid = ((feat_x, hid_x), (feat_y, hid_y))[side]
        at = slice(r * block, (r + 1) * block)
        cols = slice(side * half, (side + 1) * half)
        return dot(feat[at, :], dec_v[:, cols]) - dot(hid[at, :], down_v[:, cols])

    write_parts(products, outs)


def hop_far(parts, axis):
    return fetch(parts[0], axis, -1), fetch(parts[1], axis, 1)


def hop_near(parts, arrived, axis):
    up, down = (v.astype(F32) for v in arrived)
    zeros = jnp.zeros_like(up)
    ahead = parts[2] + jnp.concatenate([up, zeros], axis=0)
    behind = parts[3] + jnp.concatenate([zeros, down], axis=0)
    return fetch(ahead.astype(BF), axis, -1), fetch(behind.astype(BF), axis, 1)


def total_of(own, arrived):
    for value in arrived:
        own = own + value.astype(F32)
    return own


def split_rows(array, count):
    rows = array.shape[0] // count
    return [array[i * rows:(i + 1) * rows] for i in range(count)]


def direct(total, axis):
    parts = split_rows(total, 4)
    return parts[0], [fetch(parts[r].astype(BF), axis, -r) for r in (1, 2, 3)]


def body(resid, norm_gain, w_gate, w_up, w_down, w_enc, b_enc, w_dec, carry_in):
    rows = resid.shape[1]
    width = resid.shape[2]
    half = width // 2
    block = 8 * rows
    total_rows = 32 * rows
    stream = resid[0].astype(F32)
    inv_rms = lax.rsqrt(jnp.mean(stream * stream, axis=1, keepdims=True) + 1e-05)
    normed = (stream * inv_rms * norm_gain[0]).astype(BF)

    other = fetch(normed, FZ, 1)
    plane = jnp.concatenate(ring_gather(normed, FX), axis=0)
    other_plane = jnp.concatenate(ring_gather(other, FY), axis=0)
    plane, other_plane = tie(plane, other_plane)
    pieces = ring_gather(plane, FY) + ring_gather(other_plane, FX)

    enc, dec = w_enc[0], w_dec[0]
    features = enc.shape[1]
    shapes = part_shapes(block, half)
    order = jax.ShapeDtypeStruct((total_rows, features), BF)
    params = pltpu.CompilerParams(vmem_limit_bytes=40 << 20)
    *fwd, feat_x, feat_y = pl.pallas_call(
        functools.partial(fwd_kernel, rows),
        out_shape=shapes + [order, order],
        in_specs=[VMEM] * 8 + [HBM, VMEM, HBM],
        out_specs=[VMEM] * 12,
        scratch_shapes=[
            pltpu.VMEM(enc.shape, BF),
            pltpu.VMEM((features, width), BF),
            pltpu.VMEM((total_rows, features), BF),
            pltpu.SemaphoreType.DMA((5,)),
        ],
        compiler_params=params,
        cost_estimate=CHEAP,
        name="enc_fwd",
    )(*pieces, enc, b_enc, dec)
    fa, fb = fwd[:5], fwd[5:]

    hidden = w_gate.shape[2]
    err = pl.pallas_call(
        functools.partial(err_kernel, rows),
        out_shape=shapes,
        in_specs=[VMEM] * 10 + [HBM] * 4,
        out_specs=[VMEM] * 10,
        scratch_shapes=[
            pltpu.VMEM((hidden, width), BF),
            pltpu.VMEM((hidden, width), BF),
            pltpu.VMEM((hidden, width), BF),
            pltpu.VMEM((features, width), BF),
            pltpu.VMEM((total_rows, hidden), BF),
            pltpu.VMEM((total_rows, hidden), BF),
            pltpu.VMEM((total_rows, hidden), BF),
            pltpu.SemaphoreType.DMA((4,)),
        ],
        compiler_params=pltpu.CompilerParams(vmem_limit_bytes=48 << 20),
        cost_estimate=CHEAP,
        name="mlp_err",
    )(*pieces, feat_x, feat_y, w_gate[0].T, w_up[0].T, w_down[0], dec)
    ea, eb = err[:5], err[5:]

    f1a, f1b = hop_far(fa, FX), hop_far(fb, FY)
    e1a, e1b = hop_far(ea, FX), hop_far(eb, FY)
    f2a, f2b = hop_near(fa, f1a, FX), hop_near(fb, f1b, FY)
    e2a, e2b = hop_near(ea, e1a, FX), hop_near(eb, e1b, FY)
    sum_a = jnp.concatenate([total_of(fa[4], f2a), total_of(ea[4], e2a)], axis=1)
    sum_b = jnp.concatenate([total_of(fb[4], f2b), total_of(eb[4], e2b)], axis=1)
    da, db = direct(sum_a, FY), direct(sum_b, FX)
    low_a, low_b = total_of(*da), total_of(*db)

    def finish(cols):
        low = jnp.concatenate([low_a[:, cols], low_b[:, cols]], axis=1)
        own, oth = split_rows(low, 2)
        return own + fetch(oth.astype(BF), FZ, 1).astype(F32)

    to_next = finish(slice(0, half))
    count = lax.axis_size("grp")
    passed = lax.ppermute(to_next, "grp", [(i, i + 1) for i in range(count - 1)])
    incoming = jnp.where(lax.axis_index("grp") == 0, carry_in, passed)
    return ((finish(slice(half, width)) + incoming)[None], to_next[None])


def solution(mesh):
    finer = Mesh(
        mesh.devices.reshape(mesh.shape["grp"], 4, 4, 2), ("grp", FX, FY, FZ)
    )
    return jax.shard_map(
        body,
        mesh=finer,
        in_specs=(
            P("grp", FEAT, None),
            P("grp", None),
            P("grp", None, FEAT),
            P("grp", None, FEAT),
            P("grp", FEAT, None),
            P("grp", None, FEAT),
            P("grp", FEAT),
            P("grp", FEAT, None),
            P(FEAT, None),
        ),
        out_specs=(P("grp", FEAT, None), P("grp", FEAT, None)),
        check_vma=False,
    )
```

time: 387 us -> 160 us (0.41)
  waiting for transfers between devices: 311 us -> 54.2 us
  starting transfers between devices: 3.01 us -> 78.3 us
  matrix products: 31.6 us -> 0 us
  Pallas kernels: 0 us -> 20.3 us
  between operations: 13.8 us -> 1.04 us
  other arithmetic: 16 us -> 4.86 us
  local copies, waits for them, and re-layouts: 11.3 us -> 1.01 us
    reduce_scatter x3 -> x0, waiting for transfers between devices: 222 us -> none  [own_rows(): total = lax.psum_scatter(total, axis, scatter_dimension=0, tiled=True)]
    all_gather x1 -> x0, waiting for transfers between devices: 85.7 us -> none  [body(): tile_rows = lax.all_gather(normed, FEAT, axis=0, tiled=True)]
    ppermute x1 -> x38, starting transfers between devices: 2.85 us -> 78.3 us  [the longest x37 58.3 us: fetch(): lax.ppermute(value, axis, [((i + ahead) % count, i) for i in range(count)])]
    ppermute x1 -> x38, waiting for transfers between devices: 3.29 us -> 54.2 us  [the longest x37 54.2 us: fetch(): lax.ppermute(value, axis, [((i + ahead) % count, i) for i in range(count)])]
    dot_general x4 -> x0, matrix products: 31.6 us -> none  [the longest x1 14.4 us: body(): mlp_part = jnp.dot(hidden, down_rows, preferred_element_type=jnp.float32)]
    pallas_call x0 -> x2, Pallas kernels: none -> 20.3 us  [the longest x1 13.7 us: body(): pl.pallas_call(functools.partial(err_kernel, rows), out_shape=shapes, in_...]
    concatenate x1 -> x2, other arithmetic: 11.5 us -> 0.07 us  [the longest x1 0.03 us: body(): plane = jnp.concatenate(ring_gather(normed, FX), axis=0)]
    unnamed x6 -> x20, local copies, waits for them, and re-layouts: 5.16 us -> 0.83 us
  transfers between devices with their start and end apart: 5 -> 38, of which waited for: 5 -> 18; matrix products, arithmetic and copies ran while one was open for 0% -> 1% of each run, Pallas kernels for 0% -> 9%
where the time goes in v1:
time: 160 us
  starting transfers between devices  78.3 us (49%)
  waiting for transfers between devices  54.2 us (34%)
  Pallas kernels  20.3 us (13%)
  other arithmetic  4.86 us (3%)
    ppermute x37, starting transfers between devices, fetch(): lax.ppermute(value, axis, [((i + ahead) % count, i) for i in range(count)])  58.3 us
    ppermute x37, waiting for transfers between devices, fetch(): lax.ppermute(value, axis, [((i + ahead) % count, i) for i in range(count)])  54.2 us
    ppermute x1, starting transfers between devices, body(): lax.ppermute(to_next, 'grp', [(i, i + 1) for i in range(count - 1)])  20 us
    pallas_call x1, Pallas kernels, body(): pl.pallas_call(functools.partial(err_kernel, rows), out_shape=shapes, in_...  13.7 us
    pallas_call x1, Pallas kernels, body(): pl.pallas_call(functools.partial(fwd_kernel, rows), out_shape=shapes + [o...  6.63 us
  transfers between devices with their start and end apart: 38, of which 18 were waited for; matrix products, arithmetic and copies ran while one was open for 1% of the time, Pallas kernels for 9%

profile of v1, /device:TPU:1, one launch (start us, length us, event | category | flops | bytes accessed | tf_op | source)
XLA Modules:
  0.0 159.7 jit_solution(3348539868742858137)
XLA Ops:
  2.7 4.5 %collective-permute-start.3 = (bf16[16,4096]{1,0:T(8,128)(2,1)S(1)}, bf16[16,4096]{1,0:T(8,128)(2,1)S(1)}, u32[]{:S(2)}, u32[]{:S(2)}) collective-permute-start(bf16[16,4096]{1,0:T(8,128)(2,1)S(1)} %fusion.12), channel_id=1, source_target_pairs={{1,0},{0,1},{3,2},{2,3},{5,4},{4,5},{7,6},{6,7},{9,8},{8,9},{11,10... | collective-permute-start | bytes 393224 | tf_op jit(solution)/shard_map/ppermute | solution.py:22
  8.4 2.5 %collective-permute-start.1 = (bf16[16,4096]{1,0:T(8,128)(2,1)S(1)}, bf16[16,4096]{1,0:T(8,128)(2,1)S(1)}, u32[]{:S(2)}, u32[]{:S(2)}) collective-permute-start(bf16[16,4096]{1,0:T(8,128)(2,1)S(1)} %fusion.12), channel_id=1, source_target_pairs={{16,0},{24,8},{0,16},{8,24},{17,1},{25,9},{1,17},{9,25},{18,2},{26... | collective-permute-start | bytes 393224 | tf_op jit(solution)/shard_map/ppermute | solution.py:22
  13.3 2.6 %collective-permute-start.5 = (bf16[16,4096]{1,0:T(8,128)(2,1)S(1)}, bf16[16,4096]{1,0:T(8,128)(2,1)S(1)}, u32[]{:S(2)}, u32[]{:S(2)}) collective-permute-start(bf16[16,4096]{1,0:T(8,128)(2,1)S(1)} %collective-permute-done.3), channel_id=1, source_target_pairs={{4,0},{6,2},{0,4},{2,6},{5,1},{7,3},{1,5},{3,7},{12,8},{14,10},{8,... | collective-permute-start | bytes 393224 | tf_op jit(solution)/shard_map/ppermute | solution.py:22
  17.4 2.8 %collective-permute-done.5 = bf16[16,4096]{1,0:T(8,128)(2,1)S(1)} collective-permute-done((bf16[16,4096]{1,0:T(8,128)(2,1)S(1)}, bf16[16,4096]{1,0:T(8,128)(2,1)S(1)}, u32[]{:S(2)}, u32[]{:S(2)}) %collective-permute-start.5) | collective-permute-done | bytes 131104 | tf_op jit(solution)/shard_map/ppermute | solution.py:22
  21.1 3.5 %collective-permute-start.8 = (bf16[64,4096]{1,0:T(8,128)(2,1)S(1)}, bf16[64,4096]{1,0:T(8,128)(2,1)S(1)}, u32[]{:S(2)}, u32[]{:S(2)}) collective-permute-start(bf16[64,4096]{1,0:T(8,128)(2,1)S(1)} %pad_maximum_fusion.2.refs_0_), channel_id=1, source_target_pairs={{4,0},{6,2},{0,4},{2,6},{5,1},{7,3},{1,5},{3,7},{12,8},{14,10},{8,... | collective-permute-start | bytes 1572872 | tf_op jit(solution)/shard_map/ppermute | solution.py:22
  25.0 2.3 %collective-permute-start.11 = (bf16[64,4096]{1,0:T(8,128)(2,1)S(1)}, bf16[64,4096]{1,0:T(8,128)(2,1)S(1)}, u32[]{:S(2)}, u32[]{:S(2)}) collective-permute-start(bf16[64,4096]{1,0:T(8,128)(2,1)S(1)} %pad_maximum_fusion.3.refs_4_), channel_id=1, source_target_pairs={{16,0},{24,8},{0,16},{8,24},{17,1},{25,9},{1,17},{9,25},{18,2},{26... | collective-permute-start | bytes 1572872 | tf_op jit(solution)/shard_map/ppermute | solution.py:22
  27.4 6.1 %collective-permute-done.9.refs_3_ = bf16[64,4096]{1,0:T(8,128)(2,1)S(1)} collective-permute-done((bf16[64,4096]{1,0:T(8,128)(2,1)S(1)}, bf16[64,4096]{1,0:T(8,128)(2,1)S(1)}, u32[]{:S(2)}, u32[]{:S(2)}) %collective-permute-start.9) | collective-permute-done | bytes 524320 | tf_op jit(solution)/shard_map/ppermute | solution.py:22
  33.5 1.9 %collective-permute-start.10 = (bf16[64,4096]{1,0:T(8,128)(2,1)S(1)}, bf16[64,4096]{1,0:T(8,128)(2,1)S(1)}, u32[]{:S(2)}, u32[]{:S(2)}) collective-permute-start(bf16[64,4096]{1,0:T(8,128)(2,1)S(1)} %pad_maximum_fusion.3.refs_4_), channel_id=1, source_target_pairs={{8,0},{16,8},{24,16},{0,24},{9,1},{17,9},{25,17},{1,25},{10,2},{18... | collective-permute-start | bytes 1572872 | tf_op jit(solution)/shard_map/ppermute | solution.py:22
  35.4 10.1 %collective-permute-done.8.refs_2_ = bf16[64,4096]{1,0:T(8,128)(2,1)S(1)} collective-permute-done((bf16[64,4096]{1,0:T(8,128)(2,1)S(1)}, bf16[64,4096]{1,0:T(8,128)(2,1)S(1)}, u32[]{:S(2)}, u32[]{:S(2)}) %collective-permute-start.8) | collective-permute-done | bytes 524320 | tf_op jit(solution)/shard_map/ppermute | solution.py:22
  45.5 1.5 collective-permute-done.7.refs_1_
  47.3 1.5 collective-permute-done.10.refs_5_
  48.8 6.6 %enc_fwd.1 = (bf16[64,2048]{1,0:T(8,128)(2,1)S(1)}, bf16[64,2048]{1,0:T(8,128)(2,1)S(1)}, f32[128,2048]{1,0:T(8,128)S(1)}, f32[128,2048]{1,0:T(8,128)S(1)}, f32[...) custom-call(bf16[64,4096]{1,0:T(8,128)(2,1)S(1)} %pad_maximum_fusion, ...), custom_call_target="tpu_custom_call" | custom-call | flops 1 | bytes 1 | tf_op jit(solution)/shard_map/enc_fwd/pallas_call | solution.py:196
  56.3 1.7 %collective-permute-start.13 = (bf16[64,2048]{1,0:T(8,128)(2,1)S(1)}, bf16[64,2048]{1,0:T(8,128)(2,1)S(1)}, u32[]{:S(2)}, u32[]{:S(2)}) collective-permute-start(bf16[64,2048]{1,0:T(8,128)(2,1)S(1)} %get-tuple-element.30), channel_id=1, source_target_pairs={{24,0},{0,8},{8,16},{16,24},{25,1},{1,9},{9,17},{17,25},{26,2},{2,... | collective-permute-start | bytes 786440 | tf_op jit(solution)/shard_map/ppermute | solution.py:22
  58.0 1.7 %collective-permute-start.15 = (bf16[64,2048]{1,0:T(8,128)(2,1)S(1)}, bf16[64,2048]{1,0:T(8,128)(2,1)S(1)}, u32[]{:S(2)}, u32[]{:S(2)}) collective-permute-start(bf16[64,2048]{1,0:T(8,128)(2,1)S(1)} %get-tuple-element.32), channel_id=1, source_target_pairs={{8,0},{16,8},{24,16},{0,24},{9,1},{17,9},{25,17},{1,25},{10,2},{18... | collective-permute-start | bytes 786440 | tf_op jit(solution)/shard_map/ppermute | solution.py:22
  60.7 1.6 %collective-permute-start.26 = (bf16[64,2048]{1,0:T(8,128)(2,1)S(1)}, bf16[64,2048]{1,0:T(8,128)(2,1)S(1)}, u32[]{:S(2)}, u32[]{:S(2)}) collective-permute-start(bf16[64,2048]{1,0:T(8,128)(2,1)S(1)} %get-tuple-element.44), channel_id=1, source_target_pairs={{2,0},{4,2},{6,4},{0,6},{3,1},{5,3},{7,5},{1,7},{10,8},{12,10},{14... | collective-permute-start | bytes 786440 | tf_op jit(solution)/shard_map/ppermute | solution.py:22
  62.3 13.7 %mlp_err.1 = (bf16[64,2048]{1,0:T(8,128)(2,1)S(1)}, bf16[64,2048]{1,0:T(8,128)(2,1)S(1)}, f32[128,2048]{1,0:T(8,128)}, f32[128,2048]{1,0:T(8,128)}, f32[128,2048...) custom-call(bf16[64,4096]{1,0:T(8,128)(2,1)S(1)} %pad_maximum_fusion, ...), custom_call_target="tpu_custom_call" | custom-call | flops 1 | bytes 1 | tf_op jit(solution)/shard_map/mlp_err/pallas_call | solution.py:214
  76.1 2.7 %collective-permute-start.19 = (bf16[64,2048]{1,0:T(8,128)(2,1)S(1)}, bf16[64,2048]{1,0:T(8,128)(2,1)S(1)}, u32[]{:S(2)}, u32[]{:S(2)}) collective-permute-start(bf16[64,2048]{1,0:T(8,128)(2,1)S(1)} %get-tuple-element.39), channel_id=1, source_target_pairs={{8,0},{16,8},{24,16},{0,24},{9,1},{17,9},{25,17},{1,25},{10,2},{18... | collective-permute-start | bytes 786440 | tf_op jit(solution)/shard_map/ppermute | solution.py:22
  79.1 2.7 %collective-permute-start.30 = (bf16[64,2048]{1,0:T(8,128)(2,1)S(1)}, bf16[64,2048]{1,0:T(8,128)(2,1)S(1)}, u32[]{:S(2)}, u32[]{:S(2)}) collective-permute-start(bf16[64,2048]{1,0:T(8,128)(2,1)S(1)} %get-tuple-element.49), channel_id=1, source_target_pairs={{2,0},{4,2},{6,4},{0,6},{3,1},{5,3},{7,5},{1,7},{10,8},{12,10},{14... | collective-permute-start | bytes 786440 | tf_op jit(solution)/shard_map/ppermute | solution.py:22
  85.7 3.3 %collective-permute-start.31 = (bf16[128,2048]{1,0:T(8,128)(2,1)S(1)}, bf16[128,2048]{1,0:T(8,128)(2,1)S(1)}, u32[]{:S(2)}, u32[]{:S(2)}) collective-permute-start(bf16[128,2048]{1,0:T(8,128)(2,1)S(1)} %add_convert_fusion), channel_id=1, source_target_pairs={{2,0},{4,2},{6,4},{0,6},{3,1},{5,3},{7,5},{1,7},{10,8},{12,10},{14... | collective-permute-start | bytes 1572872 | tf_op jit(solution)/shard_map/ppermute | solution.py:22
  89.0 3.1 %collective-permute-done.16 = bf16[128,2048]{1,0:T(8,128)(2,1)S(1)} collective-permute-done((bf16[128,2048]{1,0:T(8,128)(2,1)S(1)}, bf16[128,2048]{1,0:T(8,128)(2,1)S(1)}, u32[]{:S(2)}, u32[]{:S(2)}) %collective-permute-start.16) | collective-permute-done | bytes 524320 | tf_op jit(solution)/shard_map/ppermute | solution.py:22
  92.2 3.3 %collective-permute-start.20 = (bf16[128,2048]{1,0:T(8,128)(2,1)S(1)}, bf16[128,2048]{1,0:T(8,128)(2,1)S(1)}, u32[]{:S(2)}, u32[]{:S(2)}) collective-permute-start(bf16[128,2048]{1,0:T(8,128)(2,1)S(1)} %add_convert_fusion.4), channel_id=1, source_target_pairs={{8,0},{16,8},{24,16},{0,24},{9,1},{17,9},{25,17},{1,25},{10,2},{18... | collective-permute-start | bytes 1572872 | tf_op jit(solution)/shard_map/ppermute | solution.py:22
  95.7 8.3 %collective-permute-done.20 = bf16[128,2048]{1,0:T(8,128)(2,1)S(1)} collective-permute-done((bf16[128,2048]{1,0:T(8,128)(2,1)S(1)}, bf16[128,2048]{1,0:T(8,128)(2,1)S(1)}, u32[]{:S(2)}, u32[]{:S(2)}) %collective-permute-start.20) | collective-permute-done | bytes 524320 | tf_op jit(solution)/shard_map/ppermute | solution.py:22
  104.0 3.0 %collective-permute-start.29 = (bf16[128,2048]{1,0:T(8,128)(2,1)S(1)}, bf16[128,2048]{1,0:T(8,128)(2,1)S(1)}, u32[]{:S(2)}, u32[]{:S(2)}) collective-permute-start(bf16[128,2048]{1,0:T(8,128)(2,1)S(1)} %add_convert_fusion.1), channel_id=1, source_target_pairs={{6,0},{0,2},{2,4},{4,6},{7,1},{1,3},{3,5},{5,7},{14,8},{8,10},{10,... | collective-permute-start | bytes 1572872 | tf_op jit(solution)/shard_map/ppermute | solution.py:22
  107.0 3.0 %collective-permute-done.18 = bf16[128,2048]{1,0:T(8,128)(2,1)S(1)} collective-permute-done((bf16[128,2048]{1,0:T(8,128)(2,1)S(1)}, bf16[128,2048]{1,0:T(8,128)(2,1)S(1)}, u32[]{:S(2)}, u32[]{:S(2)}) %collective-permute-start.18) | collective-permute-done | bytes 524320 | tf_op jit(solution)/shard_map/ppermute | solution.py:22
  110.3 2.0 %collective-permute-start.21 = (bf16[32,4096]{1,0:T(8,128)(2,1)S(1)}, bf16[32,4096]{1,0:T(8,128)(2,1)S(1)}, u32[]{:S(2)}, u32[]{:S(2)}) collective-permute-start(bf16[32,4096]{1,0:T(8,128)(2,1)S(1)} %get-tuple-element.53), channel_id=1, source_target_pairs={{6,0},{0,2},{2,4},{4,6},{7,1},{1,3},{3,5},{5,7},{14,8},{8,10},{10,... | collective-permute-start | bytes 786440 | tf_op jit(solution)/shard_map/ppermute | solution.py:22
  114.9 3.2 %collective-permute-start.34 = (bf16[32,4096]{1,0:T(8,128)(2,1)S(1)}, bf16[32,4096]{1,0:T(8,128)(2,1)S(1)}, u32[]{:S(2)}, u32[]{:S(2)}) collective-permute-start(bf16[32,4096]{1,0:T(8,128)(2,1)S(1)} %get-tuple-element.51), channel_id=1, source_target_pairs={{8,0},{16,8},{24,16},{0,24},{9,1},{17,9},{25,17},{1,25},{10,2},{18... | collective-permute-start | bytes 786440 | tf_op jit(solution)/shard_map/ppermute | solution.py:22
  119.2 2.4 %collective-permute-done.22 = bf16[32,4096]{1,0:T(8,128)(2,1)S(1)} collective-permute-done((bf16[32,4096]{1,0:T(8,128)(2,1)S(1)}, bf16[32,4096]{1,0:T(8,128)(2,1)S(1)}, u32[]{:S(2)}, u32[]{:S(2)}) %collective-permute-start.22) | collective-permute-done | bytes 262176 | tf_op jit(solution)/shard_map/ppermute | solution.py:22
  123.2 2.6 %collective-permute-done.33 = bf16[32,4096]{1,0:T(8,128)(2,1)S(1)} collective-permute-done((bf16[32,4096]{1,0:T(8,128)(2,1)S(1)}, bf16[32,4096]{1,0:T(8,128)(2,1)S(1)}, u32[]{:S(2)}, u32[]{:S(2)}) %collective-permute-start.33) | collective-permute-done | bytes 262176 | tf_op jit(solution)/shard_map/ppermute | solution.py:22
  126.0 2.5 %collective-permute-start.36 = (bf16[16,4096]{1,0:T(8,128)(2,1)S(1)}, bf16[16,4096]{1,0:T(8,128)(2,1)S(1)}, u32[]{:S(2)}, u32[]{:S(2)}) collective-permute-start(bf16[16,4096]{1,0:T(8,128)(2,1)S(1)} %fusion.19), channel_id=1, source_target_pairs={{1,0},{0,1},{3,2},{2,3},{5,4},{4,5},{7,6},{6,7},{9,8},{8,9},{11,10... | collective-permute-start | bytes 393224 | tf_op jit(solution)/shard_map/ppermute | solution.py:22
  128.5 2.9 %collective-permute-done.36 = bf16[16,4096]{1,0:T(8,128)(2,1)S(1)} collective-permute-done((bf16[16,4096]{1,0:T(8,128)(2,1)S(1)}, bf16[16,4096]{1,0:T(8,128)(2,1)S(1)}, u32[]{:S(2)}, u32[]{:S(2)}) %collective-permute-start.36) | collective-permute-done | bytes 131104 | tf_op jit(solution)/shard_map/ppermute | solution.py:22
  131.4 20.0 %collective-permute-start.37 = (f32[16,4096]{1,0:T(8,128)S(1)}, f32[16,4096]{1,0:T(8,128)S(1)}, u32[]{:S(2)}, u32[]{:S(2)}) collective-permute-start(f32[16,4096]{1,0:T(8,128)S(1)} %fusion.14), channel_id=1, source_target_pairs={{0,32},{32,64},{64,96},{1,33},{33,65},{65,97},{2,34},{34,66},{66,9... | collective-permute-start | bytes 786440 | tf_op jit(solution)/shard_map/ppermute | solution.py:251
  152.5 6.4 %collective-permute-done.35 = bf16[16,4096]{1,0:T(8,128)(2,1)S(1)} collective-permute-done((bf16[16,4096]{1,0:T(8,128)(2,1)S(1)}, bf16[16,4096]{1,0:T(8,128)(2,1)S(1)}, u32[]{:S(2)}, u32[]{:S(2)}) %collective-permute-start.35) | collective-permute-done | bytes 131104 | tf_op jit(solution)/shard_map/ppermute | solution.py:22
  (95 shorter events, 22.7 us)
Async XLA Ops:
  2.7 9.3 %collective-permute-start.3 = (bf16[16,4096]{1,0:T(8,128)(2,1)S(1)}, bf16[16,4096]{1,0:T(8,128)(2,1)S(1)}, u32[]{:S(2)}, u32[]{:S(2)}) collective-permute-start(bf16[16,4096]{1,0:T(8,128)(2,1)S(1)} %fusion.12), channel_id=1, source_target_pairs={{1,0},{0,1},{3,2},{2,3},{5,4},{4,5},{7,6},{6,7},{9,8},{8,9},{11,10... | collective-permute-start | bytes 393224 | tf_op jit(solution)/shard_map/ppermute | solution.py:22
  7.2 8.7 %collective-permute-start.2 = (bf16[16,4096]{1,0:T(8,128)(2,1)S(1)}, bf16[16,4096]{1,0:T(8,128)(2,1)S(1)}, u32[]{:S(2)}, u32[]{:S(2)}) collective-permute-start(bf16[16,4096]{1,0:T(8,128)(2,1)S(1)} %fusion.12), channel_id=1, source_target_pairs={{24,0},{0,8},{8,16},{16,24},{25,1},{1,9},{9,17},{17,25},{26,2},{2,... | collective-permute-start | bytes 393224 | tf_op jit(solution)/shard_map/ppermute | solution.py:22
  8.4 8.6 %collective-permute-start.1 = (bf16[16,4096]{1,0:T(8,128)(2,1)S(1)}, bf16[16,4096]{1,0:T(8,128)(2,1)S(1)}, u32[]{:S(2)}, u32[]{:S(2)}) collective-permute-start(bf16[16,4096]{1,0:T(8,128)(2,1)S(1)} %fusion.12), channel_id=1, source_target_pairs={{16,0},{24,8},{0,16},{8,24},{17,1},{25,9},{1,17},{9,25},{18,2},{26... | collective-permute-start | bytes 393224 | tf_op jit(solution)/shard_map/ppermute | solution.py:22
  13.3 6.9 %collective-permute-start.5 = (bf16[16,4096]{1,0:T(8,128)(2,1)S(1)}, bf16[16,4096]{1,0:T(8,128)(2,1)S(1)}, u32[]{:S(2)}, u32[]{:S(2)}) collective-permute-start(bf16[16,4096]{1,0:T(8,128)(2,1)S(1)} %collective-permute-done.3), channel_id=1, source_target_pairs={{4,0},{6,2},{0,4},{2,6},{5,1},{7,3},{1,5},{3,7},{12,8},{14,10},{8,... | collective-permute-start | bytes 393224 | tf_op jit(solution)/shard_map/ppermute | solution.py:22
  21.1 12.4 %collective-permute-start.9 = (bf16[64,4096]{1,0:T(8,128)(2,1)S(1)}, bf16[64,4096]{1,0:T(8,128)(2,1)S(1)}, u32[]{:S(2)}, u32[]{:S(2)}) collective-permute-start(bf16[64,4096]{1,0:T(8,128)(2,1)S(1)} %pad_maximum_fusion.2.refs_0_), channel_id=1, source_target_pairs={{6,0},{0,2},{2,4},{4,6},{7,1},{1,3},{3,5},{5,7},{14,8},{8,10},{10,... | collective-permute-start | bytes 1572872 | tf_op jit(solution)/shard_map/ppermute | solution.py:22
  21.1 24.3 %collective-permute-start.8 = (bf16[64,4096]{1,0:T(8,128)(2,1)S(1)}, bf16[64,4096]{1,0:T(8,128)(2,1)S(1)}, u32[]{:S(2)}, u32[]{:S(2)}) collective-permute-start(bf16[64,4096]{1,0:T(8,128)(2,1)S(1)} %pad_maximum_fusion.2.refs_0_), channel_id=1, source_target_pairs={{4,0},{6,2},{0,4},{2,6},{5,1},{7,3},{1,5},{3,7},{12,8},{14,10},{8,... | collective-permute-start | bytes 1572872 | tf_op jit(solution)/shard_map/ppermute | solution.py:22
  24.6 22.4 %collective-permute-start.7 = (bf16[64,4096]{1,0:T(8,128)(2,1)S(1)}, bf16[64,4096]{1,0:T(8,128)(2,1)S(1)}, u32[]{:S(2)}, u32[]{:S(2)}) collective-permute-start(bf16[64,4096]{1,0:T(8,128)(2,1)S(1)} %pad_maximum_fusion.2.refs_0_), channel_id=1, source_target_pairs={{2,0},{4,2},{6,4},{0,6},{3,1},{5,3},{7,5},{1,7},{10,8},{12,10},{14... | collective-permute-start | bytes 1572872 | tf_op jit(solution)/shard_map/ppermute | solution.py:22
  24.7 22.3 %collective-permute-start.12 = (bf16[64,4096]{1,0:T(8,128)(2,1)S(1)}, bf16[64,4096]{1,0:T(8,128)(2,1)S(1)}, u32[]{:S(2)}, u32[]{:S(2)}) collective-permute-start(bf16[64,4096]{1,0:T(8,128)(2,1)S(1)} %pad_maximum_fusion.3.refs_4_), channel_id=1, source_target_pairs={{24,0},{0,8},{8,16},{16,24},{25,1},{1,9},{9,17},{17,25},{26,2},{2,... | collective-permute-start | bytes 1572872 | tf_op jit(solution)/shard_map/ppermute | solution.py:22
  25.0 22.3 %collective-permute-start.11 = (bf16[64,4096]{1,0:T(8,128)(2,1)S(1)}, bf16[64,4096]{1,0:T(8,128)(2,1)S(1)}, u32[]{:S(2)}, u32[]{:S(2)}) collective-permute-start(bf16[64,4096]{1,0:T(8,128)(2,1)S(1)} %pad_maximum_fusion.3.refs_4_), channel_id=1, source_target_pairs={{16,0},{24,8},{0,16},{8,24},{17,1},{25,9},{1,17},{9,25},{18,2},{26... | collective-permute-start | bytes 1572872 | tf_op jit(solution)/shard_map/ppermute | solution.py:22
  33.5 15.3 %collective-permute-start.10 = (bf16[64,4096]{1,0:T(8,128)(2,1)S(1)}, bf16[64,4096]{1,0:T(8,128)(2,1)S(1)}, u32[]{:S(2)}, u32[]{:S(2)}) collective-permute-start(bf16[64,4096]{1,0:T(8,128)(2,1)S(1)} %pad_maximum_fusion.3.refs_4_), channel_id=1, source_target_pairs={{8,0},{16,8},{24,16},{0,24},{9,1},{17,9},{25,17},{1,25},{10,2},{18... | collective-permute-start | bytes 1572872 | tf_op jit(solution)/shard_map/ppermute | solution.py:22
  56.3 19.9 %collective-permute-start.13 = (bf16[64,2048]{1,0:T(8,128)(2,1)S(1)}, bf16[64,2048]{1,0:T(8,128)(2,1)S(1)}, u32[]{:S(2)}, u32[]{:S(2)}) collective-permute-start(bf16[64,2048]{1,0:T(8,128)(2,1)S(1)} %get-tuple-element.30), channel_id=1, source_target_pairs={{24,0},{0,8},{8,16},{16,24},{25,1},{1,9},{9,17},{17,25},{26,2},{2,... | collective-permute-start | bytes 786440 | tf_op jit(solution)/shard_map/ppermute | solution.py:22
  58.0 20.9 %collective-permute-start.15 = (bf16[64,2048]{1,0:T(8,128)(2,1)S(1)}, bf16[64,2048]{1,0:T(8,128)(2,1)S(1)}, u32[]{:S(2)}, u32[]{:S(2)}) collective-permute-start(bf16[64,2048]{1,0:T(8,128)(2,1)S(1)} %get-tuple-element.32), channel_id=1, source_target_pairs={{8,0},{16,8},{24,16},{0,24},{9,1},{17,9},{25,17},{1,25},{10,2},{18... | collective-permute-start | bytes 786440 | tf_op jit(solution)/shard_map/ppermute | solution.py:22
  59.7 22.3 %collective-permute-start.24 = (bf16[64,2048]{1,0:T(8,128)(2,1)S(1)}, bf16[64,2048]{1,0:T(8,128)(2,1)S(1)}, u32[]{:S(2)}, u32[]{:S(2)}) collective-permute-start(bf16[64,2048]{1,0:T(8,128)(2,1)S(1)} %get-tuple-element.42), channel_id=1, source_target_pairs={{6,0},{0,2},{2,4},{4,6},{7,1},{1,3},{3,5},{5,7},{14,8},{8,10},{10,... | collective-permute-start | bytes 786440 | tf_op jit(solution)/shard_map/ppermute | solution.py:22
  60.7 18.4 %collective-permute-start.26 = (bf16[64,2048]{1,0:T(8,128)(2,1)S(1)}, bf16[64,2048]{1,0:T(8,128)(2,1)S(1)}, u32[]{:S(2)}, u32[]{:S(2)}) collective-permute-start(bf16[64,2048]{1,0:T(8,128)(2,1)S(1)} %get-tuple-element.44), channel_id=1, source_target_pairs={{2,0},{4,2},{6,4},{0,6},{3,1},{5,3},{7,5},{1,7},{10,8},{12,10},{14... | collective-permute-start | bytes 786440 | tf_op jit(solution)/shard_map/ppermute | solution.py:22
  76.1 7.6 %collective-permute-start.19 = (bf16[64,2048]{1,0:T(8,128)(2,1)S(1)}, bf16[64,2048]{1,0:T(8,128)(2,1)S(1)}, u32[]{:S(2)}, u32[]{:S(2)}) collective-permute-start(bf16[64,2048]{1,0:T(8,128)(2,1)S(1)} %get-tuple-element.39), channel_id=1, source_target_pairs={{8,0},{16,8},{24,16},{0,24},{9,1},{17,9},{25,17},{1,25},{10,2},{18... | collective-permute-start | bytes 786440 | tf_op jit(solution)/shard_map/ppermute | solution.py:22
  78.9 6.8 %collective-permute-start.28 = (bf16[64,2048]{1,0:T(8,128)(2,1)S(1)}, bf16[64,2048]{1,0:T(8,128)(2,1)S(1)}, u32[]{:S(2)}, u32[]{:S(2)}) collective-permute-start(bf16[64,2048]{1,0:T(8,128)(2,1)S(1)} %get-tuple-element.47), channel_id=1, source_target_pairs={{6,0},{0,2},{2,4},{4,6},{7,1},{1,3},{3,5},{5,7},{14,8},{8,10},{10,... | collective-permute-start | bytes 786440 | tf_op jit(solution)/shard_map/ppermute | solution.py:22
  81.9 30.4 %collective-permute-start.27 = (bf16[128,2048]{1,0:T(8,128)(2,1)S(1)}, bf16[128,2048]{1,0:T(8,128)(2,1)S(1)}, u32[]{:S(2)}, u32[]{:S(2)}) collective-permute-start(bf16[128,2048]{1,0:T(8,128)(2,1)S(1)} %add_convert_fusion.2), channel_id=1, source_target_pairs={{2,0},{4,2},{6,4},{0,6},{3,1},{5,3},{7,5},{1,7},{10,8},{12,10},{14... | collective-permute-start | bytes 1572872 | tf_op jit(solution)/shard_map/ppermute | solution.py:22
  82.5 30.6 %collective-permute-start.25 = (bf16[128,2048]{1,0:T(8,128)(2,1)S(1)}, bf16[128,2048]{1,0:T(8,128)(2,1)S(1)}, u32[]{:S(2)}, u32[]{:S(2)}) collective-permute-start(bf16[128,2048]{1,0:T(8,128)(2,1)S(1)} %add_convert_fusion.3), channel_id=1, source_target_pairs={{6,0},{0,2},{2,4},{4,6},{7,1},{1,3},{3,5},{5,7},{14,8},{8,10},{10,... | collective-permute-start | bytes 1572872 | tf_op jit(solution)/shard_map/ppermute | solution.py:22
  83.8 8.4 %collective-permute-start.16 = (bf16[128,2048]{1,0:T(8,128)(2,1)S(1)}, bf16[128,2048]{1,0:T(8,128)(2,1)S(1)}, u32[]{:S(2)}, u32[]{:S(2)}) collective-permute-start(bf16[128,2048]{1,0:T(8,128)(2,1)S(1)} %add_convert_fusion.6), channel_id=1, source_target_pairs={{8,0},{16,8},{24,16},{0,24},{9,1},{17,9},{25,17},{1,25},{10,2},{18... | collective-permute-start | bytes 1572872 | tf_op jit(solution)/shard_map/ppermute | solution.py:22
  85.3 10.2 %collective-permute-start.14 = (bf16[128,2048]{1,0:T(8,128)(2,1)S(1)}, bf16[128,2048]{1,0:T(8,128)(2,1)S(1)}, u32[]{:S(2)}, u32[]{:S(2)}) collective-permute-start(bf16[128,2048]{1,0:T(8,128)(2,1)S(1)} %add_convert_fusion.7), channel_id=1, source_target_pairs={{24,0},{0,8},{8,16},{16,24},{25,1},{1,9},{9,17},{17,25},{26,2},{2,... | collective-permute-start | bytes 1572872 | tf_op jit(solution)/shard_map/ppermute | solution.py:22
  85.7 28.7 %collective-permute-start.31 = (bf16[128,2048]{1,0:T(8,128)(2,1)S(1)}, bf16[128,2048]{1,0:T(8,128)(2,1)S(1)}, u32[]{:S(2)}, u32[]{:S(2)}) collective-permute-start(bf16[128,2048]{1,0:T(8,128)(2,1)S(1)} %add_convert_fusion), channel_id=1, source_target_pairs={{2,0},{4,2},{6,4},{0,6},{3,1},{5,3},{7,5},{1,7},{10,8},{12,10},{14... | collective-permute-start | bytes 1572872 | tf_op jit(solution)/shard_map/ppermute | solution.py:22
  92.2 11.8 %collective-permute-start.20 = (bf16[128,2048]{1,0:T(8,128)(2,1)S(1)}, bf16[128,2048]{1,0:T(8,128)(2,1)S(1)}, u32[]{:S(2)}, u32[]{:S(2)}) collective-permute-start(bf16[128,2048]{1,0:T(8,128)(2,1)S(1)} %add_convert_fusion.4), channel_id=1, source_target_pairs={{8,0},{16,8},{24,16},{0,24},{9,1},{17,9},{25,17},{1,25},{10,2},{18... | collective-permute-start | bytes 1572872 | tf_op jit(solution)/shard_map/ppermute | solution.py:22
  95.5 14.5 %collective-permute-start.18 = (bf16[128,2048]{1,0:T(8,128)(2,1)S(1)}, bf16[128,2048]{1,0:T(8,128)(2,1)S(1)}, u32[]{:S(2)}, u32[]{:S(2)}) collective-permute-start(bf16[128,2048]{1,0:T(8,128)(2,1)S(1)} %add_convert_fusion.5), channel_id=1, source_target_pairs={{24,0},{0,8},{8,16},{16,24},{25,1},{1,9},{9,17},{17,25},{26,2},{2,... | collective-permute-start | bytes 1572872 | tf_op jit(solution)/shard_map/ppermute | solution.py:22
  104.0 10.4 %collective-permute-start.29 = (bf16[128,2048]{1,0:T(8,128)(2,1)S(1)}, bf16[128,2048]{1,0:T(8,128)(2,1)S(1)}, u32[]{:S(2)}, u32[]{:S(2)}) collective-permute-start(bf16[128,2048]{1,0:T(8,128)(2,1)S(1)} %add_convert_fusion.1), channel_id=1, source_target_pairs={{6,0},{0,2},{2,4},{4,6},{7,1},{1,3},{3,5},{5,7},{14,8},{8,10},{10,... | collective-permute-start | bytes 1572872 | tf_op jit(solution)/shard_map/ppermute | solution.py:22
  110.3 7.7 %collective-permute-start.21 = (bf16[32,4096]{1,0:T(8,128)(2,1)S(1)}, bf16[32,4096]{1,0:T(8,128)(2,1)S(1)}, u32[]{:S(2)}, u32[]{:S(2)}) collective-permute-start(bf16[32,4096]{1,0:T(8,128)(2,1)S(1)} %get-tuple-element.53), channel_id=1, source_target_pairs={{6,0},{0,2},{2,4},{4,6},{7,1},{1,3},{3,5},{5,7},{14,8},{8,10},{10,... | collective-permute-start | bytes 786440 | tf_op jit(solution)/shard_map/ppermute | solution.py:22
  112.3 6.9 %collective-permute-start.23 = (bf16[32,4096]{1,0:T(8,128)(2,1)S(1)}, bf16[32,4096]{1,0:T(8,128)(2,1)S(1)}, u32[]{:S(2)}, u32[]{:S(2)}) collective-permute-start(bf16[32,4096]{1,0:T(8,128)(2,1)S(1)} %get-tuple-element.54), channel_id=1, source_target_pairs={{2,0},{4,2},{6,4},{0,6},{3,1},{5,3},{7,5},{1,7},{10,8},{12,10},{14... | collective-permute-start | bytes 786440 | tf_op jit(solution)/shard_map/ppermute | solution.py:22
  113.1 8.5 %collective-permute-start.22 = (bf16[32,4096]{1,0:T(8,128)(2,1)S(1)}, bf16[32,4096]{1,0:T(8,128)(2,1)S(1)}, u32[]{:S(2)}, u32[]{:S(2)}) collective-permute-start(bf16[32,4096]{1,0:T(8,128)(2,1)S(1)} %get-tuple-element.55), channel_id=1, source_target_pairs={{4,0},{6,2},{0,4},{2,6},{5,1},{7,3},{1,5},{3,7},{12,8},{14,10},{8,... | collective-permute-start | bytes 786440 | tf_op jit(solution)/shard_map/ppermute | solution.py:22
  114.8 8.4 %collective-permute-start.32 = (bf16[32,4096]{1,0:T(8,128)(2,1)S(1)}, bf16[32,4096]{1,0:T(8,128)(2,1)S(1)}, u32[]{:S(2)}, u32[]{:S(2)}) collective-permute-start(bf16[32,4096]{1,0:T(8,128)(2,1)S(1)} %get-tuple-element.50), channel_id=1, source_target_pairs={{24,0},{0,8},{8,16},{16,24},{25,1},{1,9},{9,17},{17,25},{26,2},{2,... | collective-permute-start | bytes 786440 | tf_op jit(solution)/shard_map/ppermute | solution.py:22
  114.9 8.3 %collective-permute-start.34 = (bf16[32,4096]{1,0:T(8,128)(2,1)S(1)}, bf16[32,4096]{1,0:T(8,128)(2,1)S(1)}, u32[]{:S(2)}, u32[]{:S(2)}) collective-permute-start(bf16[32,4096]{1,0:T(8,128)(2,1)S(1)} %get-tuple-element.51), channel_id=1, source_target_pairs={{8,0},{16,8},{24,16},{0,24},{9,1},{17,9},{25,17},{1,25},{10,2},{18... | collective-permute-start | bytes 786440 | tf_op jit(solution)/shard_map/ppermute | solution.py:22
  118.1 7.7 %collective-permute-start.33 = (bf16[32,4096]{1,0:T(8,128)(2,1)S(1)}, bf16[32,4096]{1,0:T(8,128)(2,1)S(1)}, u32[]{:S(2)}, u32[]{:S(2)}) collective-permute-start(bf16[32,4096]{1,0:T(8,128)(2,1)S(1)} %get-tuple-element.52), channel_id=1, source_target_pairs={{16,0},{24,8},{0,16},{8,24},{17,1},{25,9},{1,17},{9,25},{18,2},{26... | collective-permute-start | bytes 786440 | tf_op jit(solution)/shard_map/ppermute | solution.py:22
  131.4 27.5 %collective-permute-start.37 = (f32[16,4096]{1,0:T(8,128)S(1)}, f32[16,4096]{1,0:T(8,128)S(1)}, u32[]{:S(2)}, u32[]{:S(2)}) collective-permute-start(f32[16,4096]{1,0:T(8,128)S(1)} %fusion.14), channel_id=1, source_target_pairs={{0,32},{32,64},{64,96},{1,33},{33,65},{65,97},{2,34},{34,66},{66,9... | collective-permute-start | bytes 786440 | tf_op jit(solution)/shard_map/ppermute | solution.py:251
  151.4 7.5 %collective-permute-start.35 = (bf16[16,4096]{1,0:T(8,128)(2,1)S(1)}, bf16[16,4096]{1,0:T(8,128)(2,1)S(1)}, u32[]{:S(2)}, u32[]{:S(2)}) collective-permute-start(bf16[16,4096]{1,0:T(8,128)(2,1)S(1)} %fusion.20), channel_id=1, source_target_pairs={{1,0},{0,1},{3,2},{2,3},{5,4},{4,5},{7,6},{6,7},{9,8},{8,9},{11,10... | collective-permute-start | bytes 393224 | tf_op jit(solution)/shard_map/ppermute | solution.py:22
  (16 other events, 186.7 us)

commit v2 on v0

v2 whole, which is shorter than its diff:
```python
import functools

import jax
import jax.numpy as jnp
from jax import lax
from jax.experimental import pallas as pl
from jax.experimental.pallas import tpu as pltpu
from jax.sharding import Mesh
from jax.sharding import PartitionSpec as P

FX, FY, FZ = "feat_0", "feat_1", "feat_2"
FEAT = (FX, FY, FZ)
BF = jnp.bfloat16
F32 = jnp.float32
VMEM = pl.BlockSpec(memory_space=pltpu.VMEM)
HBM = pl.BlockSpec(memory_space=pltpu.HBM)
CHEAP = pl.CostEstimate(flops=1, bytes_accessed=1, transcendentals=0)
ORDER = (2, 1, 3, 0)


def swap(value, axis, distance):
    count = lax.axis_size(axis)
    return lax.ppermute(value, axis, [(i, i ^ distance) for i in range(count)])


def tie(*values):
    return lax.optimization_barrier(values)


def dot(a, b):
    return jnp.dot(a, b, preferred_element_type=F32)


def dot_t(a, b):
    return lax.dot_general(a, b, (((1,), (1,)), ((), ())), preferred_element_type=F32)


def ring_gather(block, axis):
    return [block, swap(block, axis, 1), swap(block, axis, 3)]


def ring_relay(pieces, axis):
    _, one, three = pieces
    half = one.shape[0] // 2
    return [swap(one[:half], axis, 3), swap(three[half:], axis, 1)]


def block_orders(rows):
    slot = {0: 0, 1: 1, 3: 2}
    own = lambda x, y: ((slot[y] if y != 2 else 6) * 4 + x) * rows
    oth = lambda x, y: ((3 + slot[x] if x != 2 else 7) * 4 + y) * rows
    x_first = [f(x, y) for x in ORDER for y in range(4) for f in (own, oth)]
    y_first = [f(x, y) for y in ORDER for x in range(4) for f in (own, oth)]
    return x_first, y_first


def place(first, rest, rows, out_x, out_y):
    early = first.shape[0]
    x_first, y_first = block_orders(rows)
    for out, order in ((out_x, x_first), (out_y, y_first)):
        for at, start in enumerate(order):
            src, start = (first, start) if start < early else (rest, start - early)
            out[at * rows:(at + 1) * rows, :] = src[start:start + rows, :]


def feature_units(tokens, enc, bias):
    return jnp.maximum(dot(tokens, enc[...]) + bias[...], 0.0).astype(BF)


def hidden_units(tokens, gate, up):
    gates = dot_t(tokens, gate[...])
    ups = dot_t(tokens, up[...])
    return (gates / (1.0 + jnp.exp(-gates)) * ups).astype(BF)


def load_kernel(_, *refs):
    count = (len(refs) - 1) // 2
    copies = [pltpu.make_async_copy(refs[i], refs[count + i], refs[-1].at[i]) for i in range(count)]
    for copy in copies:
        copy.start()
    for copy in copies:
        copy.wait()


def first_kernel(*refs):
    pieces, (enc, bias, gate, up), (feat, hid) = refs[:6], refs[6:10], refs[10:]
    tokens = jnp.concatenate([p[...] for p in pieces], axis=0)
    feat[...] = feature_units(tokens, enc, bias)
    hid[...] = hidden_units(tokens, gate, up)


def products(feat, hid, down, dec, at, side):
    width = down.shape[1]
    half = width // 2
    f, h = feat[at, :], hid[at, :]
    cols = slice(side * half, (side + 1) * half)
    ahead = slice(width + side * half, width + (side + 1) * half)
    yield slice(0, half), dot(f, dec[:, ahead])
    yield slice(half, width), dot(f, dec[:, cols]) - dot(h, down[:, cols])


def far_kernel(rows, *refs):
    pieces, (feat, hid, enc, bias, gate, up, down, dec), outs = refs[:4], refs[4:12], refs[12:16]
    feat_x, feat_y, hid_x, hid_y, feat_late, hid_late = refs[16:]
    tokens = jnp.concatenate([p[...] for p in pieces], axis=0)
    feat_late[...] = feature_units(tokens, enc, bias)
    hid_late[...] = hidden_units(tokens, gate, up)
    place(feat, feat_late, rows, feat_x, feat_y)
    place(hid, hid_late, rows, hid_x, hid_y)
    mid = 4 * rows
    for side, (f, h) in enumerate(((feat_x, hid_x), (feat_y, hid_y))):
        for cols, value in products(f, h, down, dec, slice(0, 2 * mid), side):
            outs[2 * side][:, cols] = value[:mid].astype(BF)
            outs[2 * side + 1][:, cols] = value[mid:].astype(BF)


def near_kernel(rows, feat_x, feat_y, hid_x, hid_y, down, dec, *outs):
    block = 8 * rows
    for side, (f, h) in enumerate(((feat_x, hid_x), (feat_y, hid_y))):
        for cols, value in products(f, h, down, dec, slice(block, 4 * block), side):
            for at in range(3):
                outs[3 * side + at][:, cols] = value[at * block:(at + 1) * block]


def hop_far(parts, axis):
    return swap(parts[0], axis, 1), swap(parts[1], axis, 3)


def hop_near(parts, arrived, axis):
    upper, lower = (v.astype(F32) for v in arrived)
    zeros = jnp.zeros_like(upper)
    one = parts[0] + jnp.concatenate([zeros, lower], axis=0)
    three = parts[1] + jnp.concatenate([upper, zeros], axis=0)
    return swap(one.astype(BF), axis, 1), swap(three.astype(BF), axis, 3)


def total_of(own, arrived):
    for value in arrived:
        own = own + value.astype(F32)
    return own


def split_rows(array, count):
    rows = array.shape[0] // count
    return [array[i * rows:(i + 1) * rows] for i in range(count)]


def direct(total, axis):
    parts = split_rows(total, 4)
    return parts[0], [swap(parts[r].astype(BF), axis, r) for r in (1, 2, 3)]


def body(resid, norm_gain, w_gate, w_up, w_down, w_enc, b_enc, w_dec, carry_in):
    rows = resid.shape[1]
    width = resid.shape[2]
    half = width // 2
    block = 8 * rows
    stream = resid[0].astype(F32)
    inv_rms = lax.rsqrt(jnp.mean(stream * stream, axis=1, keepdims=True) + 1e-05)
    normed = (stream * inv_rms * norm_gain[0]).astype(BF)

    other = swap(normed, FZ, 1)
    plane = jnp.concatenate([normed] + [swap(normed, FX, r) for r in (1, 2, 3)], axis=0)
    other_plane = jnp.concatenate([other] + [swap(other, FY, r) for r in (1, 2, 3)], axis=0)
    plane, other_plane = tie(plane, other_plane)
    own_early = ring_gather(plane, FY)
    oth_early = ring_gather(other_plane, FX)

    enc, dec, down, gate, up = w_enc[0], w_dec[0], w_down[0], w_gate[0].T, w_up[0].T
    features, hidden = enc.shape[1], down.shape[0]

    def shape(count, cols, dtype=BF):
        return jax.ShapeDtypeStruct((count, cols), dtype)

    def call(kernel, name, ins, outs, scratch, limit):
        return pl.pallas_call(
            kernel,
            out_shape=outs,
            in_specs=ins,
            out_specs=[VMEM] * len(outs),
            scratch_shapes=scratch,
            compiler_params=pltpu.CompilerParams(vmem_limit_bytes=limit << 20),
            cost_estimate=CHEAP,
            name=name,
        )

    weights = (enc, gate, up, down, dec)
    enc, gate, up, down, dec = call(
        load_kernel, "load_weights", [VMEM] + [HBM] * 5, [shape(*w.shape) for w in weights],
        [pltpu.SemaphoreType.DMA((5,))], 4,
    )(plane, *weights)
    *late, enc, gate, up, down, dec = tie(*own_early, *oth_early, enc, gate, up, down, dec)
    own_early, oth_early = late[:3], late[3:]
    own_late, oth_late = ring_relay(own_early, FY), ring_relay(oth_early, FX)
    early = 24 * rows
    feat, hid = call(
        first_kernel, "first_units", [VMEM] * 10, [shape(early, features), shape(early, hidden)], [], 12,
    )(*own_early, *oth_early, enc, b_enc, gate, up)
    *far_parts, feat_x, feat_y, hid_x, hid_y = call(
        functools.partial(far_kernel, rows), "far_parts", [VMEM] * 12,
        [shape(block // 2, width)] * 4 + [shape(4 * block, features)] * 2 + [shape(4 * block, hidden)] * 2,
        [pltpu.VMEM((block, features), BF), pltpu.VMEM((block, hidden), BF)], 12,
    )(*own_late, *oth_late, feat, hid, enc, b_enc, gate, up, down, dec)
    far_a, far_b = hop_far(far_parts[:2], FX), hop_far(far_parts[2:], FY)
    near_parts = call(
        functools.partial(near_kernel, rows), "near_parts", [VMEM] * 6,
        [shape(block, width, F32)] * 6, [], 12,
    )(feat_x, feat_y, hid_x, hid_y, down, dec)
    near_a = hop_near(near_parts[:2], far_a, FX)
    near_b = hop_near(near_parts[3:5], far_b, FY)
    da = direct(total_of(near_parts[2], near_a), FY)
    db = direct(total_of(near_parts[5], near_b), FX)
    low_a, low_b = total_of(*da), total_of(*db)

    def halves(cols):
        return split_rows(jnp.concatenate([low_a[:, cols], low_b[:, cols]], axis=1), 2)

    fwd_own, fwd_oth = halves(slice(0, half))
    err_own, err_oth = halves(slice(half, width))
    fwd_oth = fwd_oth.astype(BF)
    count = lax.axis_size("grp")
    onward = [(i, i + 1) for i in range(count - 1)]
    planes = lax.axis_size(FZ)
    crossed = [(i * planes + z, (i + 1) * planes + (z ^ 1)) for i in range(count - 1) for z in range(planes)]
    arrived, passed, passed_oth = tie(
        swap(jnp.concatenate([fwd_oth, err_oth.astype(BF)], axis=1), FZ, 1),
        lax.ppermute(fwd_own, "grp", onward),
        lax.ppermute(fwd_oth, ("grp", FZ), crossed),
    )
    arrived = arrived.astype(F32)
    incoming = jnp.where(lax.axis_index("grp") == 0, carry_in, passed + passed_oth.astype(F32))
    to_next = fwd_own + arrived[:, :width]
    errors = err_own + arrived[:, width:] + incoming
    return (errors[None], to_next[None])


def solution(mesh):
    finer = Mesh(
        mesh.devices.reshape(mesh.shape["grp"], 4, 4, 2), ("grp", FX, FY, FZ)
    )
    return jax.shard_map(
        body,
        mesh=finer,
        in_specs=(
            P("grp", FEAT, None),
            P("grp", None),
            P("grp", None, FEAT),
            P("grp", None, FEAT),
            P("grp", FEAT, None),
            P("grp", None, FEAT),
            P("grp", FEAT),
            P("grp", FEAT, None),
            P(FEAT, None),
        ),
        out_specs=(P("grp", FEAT, None), P("grp", FEAT, None)),
        check_vma=False,
    )
```

time: 387 us -> 125 us (0.32)
  waiting for transfers between devices: 311 us -> 41.1 us
  starting transfers between devices: 3.01 us -> 48.9 us
  matrix products: 31.6 us -> 0 us
  Pallas kernels: 0 us -> 16.6 us
  between operations: 13.8 us -> 0.98 us
  other arithmetic: 16 us -> 4.99 us
    reduce_scatter x3 -> x0, waiting for transfers between devices: 222 us -> none  [own_rows(): total = lax.psum_scatter(total, axis, scatter_dimension=0, tiled=True)]
    all_gather x1 -> x0, waiting for transfers between devices: 85.7 us -> none  [body(): tile_rows = lax.all_gather(normed, FEAT, axis=0, tiled=True)]
    ppermute x1 -> x32, starting transfers between devices: 2.85 us -> 48.9 us  [the longest x30 37 us: swap(): return lax.ppermute(value, axis, [(i, i ^ distance) for i in range(count)])]
    ppermute x1 -> x32, waiting for transfers between devices: 3.29 us -> 41.1 us  [the longest x30 35.4 us: swap(): return lax.ppermute(value, axis, [(i, i ^ distance) for i in range(count)])]
    dot_general x4 -> x0, matrix products: 31.6 us -> none  [the longest x1 14.4 us: body(): mlp_part = jnp.dot(hidden, down_rows, preferred_element_type=jnp.float32)]
    pallas_call x0 -> x4, Pallas kernels: none -> 16.6 us  [the longest x1 5.24 us: body(): call(functools.partial(near_kernel, rows), 'near_parts', [VMEM] * 6, [sha...]
    concatenate x1 -> x4, other arithmetic: 11.5 us -> 0.11 us  [the longest x1 0.03 us: body(): jnp.concatenate([normed] + [swap(normed, FX, r) for r in (1, 2, 3)], axis=0)]
    unnamed x6 -> x14, local copies, waits for them, and re-layouts: 5.16 us -> 11.7 us
  transfers between devices with their start and end apart: 5 -> 32, of which waited for: 5 -> 12; matrix products, arithmetic and copies ran while one was open for 0% -> 2% of each run, Pallas kernels for 0% -> 10%
where the time goes in v2:
time: 125 us; the launch traced here: 124 us
  starting transfers between devices  48.9 us (39%)
  waiting for transfers between devices  41.1 us (33%)
  Pallas kernels  16.6 us (13%)
  local copies, waits for them, and re-layouts  12 us (10%)
  other arithmetic  4.99 us (4%)
    ppermute x30, starting transfers between devices, swap(): return lax.ppermute(value, axis, [(i, i ^ distance) for i in range(count)])  37 us
    ppermute x30, waiting for transfers between devices, swap(): return lax.ppermute(value, axis, [(i, i ^ distance) for i in range(count)])  35.4 us
    unnamed x14, local copies, waits for them, and re-layouts  11.7 us
    ppermute x1, starting transfers between devices, body(): lax.ppermute(fwd_own, 'grp', onward)  9.84 us
    ppermute x1, waiting for transfers between devices, body(): lax.ppermute(fwd_oth, ('grp', FZ), crossed)  5.71 us
    pallas_call x1, Pallas kernels, body(): call(functools.partial(near_kernel, rows), 'near_parts', [VMEM] * 6, [sha...  5.24 us
    pallas_call x1, Pallas kernels, body(): call(first_kernel, 'first_units', [VMEM] * 10, [shape(early, features), s...  5.03 us
    pallas_call x1, Pallas kernels, body(): call(functools.partial(far_kernel, rows), 'far_parts', [VMEM] * 12, [shap...  4.66 us
  transfers between devices with their start and end apart: 32, of which 12 were waited for; matrix products, arithmetic and copies ran while one was open for 2% of the time, Pallas kernels for 10%

profile of v2, /device:TPU:1, one launch (start us, length us, event | category | flops | bytes accessed | tf_op | source)
XLA Modules:
  0.0 124.5 jit_solution(9928407836544983708)
XLA Ops:
  2.7 4.5 %collective-permute-start.3 = (bf16[16,4096]{1,0:T(8,128)(2,1)S(1)}, bf16[16,4096]{1,0:T(8,128)(2,1)S(1)}, u32[]{:S(2)}, u32[]{:S(2)}) collective-permute-start(bf16[16,4096]{1,0:T(8,128)(2,1)S(1)} %fusion.6), channel_id=1, source_target_pairs={{0,1},{1,0},{2,3},{3,2},{4,5},{5,4},{6,7},{7,6},{8,9},{9,8},{10,11... | collective-permute-start | bytes 393224 | tf_op jit(solution)/shard_map/ppermute | solution.py:23
  7.2 1.2 collective-permute-start
  8.4 2.5 %collective-permute-start.1 = (bf16[16,4096]{1,0:T(8,128)(2,1)S(1)}, bf16[16,4096]{1,0:T(8,128)(2,1)S(1)}, u32[]{:S(2)}, u32[]{:S(2)}) collective-permute-start(bf16[16,4096]{1,0:T(8,128)(2,1)S(1)} %fusion.6), channel_id=1, source_target_pairs={{0,16},{8,24},{16,0},{24,8},{1,17},{9,25},{17,1},{25,9},{2,18},{10... | collective-permute-start | bytes 393224 | tf_op jit(solution)/shard_map/ppermute | solution.py:23
  11.1 1.3 %collective-permute-start.4 = (bf16[16,4096]{1,0:T(8,128)(2,1)S(1)}, bf16[16,4096]{1,0:T(8,128)(2,1)S(1)}, u32[]{:S(2)}, u32[]{:S(2)}) collective-permute-start(bf16[16,4096]{1,0:T(8,128)(2,1)S(1)} %collective-permute-done.3), channel_id=1, source_target_pairs={{0,2},{2,0},{4,6},{6,4},{1,3},{3,1},{5,7},{7,5},{8,10},{10,8},{12,... | collective-permute-start | bytes 393224 | tf_op jit(solution)/shard_map/ppermute | solution.py:23
  12.4 2.6 %collective-permute-start.5 = (bf16[16,4096]{1,0:T(8,128)(2,1)S(1)}, bf16[16,4096]{1,0:T(8,128)(2,1)S(1)}, u32[]{:S(2)}, u32[]{:S(2)}) collective-permute-start(bf16[16,4096]{1,0:T(8,128)(2,1)S(1)} %collective-permute-done.3), channel_id=1, source_target_pairs={{0,4},{2,6},{4,0},{6,2},{1,5},{3,7},{5,1},{7,3},{8,12},{10,14},{12... | collective-permute-start | bytes 393224 | tf_op jit(solution)/shard_map/ppermute | solution.py:23
  16.0 2.8 %collective-permute-done.2 = bf16[16,4096]{1,0:T(8,128)(2,1)S(1)} collective-permute-done((bf16[16,4096]{1,0:T(8,128)(2,1)S(1)}, bf16[16,4096]{1,0:T(8,128)(2,1)S(1)}, u32[]{:S(2)}, u32[]{:S(2)}) %collective-permute-start.2) | collective-permute-done | bytes 131104 | tf_op jit(solution)/shard_map/ppermute | solution.py:23
  19.2 2.8 %collective-permute-done.6 = bf16[16,4096]{1,0:T(8,128)(2,1)S(1)} collective-permute-done((bf16[16,4096]{1,0:T(8,128)(2,1)S(1)}, bf16[16,4096]{1,0:T(8,128)(2,1)S(1)}, u32[]{:S(2)}, u32[]{:S(2)}) %collective-permute-start.6) | collective-permute-done | bytes 131104 | tf_op jit(solution)/shard_map/ppermute | solution.py:23
  22.2 1.1 collective-permute-start.8
  23.2 2.5 %collective-permute-start.10 = (bf16[64,4096]{1,0:T(8,128)(2,1)S(1)}, bf16[64,4096]{1,0:T(8,128)(2,1)S(1)}, u32[]{:S(2)}, u32[]{:S(2)}) collective-permute-start(bf16[64,4096]{1,0:T(8,128)(2,1)S(1)} %pad_maximum_fusion.1.refs_3_), channel_id=1, source_target_pairs={{0,24},{8,16},{16,8},{24,0},{1,25},{9,17},{17,9},{25,1},{2,26},{10... | collective-permute-start | bytes 1572872 | tf_op jit(solution)/shard_map/ppermute | solution.py:23
  25.7 3.4 %copy-done = bf16[1,512,8192]{2,1,0:T(8,128)(2,1)S(1)} copy-done((bf16[1,512,8192]{2,1,0:T(8,128)(2,1)S(1)}, bf16[1,512,8192]{2,1,0:T(8,128)(2,1)}, u32[]{:S(2)}) %copy-start) | copy-done | bytes 8388632
  29.1 2.2 %copy-done.1 = bf16[1,4096,512]{2,1,0:T(8,128)(2,1)S(1)} copy-done((bf16[1,4096,512]{2,1,0:T(8,128)(2,1)S(1)}, bf16[1,4096,512]{2,1,0:T(8,128)(2,1)}, u32[]{:S(2)}) %copy-start.1) | copy-done | bytes 4194328
  31.3 2.0 %copy-done.2 = bf16[1,4096,448]{1,2,0:T(8,128)(2,1)S(1)} copy-done((bf16[1,4096,448]{1,2,0:T(8,128)(2,1)S(1)}, bf16[1,4096,448]{1,2,0:T(8,128)(2,1)}, u32[]{:S(2)}) %copy-start.2) | copy-done | bytes 3670040
  33.3 2.0 %copy-done.3 = bf16[1,4096,448]{1,2,0:T(8,128)(2,1)S(1)} copy-done((bf16[1,4096,448]{1,2,0:T(8,128)(2,1)S(1)}, bf16[1,4096,448]{1,2,0:T(8,128)(2,1)}, u32[]{:S(2)}) %copy-start.3) | copy-done | bytes 3670040
  35.4 2.0 %copy-done.4 = bf16[1,448,4096]{2,1,0:T(8,128)(2,1)S(1)} copy-done((bf16[1,448,4096]{2,1,0:T(8,128)(2,1)S(1)}, bf16[1,448,4096]{2,1,0:T(8,128)(2,1)}, u32[]{:S(2)}) %copy-start.4) | copy-done | bytes 3670040
  37.4 1.6 %load_weights.1 = (bf16[4096,512]{1,0:T(8,128)(2,1)S(1)}, bf16[448,4096]{1,0:T(8,128)(2,1)S(1)}, bf16[448,4096]{1,0:T(8,128)(2,1)S(1)}, bf16[448,4096]{1,0:T(8,128)(2,1)S(1)}, bf16[512,8192]{1,0:T(8,128)(2,1)S(1)}) custom-call(bf16[64,4096]{1,0:T(8,128)(2,1)S(1)} %pad_maximum_fusion._.refs_0_, bf16[4096,512]{1,0:T(8,128)(2,1)S(1)} %bitcast.19, ...), custom_call_target="tpu_custom_call" | custom-call | flops 1 | bytes 1 | tf_op jit(solution)/shard_map/load_weights/pallas_call | solution.py:188
  39.1 1.8 %collective-permute-start.11 = (bf16[32,4096]{1,0:T(8,128)(2,1)S(1)}, bf16[32,4096]{1,0:T(8,128)(2,1)S(1)}, u32[]{:S(2)}, u32[]{:S(2)}) collective-permute-start(bf16[32,4096]{1,0:T(8,128)(2,1)S(1)} %slice.74), channel_id=1, source_target_pairs={{0,6},{2,4},{4,2},{6,0},{1,7},{3,5},{5,3},{7,1},{8,14},{10,12},{12... | collective-permute-start | bytes 786440 | tf_op jit(solution)/shard_map/ppermute | solution.py:23
  42.8 5.0 %first_units.1 = (bf16[384,512]{1,0:T(8,128)(2,1)S(1)}, bf16[384,448]{1,0:T(8,128)(2,1)S(1)}) custom-call(bf16[64,4096]{1,0:T(8,128)(2,1)S(1)} %pad_maximum_fusion._.refs_0_, bf16[64,4096]{1,0:T(8,128)(2,1)S(1)} %collective-permute-done.7.refs_1_, bf16[64,4096]{1,0:T(8,128)(2,1)S(1)} %collective-permute-done.8.refs_2_, ...), custom_call_target="tpu_custom_call" | custom-call | flops 1 | bytes 1 | tf_op jit(solution)/shard_map/first_units/pallas_call | solution.py:196
  48.0 4.7 %far_parts.1 = (bf16[64,4096]{1,0:T(8,128)(2,1)S(1)}, bf16[64,4096]{1,0:T(8,128)(2,1)S(1)}, bf16[64,4096]{1,0:T(8,128)(2,1)S(1)}, bf16[64,4096]{1,0:T(8,128)(2,1...) custom-call(bf16[32,4096]{1,0:T(8,128)(2,1)S(1)} %collective-permute, ...), custom_call_target="tpu_custom_call" | custom-call | flops 1 | bytes 1 | tf_op jit(solution)/shard_map/far_parts/pallas_call | solution.py:199
  52.6 2.1 %collective-permute-start.15 = (bf16[64,4096]{1,0:T(8,128)(2,1)S(1)}, bf16[64,4096]{1,0:T(8,128)(2,1)S(1)}, u32[]{:S(2)}, u32[]{:S(2)}) collective-permute-start(bf16[64,4096]{1,0:T(8,128)(2,1)S(1)} %get-tuple-element.65), channel_id=1, source_target_pairs={{0,24},{8,16},{16,8},{24,0},{1,25},{9,17},{17,9},{25,1},{2,26},{10... | collective-permute-start | bytes 1572872 | tf_op jit(solution)/shard_map/ppermute | solution.py:23
  56.4 5.2 %near_parts.1 = (f32[128,4096]{1,0:T(8,128)S(1)}, f32[128,4096]{1,0:T(8,128)S(1)}, f32[128,4096]{1,0:T(8,128)S(1)}, f32[128,4096]{1,0:T(8,128)S(1)}, f32[128,4096]{1,0:T(8,128)S(1)}, /*index=5*/f32[128,4096]{1,0:T(8,128)S(1)}) custom-call(bf16[512,512]{1,0:T(8,128)(2,1)S(1)} %get-tuple-element.59.feat_x, bf16[512,512]{1,0:T(8,128)(2,1)S(1)} %get-tuple-element.60.feat_y, ...), custom_call_target="tpu_custom_call" | custom-call | flops 1 | bytes 1 | tf_op jit(solution)/shard_map/near_parts/pallas_call | solution.py:205
  61.7 1.7 %collective-permute-done.15 = bf16[64,4096]{1,0:T(8,128)(2,1)S(1)} collective-permute-done((bf16[64,4096]{1,0:T(8,128)(2,1)S(1)}, bf16[64,4096]{1,0:T(8,128)(2,1)S(1)}, u32[]{:S(2)}, u32[]{:S(2)}) %collective-permute-start.15) | collective-permute-done | bytes 524320 | tf_op jit(solution)/shard_map/ppermute | solution.py:23
  64.0 1.9 %collective-permute-start.18 = (bf16[128,4096]{1,0:T(8,128)(2,1)S(1)}, bf16[128,4096]{1,0:T(8,128)(2,1)S(1)}, u32[]{:S(2)}, u32[]{:S(2)}) collective-permute-start(bf16[128,4096]{1,0:T(8,128)(2,1)S(1)} %add_convert_fusion.2), channel_id=1, source_target_pairs={{0,24},{8,16},{16,8},{24,0},{1,25},{9,17},{17,9},{25,1},{2,26},{10... | collective-permute-start | bytes 3145736 | tf_op jit(solution)/shard_map/ppermute | solution.py:23
  66.1 1.7 %collective-permute-start.23 = (bf16[128,4096]{1,0:T(8,128)(2,1)S(1)}, bf16[128,4096]{1,0:T(8,128)(2,1)S(1)}, u32[]{:S(2)}, u32[]{:S(2)}) collective-permute-start(bf16[128,4096]{1,0:T(8,128)(2,1)S(1)} %add_convert_fusion.1), channel_id=1, source_target_pairs={{0,2},{2,0},{4,6},{6,4},{1,3},{3,1},{5,7},{7,5},{8,10},{10,8},{12,... | collective-permute-start | bytes 3145736 | tf_op jit(solution)/shard_map/ppermute | solution.py:23
  68.8 19.2 %collective-permute-done.16 = bf16[128,4096]{1,0:T(8,128)(2,1)S(1)} collective-permute-done((bf16[128,4096]{1,0:T(8,128)(2,1)S(1)}, bf16[128,4096]{1,0:T(8,128)(2,1)S(1)}, u32[]{:S(2)}, u32[]{:S(2)}) %collective-permute-start.16) | collective-permute-done | bytes 1048608 | tf_op jit(solution)/shard_map/ppermute | solution.py:23
  88.5 1.5 %collective-permute-start.19 = (bf16[32,4096]{1,0:T(8,128)(2,1)S(1)}, bf16[32,4096]{1,0:T(8,128)(2,1)S(1)}, u32[]{:S(2)}, u32[]{:S(2)}) collective-permute-start(bf16[32,4096]{1,0:T(8,128)(2,1)S(1)} %get-tuple-element.83), channel_id=1, source_target_pairs={{0,2},{2,0},{4,6},{6,4},{1,3},{3,1},{5,7},{7,5},{8,10},{10,8},{12,... | collective-permute-start | bytes 786440 | tf_op jit(solution)/shard_map/ppermute | solution.py:23
  90.8 1.7 %collective-permute-start.21 = (bf16[32,4096]{1,0:T(8,128)(2,1)S(1)}, bf16[32,4096]{1,0:T(8,128)(2,1)S(1)}, u32[]{:S(2)}, u32[]{:S(2)}) collective-permute-start(bf16[32,4096]{1,0:T(8,128)(2,1)S(1)} %get-tuple-element.84), channel_id=1, source_target_pairs={{0,6},{2,4},{4,2},{6,0},{1,7},{3,5},{5,3},{7,1},{8,14},{10,12},{12... | collective-permute-start | bytes 786440 | tf_op jit(solution)/shard_map/ppermute | solution.py:23
  94.6 2.3 %collective-permute-start.28 = (bf16[32,4096]{1,0:T(8,128)(2,1)S(1)}, bf16[32,4096]{1,0:T(8,128)(2,1)S(1)}, u32[]{:S(2)}, u32[]{:S(2)}) collective-permute-start(bf16[32,4096]{1,0:T(8,128)(2,1)S(1)} %get-tuple-element.81), channel_id=1, source_target_pairs={{0,24},{8,16},{16,8},{24,0},{1,25},{9,17},{17,9},{25,1},{2,26},{10... | collective-permute-start | bytes 786440 | tf_op jit(solution)/shard_map/ppermute | solution.py:23
  96.9 5.6 %collective-permute-done.20 = bf16[32,4096]{1,0:T(8,128)(2,1)S(1)} collective-permute-done((bf16[32,4096]{1,0:T(8,128)(2,1)S(1)}, bf16[32,4096]{1,0:T(8,128)(2,1)S(1)}, u32[]{:S(2)}, u32[]{:S(2)}) %collective-permute-start.20) | collective-permute-done | bytes 262176 | tf_op jit(solution)/shard_map/ppermute | solution.py:23
  103.6 2.3 %collective-permute-start.29 = (bf16[16,8192]{1,0:T(8,128)(2,1)S(1)}, bf16[16,8192]{1,0:T(8,128)(2,1)S(1)}, u32[]{:S(2)}, u32[]{:S(2)}) collective-permute-start(bf16[16,8192]{1,0:T(8,128)(2,1)S(1)} %pad_maximum_fusion.4), channel_id=1, source_target_pairs={{0,1},{1,0},{2,3},{3,2},{4,5},{5,4},{6,7},{7,6},{8,9},{9,8},{10,11... | collective-permute-start | bytes 786440 | tf_op jit(solution)/shard_map/ppermute | solution.py:23
  105.9 9.8 %collective-permute-start.30 = (f32[16,4096]{1,0:T(8,128)S(1)}, f32[16,4096]{1,0:T(8,128)S(1)}, u32[]{:S(2)}, u32[]{:S(2)}) collective-permute-start(f32[16,4096]{1,0:T(8,128)S(1)} %pad_maximum_fusion.2), channel_id=1, source_target_pairs={{0,32},{32,64},{64,96},{1,33},{33,65},{65,97},{2,34},{34,66},{66,9... | collective-permute-start | bytes 786440 | tf_op jit(solution)/shard_map/ppermute | solution.py:227
  115.7 2.1 %collective-permute-start.31 = (bf16[16,4096]{1,0:T(8,128)(2,1)S(1)}, bf16[16,4096]{1,0:T(8,128)(2,1)S(1)}, u32[]{:S(2)}, u32[]{:S(2)}) collective-permute-start(bf16[16,4096]{1,0:T(8,128)(2,1)S(1)} %fusion.8), channel_id=1, source_target_pairs={{0,33},{1,32},{32,65},{33,64},{64,97},{65,96},{2,35},{3,34},{34,67... | collective-permute-start | bytes 393224 | tf_op jit(solution)/shard_map/ppermute | solution.py:228
  117.8 5.7 %collective-permute-done.31 = bf16[16,4096]{1,0:T(8,128)(2,1)S(1)} collective-permute-done((bf16[16,4096]{1,0:T(8,128)(2,1)S(1)}, bf16[16,4096]{1,0:T(8,128)(2,1)S(1)}, u32[]{:S(2)}, u32[]{:S(2)}) %collective-permute-start.31) | collective-permute-done | bytes 131104 | tf_op jit(solution)/shard_map/ppermute | solution.py:228
  (77 shorter events, 14.8 us)
Async XLA Ops:
  2.7 8.4 %collective-permute-start.3 = (bf16[16,4096]{1,0:T(8,128)(2,1)S(1)}, bf16[16,4096]{1,0:T(8,128)(2,1)S(1)}, u32[]{:S(2)}, u32[]{:S(2)}) collective-permute-start(bf16[16,4096]{1,0:T(8,128)(2,1)S(1)} %fusion.6), channel_id=1, source_target_pairs={{0,1},{1,0},{2,3},{3,2},{4,5},{5,4},{6,7},{7,6},{8,9},{9,8},{10,11... | collective-permute-start | bytes 393224 | tf_op jit(solution)/shard_map/ppermute | solution.py:23
  7.2 7.8 %collective-permute-start = (bf16[16,4096]{1,0:T(8,128)(2,1)S(1)}, bf16[16,4096]{1,0:T(8,128)(2,1)S(1)}, u32[]{:S(2)}, u32[]{:S(2)}) collective-permute-start(bf16[16,4096]{1,0:T(8,128)(2,1)S(1)} %fusion.6), channel_id=1, source_target_pairs={{0,8},{8,0},{16,24},{24,16},{1,9},{9,1},{17,25},{25,17},{2,10},{10... | collective-permute-start | bytes 393224 | tf_op jit(solution)/shard_map/ppermute | solution.py:23
  8.4 7.5 %collective-permute-start.1 = (bf16[16,4096]{1,0:T(8,128)(2,1)S(1)}, bf16[16,4096]{1,0:T(8,128)(2,1)S(1)}, u32[]{:S(2)}, u32[]{:S(2)}) collective-permute-start(bf16[16,4096]{1,0:T(8,128)(2,1)S(1)} %fusion.6), channel_id=1, source_target_pairs={{0,16},{8,24},{16,0},{24,8},{1,17},{9,25},{17,1},{25,9},{2,18},{10... | collective-permute-start | bytes 393224 | tf_op jit(solution)/shard_map/ppermute | solution.py:23
  10.9 7.9 %collective-permute-start.2 = (bf16[16,4096]{1,0:T(8,128)(2,1)S(1)}, bf16[16,4096]{1,0:T(8,128)(2,1)S(1)}, u32[]{:S(2)}, u32[]{:S(2)}) collective-permute-start(bf16[16,4096]{1,0:T(8,128)(2,1)S(1)} %fusion.6), channel_id=1, source_target_pairs={{0,24},{8,16},{16,8},{24,0},{1,25},{9,17},{17,9},{25,1},{2,26},{10... | collective-permute-start | bytes 393224 | tf_op jit(solution)/shard_map/ppermute | solution.py:23
  11.1 7.7 %collective-permute-start.4 = (bf16[16,4096]{1,0:T(8,128)(2,1)S(1)}, bf16[16,4096]{1,0:T(8,128)(2,1)S(1)}, u32[]{:S(2)}, u32[]{:S(2)}) collective-permute-start(bf16[16,4096]{1,0:T(8,128)(2,1)S(1)} %collective-permute-done.3), channel_id=1, source_target_pairs={{0,2},{2,0},{4,6},{6,4},{1,3},{3,1},{5,7},{7,5},{8,10},{10,8},{12,... | collective-permute-start | bytes 393224 | tf_op jit(solution)/shard_map/ppermute | solution.py:23
  12.4 6.9 %collective-permute-start.5 = (bf16[16,4096]{1,0:T(8,128)(2,1)S(1)}, bf16[16,4096]{1,0:T(8,128)(2,1)S(1)}, u32[]{:S(2)}, u32[]{:S(2)}) collective-permute-start(bf16[16,4096]{1,0:T(8,128)(2,1)S(1)} %collective-permute-done.3), channel_id=1, source_target_pairs={{0,4},{2,6},{4,0},{6,2},{1,5},{3,7},{5,1},{7,3},{8,12},{10,14},{12... | collective-permute-start | bytes 393224 | tf_op jit(solution)/shard_map/ppermute | solution.py:23
  15.0 7.0 %collective-permute-start.6 = (bf16[16,4096]{1,0:T(8,128)(2,1)S(1)}, bf16[16,4096]{1,0:T(8,128)(2,1)S(1)}, u32[]{:S(2)}, u32[]{:S(2)}) collective-permute-start(bf16[16,4096]{1,0:T(8,128)(2,1)S(1)} %collective-permute-done.3), channel_id=1, source_target_pairs={{0,6},{2,4},{4,2},{6,0},{1,7},{3,5},{5,3},{7,1},{8,14},{10,12},{12... | collective-permute-start | bytes 393224 | tf_op jit(solution)/shard_map/ppermute | solution.py:23
  22.1 17.0 %collective-permute-start.7 = (bf16[64,4096]{1,0:T(8,128)(2,1)S(1)}, bf16[64,4096]{1,0:T(8,128)(2,1)S(1)}, u32[]{:S(2)}, u32[]{:S(2)}) collective-permute-start(bf16[64,4096]{1,0:T(8,128)(2,1)S(1)} %pad_maximum_fusion._.refs_0_), channel_id=1, source_target_pairs={{0,2},{2,0},{4,6},{6,4},{1,3},{3,1},{5,7},{7,5},{8,10},{10,8},{12,... | collective-permute-start | bytes 1572872 | tf_op jit(solution)/shard_map/ppermute | solution.py:23
  22.2 16.9 %collective-permute-start.8 = (bf16[64,4096]{1,0:T(8,128)(2,1)S(1)}, bf16[64,4096]{1,0:T(8,128)(2,1)S(1)}, u32[]{:S(2)}, u32[]{:S(2)}) collective-permute-start(bf16[64,4096]{1,0:T(8,128)(2,1)S(1)} %pad_maximum_fusion._.refs_0_), channel_id=1, source_target_pairs={{0,6},{2,4},{4,2},{6,0},{1,7},{3,5},{5,3},{7,1},{8,14},{10,12},{12... | collective-permute-start | bytes 1572872 | tf_op jit(solution)/shard_map/ppermute | solution.py:23
  23.2 15.8 %collective-permute-start.10 = (bf16[64,4096]{1,0:T(8,128)(2,1)S(1)}, bf16[64,4096]{1,0:T(8,128)(2,1)S(1)}, u32[]{:S(2)}, u32[]{:S(2)}) collective-permute-start(bf16[64,4096]{1,0:T(8,128)(2,1)S(1)} %pad_maximum_fusion.1.refs_3_), channel_id=1, source_target_pairs={{0,24},{8,16},{16,8},{24,0},{1,25},{9,17},{17,9},{25,1},{2,26},{10... | collective-permute-start | bytes 1572872 | tf_op jit(solution)/shard_map/ppermute | solution.py:23
  25.7 13.4 %collective-permute-start.9 = (bf16[64,4096]{1,0:T(8,128)(2,1)S(1)}, bf16[64,4096]{1,0:T(8,128)(2,1)S(1)}, u32[]{:S(2)}, u32[]{:S(2)}) collective-permute-start(bf16[64,4096]{1,0:T(8,128)(2,1)S(1)} %pad_maximum_fusion.1.refs_3_), channel_id=1, source_target_pairs={{0,8},{8,0},{16,24},{24,16},{1,9},{9,1},{17,25},{25,17},{2,10},{10... | collective-permute-start | bytes 1572872 | tf_op jit(solution)/shard_map/ppermute | solution.py:23
  39.1 8.8 %collective-permute-start.11 = (bf16[32,4096]{1,0:T(8,128)(2,1)S(1)}, bf16[32,4096]{1,0:T(8,128)(2,1)S(1)}, u32[]{:S(2)}, u32[]{:S(2)}) collective-permute-start(bf16[32,4096]{1,0:T(8,128)(2,1)S(1)} %slice.74), channel_id=1, source_target_pairs={{0,6},{2,4},{4,2},{6,0},{1,7},{3,5},{5,3},{7,1},{8,14},{10,12},{12... | collective-permute-start | bytes 786440 | tf_op jit(solution)/shard_map/ppermute | solution.py:23
  40.9 7.0 %collective-permute-start.12 = (bf16[32,4096]{1,0:T(8,128)(2,1)S(1)}, bf16[32,4096]{1,0:T(8,128)(2,1)S(1)}, u32[]{:S(2)}, u32[]{:S(2)}) collective-permute-start(bf16[32,4096]{1,0:T(8,128)(2,1)S(1)} %slice.75), channel_id=1, source_target_pairs={{0,2},{2,0},{4,6},{6,4},{1,3},{3,1},{5,7},{7,5},{8,10},{10,8},{12,... | collective-permute-start | bytes 786440 | tf_op jit(solution)/shard_map/ppermute | solution.py:23
  41.2 6.8 %collective-permute-start.13 = (bf16[32,4096]{1,0:T(8,128)(2,1)S(1)}, bf16[32,4096]{1,0:T(8,128)(2,1)S(1)}, u32[]{:S(2)}, u32[]{:S(2)}) collective-permute-start(bf16[32,4096]{1,0:T(8,128)(2,1)S(1)} %slice.76), channel_id=1, source_target_pairs={{0,24},{8,16},{16,8},{24,0},{1,25},{9,17},{17,9},{25,1},{2,26},{10... | collective-permute-start | bytes 786440 | tf_op jit(solution)/shard_map/ppermute | solution.py:23
  42.0 6.0 %collective-permute-start.14 = (bf16[32,4096]{1,0:T(8,128)(2,1)S(1)}, bf16[32,4096]{1,0:T(8,128)(2,1)S(1)}, u32[]{:S(2)}, u32[]{:S(2)}) collective-permute-start(bf16[32,4096]{1,0:T(8,128)(2,1)S(1)} %slice.77), channel_id=1, source_target_pairs={{0,8},{8,0},{16,24},{24,16},{1,9},{9,1},{17,25},{25,17},{2,10},{10... | collective-permute-start | bytes 786440 | tf_op jit(solution)/shard_map/ppermute | solution.py:23
  52.6 10.7 %collective-permute-start.15 = (bf16[64,4096]{1,0:T(8,128)(2,1)S(1)}, bf16[64,4096]{1,0:T(8,128)(2,1)S(1)}, u32[]{:S(2)}, u32[]{:S(2)}) collective-permute-start(bf16[64,4096]{1,0:T(8,128)(2,1)S(1)} %get-tuple-element.65), channel_id=1, source_target_pairs={{0,24},{8,16},{16,8},{24,0},{1,25},{9,17},{17,9},{25,1},{2,26},{10... | collective-permute-start | bytes 1572872 | tf_op jit(solution)/shard_map/ppermute | solution.py:23
  54.7 9.1 %collective-permute-start.17 = (bf16[64,4096]{1,0:T(8,128)(2,1)S(1)}, bf16[64,4096]{1,0:T(8,128)(2,1)S(1)}, u32[]{:S(2)}, u32[]{:S(2)}) collective-permute-start(bf16[64,4096]{1,0:T(8,128)(2,1)S(1)} %get-tuple-element.67), channel_id=1, source_target_pairs={{0,8},{8,0},{16,24},{24,16},{1,9},{9,1},{17,25},{25,17},{2,10},{10... | collective-permute-start | bytes 1572872 | tf_op jit(solution)/shard_map/ppermute | solution.py:23
  54.7 11.2 %collective-permute-start.22 = (bf16[64,4096]{1,0:T(8,128)(2,1)S(1)}, bf16[64,4096]{1,0:T(8,128)(2,1)S(1)}, u32[]{:S(2)}, u32[]{:S(2)}) collective-permute-start(bf16[64,4096]{1,0:T(8,128)(2,1)S(1)} %get-tuple-element.70), channel_id=1, source_target_pairs={{0,6},{2,4},{4,2},{6,0},{1,7},{3,5},{5,3},{7,1},{8,14},{10,12},{12... | collective-permute-start | bytes 1572872 | tf_op jit(solution)/shard_map/ppermute | solution.py:23
  55.7 12.1 %collective-permute-start.24 = (bf16[64,4096]{1,0:T(8,128)(2,1)S(1)}, bf16[64,4096]{1,0:T(8,128)(2,1)S(1)}, u32[]{:S(2)}, u32[]{:S(2)}) collective-permute-start(bf16[64,4096]{1,0:T(8,128)(2,1)S(1)} %get-tuple-element.72), channel_id=1, source_target_pairs={{0,2},{2,0},{4,6},{6,4},{1,3},{3,1},{5,7},{7,5},{8,10},{10,8},{12,... | collective-permute-start | bytes 1572872 | tf_op jit(solution)/shard_map/ppermute | solution.py:23
  63.5 24.5 %collective-permute-start.16 = (bf16[128,4096]{1,0:T(8,128)(2,1)S(1)}, bf16[128,4096]{1,0:T(8,128)(2,1)S(1)}, u32[]{:S(2)}, u32[]{:S(2)}) collective-permute-start(bf16[128,4096]{1,0:T(8,128)(2,1)S(1)} %add_convert_fusion.3), channel_id=1, source_target_pairs={{0,8},{8,0},{16,24},{24,16},{1,9},{9,1},{17,25},{25,17},{2,10},{10... | collective-permute-start | bytes 3145736 | tf_op jit(solution)/shard_map/ppermute | solution.py:23
  64.0 24.0 %collective-permute-start.18 = (bf16[128,4096]{1,0:T(8,128)(2,1)S(1)}, bf16[128,4096]{1,0:T(8,128)(2,1)S(1)}, u32[]{:S(2)}, u32[]{:S(2)}) collective-permute-start(bf16[128,4096]{1,0:T(8,128)(2,1)S(1)} %add_convert_fusion.2), channel_id=1, source_target_pairs={{0,24},{8,16},{16,8},{24,0},{1,25},{9,17},{17,9},{25,1},{2,26},{10... | collective-permute-start | bytes 3145736 | tf_op jit(solution)/shard_map/ppermute | solution.py:23
  66.1 26.4 %collective-permute-start.23 = (bf16[128,4096]{1,0:T(8,128)(2,1)S(1)}, bf16[128,4096]{1,0:T(8,128)(2,1)S(1)}, u32[]{:S(2)}, u32[]{:S(2)}) collective-permute-start(bf16[128,4096]{1,0:T(8,128)(2,1)S(1)} %add_convert_fusion.1), channel_id=1, source_target_pairs={{0,2},{2,0},{4,6},{6,4},{1,3},{3,1},{5,7},{7,5},{8,10},{10,8},{12,... | collective-permute-start | bytes 3145736 | tf_op jit(solution)/shard_map/ppermute | solution.py:23
  68.0 24.5 %collective-permute-start.25 = (bf16[128,4096]{1,0:T(8,128)(2,1)S(1)}, bf16[128,4096]{1,0:T(8,128)(2,1)S(1)}, u32[]{:S(2)}, u32[]{:S(2)}) collective-permute-start(bf16[128,4096]{1,0:T(8,128)(2,1)S(1)} %add_convert_fusion), channel_id=1, source_target_pairs={{0,6},{2,4},{4,2},{6,0},{1,7},{3,5},{5,3},{7,1},{8,14},{10,12},{12... | collective-permute-start | bytes 3145736 | tf_op jit(solution)/shard_map/ppermute | solution.py:23
  88.5 6.1 %collective-permute-start.19 = (bf16[32,4096]{1,0:T(8,128)(2,1)S(1)}, bf16[32,4096]{1,0:T(8,128)(2,1)S(1)}, u32[]{:S(2)}, u32[]{:S(2)}) collective-permute-start(bf16[32,4096]{1,0:T(8,128)(2,1)S(1)} %get-tuple-element.83), channel_id=1, source_target_pairs={{0,2},{2,0},{4,6},{6,4},{1,3},{3,1},{5,7},{7,5},{8,10},{10,8},{12,... | collective-permute-start | bytes 786440 | tf_op jit(solution)/shard_map/ppermute | solution.py:23
  90.0 12.5 %collective-permute-start.20 = (bf16[32,4096]{1,0:T(8,128)(2,1)S(1)}, bf16[32,4096]{1,0:T(8,128)(2,1)S(1)}, u32[]{:S(2)}, u32[]{:S(2)}) collective-permute-start(bf16[32,4096]{1,0:T(8,128)(2,1)S(1)} %get-tuple-element.85), channel_id=1, source_target_pairs={{0,4},{2,6},{4,0},{6,2},{1,5},{3,7},{5,1},{7,3},{8,12},{10,14},{12... | collective-permute-start | bytes 786440 | tf_op jit(solution)/shard_map/ppermute | solution.py:23
  90.8 11.7 %collective-permute-start.21 = (bf16[32,4096]{1,0:T(8,128)(2,1)S(1)}, bf16[32,4096]{1,0:T(8,128)(2,1)S(1)}, u32[]{:S(2)}, u32[]{:S(2)}) collective-permute-start(bf16[32,4096]{1,0:T(8,128)(2,1)S(1)} %get-tuple-element.84), channel_id=1, source_target_pairs={{0,6},{2,4},{4,2},{6,0},{1,7},{3,5},{5,3},{7,1},{8,14},{10,12},{12... | collective-permute-start | bytes 786440 | tf_op jit(solution)/shard_map/ppermute | solution.py:23
  93.0 9.7 %collective-permute-start.26 = (bf16[32,4096]{1,0:T(8,128)(2,1)S(1)}, bf16[32,4096]{1,0:T(8,128)(2,1)S(1)}, u32[]{:S(2)}, u32[]{:S(2)}) collective-permute-start(bf16[32,4096]{1,0:T(8,128)(2,1)S(1)} %get-tuple-element.80), channel_id=1, source_target_pairs={{0,8},{8,0},{16,24},{24,16},{1,9},{9,1},{17,25},{25,17},{2,10},{10... | collective-permute-start | bytes 786440 | tf_op jit(solution)/shard_map/ppermute | solution.py:23
  93.3 9.3 %collective-permute-start.27 = (bf16[32,4096]{1,0:T(8,128)(2,1)S(1)}, bf16[32,4096]{1,0:T(8,128)(2,1)S(1)}, u32[]{:S(2)}, u32[]{:S(2)}) collective-permute-start(bf16[32,4096]{1,0:T(8,128)(2,1)S(1)} %get-tuple-element.82), channel_id=1, source_target_pairs={{0,16},{8,24},{16,0},{24,8},{1,17},{9,25},{17,1},{25,9},{2,18},{10... | collective-permute-start | bytes 786440 | tf_op jit(solution)/shard_map/ppermute | solution.py:23
  94.6 8.6 %collective-permute-start.28 = (bf16[32,4096]{1,0:T(8,128)(2,1)S(1)}, bf16[32,4096]{1,0:T(8,128)(2,1)S(1)}, u32[]{:S(2)}, u32[]{:S(2)}) collective-permute-start(bf16[32,4096]{1,0:T(8,128)(2,1)S(1)} %get-tuple-element.81), channel_id=1, source_target_pairs={{0,24},{8,16},{16,8},{24,0},{1,25},{9,17},{17,9},{25,1},{2,26},{10... | collective-permute-start | bytes 786440 | tf_op jit(solution)/shard_map/ppermute | solution.py:23
  103.6 20.0 %collective-permute-start.29 = (bf16[16,8192]{1,0:T(8,128)(2,1)S(1)}, bf16[16,8192]{1,0:T(8,128)(2,1)S(1)}, u32[]{:S(2)}, u32[]{:S(2)}) collective-permute-start(bf16[16,8192]{1,0:T(8,128)(2,1)S(1)} %pad_maximum_fusion.4), channel_id=1, source_target_pairs={{0,1},{1,0},{2,3},{3,2},{4,5},{5,4},{6,7},{7,6},{8,9},{9,8},{10,11... | collective-permute-start | bytes 786440 | tf_op jit(solution)/shard_map/ppermute | solution.py:23
  105.9 17.6 %collective-permute-start.30 = (f32[16,4096]{1,0:T(8,128)S(1)}, f32[16,4096]{1,0:T(8,128)S(1)}, u32[]{:S(2)}, u32[]{:S(2)}) collective-permute-start(f32[16,4096]{1,0:T(8,128)S(1)} %pad_maximum_fusion.2), channel_id=1, source_target_pairs={{0,32},{32,64},{64,96},{1,33},{33,65},{65,97},{2,34},{34,66},{66,9... | collective-permute-start | bytes 786440 | tf_op jit(solution)/shard_map/ppermute | solution.py:227
  115.7 7.8 %collective-permute-start.31 = (bf16[16,4096]{1,0:T(8,128)(2,1)S(1)}, bf16[16,4096]{1,0:T(8,128)(2,1)S(1)}, u32[]{:S(2)}, u32[]{:S(2)}) collective-permute-start(bf16[16,4096]{1,0:T(8,128)(2,1)S(1)} %fusion.8), channel_id=1, source_target_pairs={{0,33},{1,32},{32,65},{33,64},{64,97},{65,96},{2,35},{3,34},{34,67... | collective-permute-start | bytes 393224 | tf_op jit(solution)/shard_map/ppermute | solution.py:228
  (7 other events, 35.7 us)

commit v3 on v2

--- a/solution.py
+++ b/solution.py
@@ -71,6 +71,12 @@
     gates = dot_t(tokens, gate[...])
     ups = dot_t(tokens, up[...])
     return (gates / (1.0 + jnp.exp(-gates)) * ups).astype(BF)
+
+
+def norm_kernel(resid, gain, out):
+    stream = resid[...].astype(F32)
+    inv_rms = lax.rsqrt(jnp.mean(stream * stream, axis=1, keepdims=True) + 1e-05)
+    out[...] = (stream * inv_rms * gain[...]).astype(BF)
 
 
 def load_kernel(_, *refs):
@@ -155,20 +161,6 @@
     width = resid.shape[2]
     half = width // 2
     block = 8 * rows
-    stream = resid[0].astype(F32)
-    inv_rms = lax.rsqrt(jnp.mean(stream * stream, axis=1, keepdims=True) + 1e-05)
-    normed = (stream * inv_rms * norm_gain[0]).astype(BF)
-
-    other = swap(normed, FZ, 1)
-    plane = jnp.concatenate([normed] + [swap(normed, FX, r) for r in (1, 2, 3)], axis=0)
-    other_plane = jnp.concatenate([other] + [swap(other, FY, r) for r in (1, 2, 3)], axis=0)
-    plane, other_plane = tie(plane, other_plane)
-    own_early = ring_gather(plane, FY)
-    oth_early = ring_gather(other_plane, FX)
-
-    enc, dec, down, gate, up = w_enc[0], w_dec[0], w_down[0], w_gate[0].T, w_up[0].T
-    features, hidden = enc.shape[1], down.shape[0]
-
     def shape(count, cols, dtype=BF):
         return jax.ShapeDtypeStruct((count, cols), dtype)
 
@@ -184,13 +176,28 @@
             name=name,
         )
 
-    weights = (enc, gate, up, down, dec)
-    enc, gate, up, down, dec = call(
-        load_kernel, "load_weights", [VMEM] + [HBM] * 5, [shape(*w.shape) for w in weights],
-        [pltpu.SemaphoreType.DMA((5,))], 4,
+    def norm(stream):
+        return call(norm_kernel, "norm", [VMEM] * 2, [shape(rows, width)], [], 4)(stream, norm_gain)[0]
+
+    other = swap(resid[0], FZ, 1)
+    normed = norm(resid[0])
+    other = norm(other)
+    plane = jnp.concatenate([normed] + [swap(normed, FX, r) for r in (1, 2, 3)], axis=0)
+    other_plane = jnp.concatenate([other] + [swap(other, FY, r) for r in (1, 2, 3)], axis=0)
+    plane = tie(plane, other)[0]
+    own_early = ring_gather(plane, FY)
+    oth_early = ring_gather(other_plane, FX)
+
+    enc, dec, down, gate, up = w_enc[0], w_dec[0], w_down[0], w_gate[0].T, w_up[0].T
+    features, hidden = enc.shape[1], down.shape[0]
+
+    weights = (enc, gate, up)
+    enc, gate, up = call(
+        load_kernel, "load_weights", [VMEM] + [HBM] * 3, [shape(*w.shape) for w in weights],
+        [pltpu.SemaphoreType.DMA((3,))], 4,
     )(plane, *weights)
-    *late, enc, gate, up, down, dec = tie(*own_early, *oth_early, enc, gate, up, down, dec)
-    own_early, oth_early = late[:3], late[3:]
+    *own_early, enc, gate, up = tie(*own_early, enc, gate, up)
+    *oth_early, enc, gate, up = tie(*oth_early, enc, gate, up)
     own_late, oth_late = ring_relay(own_early, FY), ring_relay(oth_early, FX)
     early = 24 * rows
     feat, hid = call(

time: 125 us -> 121 us (0.968)
  local copies, waits for them, and re-layouts: 12 us -> 8.2 us
  other arithmetic: 4.99 us -> 2.92 us
  waiting for transfers between devices: 41.1 us -> 42.5 us
  starting transfers between devices: 48.9 us -> 50.2 us
    unnamed x14 -> x20, local copies, waits for them, and re-layouts: 11.7 us -> 7.95 us
    ppermute x30, waiting for transfers between devices: 35.4 us -> 38.2 us  [swap(): return lax.ppermute(value, axis, [(i, i ^ distance) for i in range(count)])]
    ppermute x1, starting transfers between devices: 2.07 us -> 4.02 us  [body(): lax.ppermute(fwd_oth, ('grp', FZ), crossed)]
    ppermute x1, waiting for transfers between devices: 5.71 us -> 4.39 us  [body(): lax.ppermute(fwd_oth, ('grp', FZ), crossed)]
  transfers between devices with their start and end apart: 32 -> 32, of which waited for: 12 -> 12; matrix products, arithmetic and copies ran while one was open for 2% -> 2% of each run, Pallas kernels for 10% -> 9%
where the time goes in v3:
time: 121 us
  starting transfers between devices  50.2 us (41%)
  waiting for transfers between devices  42.5 us (35%)
  Pallas kernels  16 us (13%)
  local copies, waits for them, and re-layouts  8.2 us (7%)
  other arithmetic  2.92 us (2%)
    ppermute x30, waiting for transfers between devices, swap(): return lax.ppermute(value, axis, [(i, i ^ distance) for i in range(count)])  38.2 us
    ppermute x30, starting transfers between devices, swap(): return lax.ppermute(value, axis, [(i, i ^ distance) for i in range(count)])  36.9 us
    ppermute x1, starting transfers between devices, body(): lax.ppermute(fwd_own, 'grp', onward)  9.29 us
    unnamed x20, local copies, waits for them, and re-layouts  7.95 us
    pallas_call x1, Pallas kernels, body(): call(functools.partial(near_kernel, rows), 'near_parts', [VMEM] * 6, [sha...  5.14 us
    pallas_call x1, Pallas kernels, body(): call(first_kernel, 'first_units', [VMEM] * 10, [shape(early, features), s...  5.07 us
    pallas_call x1, Pallas kernels, body(): call(functools.partial(far_kernel, rows), 'far_parts', [VMEM] * 12, [shap...  4.68 us
    ppermute x1, waiting for transfers between devices, body(): lax.ppermute(fwd_oth, ('grp', FZ), crossed)  4.39 us
  transfers between devices with their start and end apart: 32, of which 12 were waited for; matrix products, arithmetic and copies ran while one was open for 2% of the time, Pallas kernels for 9%

profile of v3, /device:TPU:1, one launch (start us, length us, event | category | flops | bytes accessed | tf_op | source)
XLA Modules:
  0.0 120.9 jit_solution(4655252503834392809)
XLA Ops:
  0.6 4.5 %collective-permute-start.3 = (bf16[16,4096]{1,0:T(8,128)(2,1)}, bf16[16,4096]{1,0:T(8,128)(2,1)S(1)}, u32[]{:S(2)}, u32[]{:S(2)}) collective-permute-start(bf16[16,4096]{1,0:T(8,128)(2,1)} %bitcast.23), channel_id=1, source_target_pairs={{0,1},{1,0},{2,3},{3,2},{4,5},{5,4},{6,7},{7,6},{8,9},{9,8},{10,11... | collective-permute-start | bytes 393224 | tf_op jit(solution)/shard_map/ppermute | solution.py:23
  6.9 1.3 %collective-permute-start = (bf16[16,4096]{1,0:T(8,128)(2,1)S(1)}, bf16[16,4096]{1,0:T(8,128)(2,1)S(1)}, u32[]{:S(2)}, u32[]{:S(2)}) collective-permute-start(bf16[16,4096]{1,0:T(8,128)(2,1)S(1)} %norm.2), channel_id=1, source_target_pairs={{0,8},{8,0},{16,24},{24,16},{1,9},{9,1},{17,25},{25,17},{2,10},{10... | collective-permute-start | bytes 393224 | tf_op jit(solution)/shard_map/ppermute | solution.py:23
  8.2 2.5 %collective-permute-start.1 = (bf16[16,4096]{1,0:T(8,128)(2,1)S(1)}, bf16[16,4096]{1,0:T(8,128)(2,1)S(1)}, u32[]{:S(2)}, u32[]{:S(2)}) collective-permute-start(bf16[16,4096]{1,0:T(8,128)(2,1)S(1)} %norm.2), channel_id=1, source_target_pairs={{0,16},{8,24},{16,0},{24,8},{1,17},{9,25},{17,1},{25,9},{2,18},{10... | collective-permute-start | bytes 393224 | tf_op jit(solution)/shard_map/ppermute | solution.py:23
  11.0 2.8 %collective-permute-start.10 = (bf16[16,4096]{1,0:T(8,128)(2,1)S(1)}, bf16[16,4096]{1,0:T(8,128)(2,1)S(1)}, u32[]{:S(2)}, u32[]{:S(2)}) collective-permute-start(bf16[16,4096]{1,0:T(8,128)(2,1)S(1)} %norm.3), channel_id=1, source_target_pairs={{0,6},{2,4},{4,2},{6,0},{1,7},{3,5},{5,3},{7,1},{8,14},{10,12},{12... | collective-permute-start | bytes 393224 | tf_op jit(solution)/shard_map/ppermute | solution.py:23
  13.9 1.3 %collective-permute-start.9 = (bf16[16,4096]{1,0:T(8,128)(2,1)S(1)}, bf16[16,4096]{1,0:T(8,128)(2,1)S(1)}, u32[]{:S(2)}, u32[]{:S(2)}) collective-permute-start(bf16[16,4096]{1,0:T(8,128)(2,1)S(1)} %norm.3), channel_id=1, source_target_pairs={{0,4},{2,6},{4,0},{6,2},{1,5},{3,7},{5,1},{7,3},{8,12},{10,14},{12... | collective-permute-start | bytes 393224 | tf_op jit(solution)/shard_map/ppermute | solution.py:23
  15.8 2.8 %collective-permute-done.2 = bf16[16,4096]{1,0:T(8,128)(2,1)S(1)} collective-permute-done((bf16[16,4096]{1,0:T(8,128)(2,1)S(1)}, bf16[16,4096]{1,0:T(8,128)(2,1)S(1)}, u32[]{:S(2)}, u32[]{:S(2)}) %collective-permute-start.2) | collective-permute-done | bytes 131104 | tf_op jit(solution)/shard_map/ppermute | solution.py:23
  18.6 1.4 %collective-permute-start.4 = (bf16[64,4096]{1,0:T(8,128)(2,1)S(1)}, bf16[64,4096]{1,0:T(8,128)(2,1)S(1)}, u32[]{:S(2)}, u32[]{:S(2)}) collective-permute-start(bf16[64,4096]{1,0:T(8,128)(2,1)S(1)} %pad_maximum_fusion._.refs_0_), channel_id=1, source_target_pairs={{0,2},{2,0},{4,6},{6,4},{1,3},{3,1},{5,7},{7,5},{8,10},{10,8},{12,... | collective-permute-start | bytes 1572872 | tf_op jit(solution)/shard_map/ppermute | solution.py:23
  20.0 1.9 %collective-permute-start.5 = (bf16[64,4096]{1,0:T(8,128)(2,1)S(1)}, bf16[64,4096]{1,0:T(8,128)(2,1)S(1)}, u32[]{:S(2)}, u32[]{:S(2)}) collective-permute-start(bf16[64,4096]{1,0:T(8,128)(2,1)S(1)} %pad_maximum_fusion._.refs_0_), channel_id=1, source_target_pairs={{0,6},{2,4},{4,2},{6,0},{1,7},{3,5},{5,3},{7,1},{8,14},{10,12},{12... | collective-permute-start | bytes 1572872 | tf_op jit(solution)/shard_map/ppermute | solution.py:23
  22.1 1.0 collective-permute-start.12
  23.1 2.2 %copy-done.1 = bf16[1,4096,512]{2,1,0:T(8,128)(2,1)S(1)} copy-done((bf16[1,4096,512]{2,1,0:T(8,128)(2,1)S(1)}, bf16[1,4096,512]{2,1,0:T(8,128)(2,1)}, u32[]{:S(2)}) %copy-start.1) | copy-done | bytes 4194328
  25.3 2.0 %copy-done.2 = bf16[1,4096,448]{1,2,0:T(8,128)(2,1)S(1)} copy-done((bf16[1,4096,448]{1,2,0:T(8,128)(2,1)S(1)}, bf16[1,4096,448]{1,2,0:T(8,128)(2,1)}, u32[]{:S(2)}) %copy-start.2) | copy-done | bytes 3670040
  27.3 2.0 %copy-done.3 = bf16[1,4096,448]{1,2,0:T(8,128)(2,1)S(1)} copy-done((bf16[1,4096,448]{1,2,0:T(8,128)(2,1)S(1)}, bf16[1,4096,448]{1,2,0:T(8,128)(2,1)}, u32[]{:S(2)}) %copy-start.3) | copy-done | bytes 3670040
  30.2 2.2 %collective-permute-done.4.refs_1_ = bf16[64,4096]{1,0:T(8,128)(2,1)S(1)} collective-permute-done((bf16[64,4096]{1,0:T(8,128)(2,1)S(1)}, bf16[64,4096]{1,0:T(8,128)(2,1)S(1)}, u32[]{:S(2)}, u32[]{:S(2)}) %collective-permute-start.4) | collective-permute-done | bytes 524320 | tf_op jit(solution)/shard_map/ppermute | solution.py:23
  33.0 2.0 %collective-permute-start.6 = (bf16[32,4096]{1,0:T(8,128)(2,1)S(1)}, bf16[32,4096]{1,0:T(8,128)(2,1)S(1)}, u32[]{:S(2)}, u32[]{:S(2)}) collective-permute-start(bf16[32,4096]{1,0:T(8,128)(2,1)S(1)} %slice.74), channel_id=1, source_target_pairs={{0,6},{2,4},{4,2},{6,0},{1,7},{3,5},{5,3},{7,1},{8,14},{10,12},{12... | collective-permute-start | bytes 786440 | tf_op jit(solution)/shard_map/ppermute | solution.py:23
  35.2 3.6 %collective-permute-start.13 = (bf16[32,4096]{1,0:T(8,128)(2,1)S(1)}, bf16[32,4096]{1,0:T(8,128)(2,1)S(1)}, u32[]{:S(2)}, u32[]{:S(2)}) collective-permute-start(bf16[32,4096]{1,0:T(8,128)(2,1)S(1)} %slice.76), channel_id=1, source_target_pairs={{0,24},{8,16},{16,8},{24,0},{1,25},{9,17},{17,9},{25,1},{2,26},{10... | collective-permute-start | bytes 786440 | tf_op jit(solution)/shard_map/ppermute | solution.py:23
  38.9 5.1 %first_units.1 = (bf16[384,512]{1,0:T(8,128)(2,1)S(1)}, bf16[384,448]{1,0:T(8,128)(2,1)S(1)}) custom-call(bf16[64,4096]{1,0:T(8,128)(2,1)S(1)} %pad_maximum_fusion._.refs_0_, bf16[64,4096]{1,0:T(8,128)(2,1)S(1)} %collective-permute-done.4.refs_1_, bf16[64,4096]{1,0:T(8,128)(2,1)S(1)} %collective-permute-done.5.refs_2_, ...), custom_call_target="tpu_custom_call" | custom-call | flops 1 | bytes 1 | tf_op jit(solution)/shard_map/first_units/pallas_call | solution.py:203
  44.8 4.7 %far_parts.1 = (bf16[64,4096]{1,0:T(8,128)(2,1)S(1)}, bf16[64,4096]{1,0:T(8,128)(2,1)S(1)}, bf16[64,4096]{1,0:T(8,128)(2,1)S(1)}, bf16[64,4096]{1,0:T(8,128)(2,1...) custom-call(bf16[32,4096]{1,0:T(8,128)(2,1)S(1)} %collective-permute, ...), custom_call_target="tpu_custom_call" | custom-call | flops 1 | bytes 1 | tf_op jit(solution)/shard_map/far_parts/pallas_call | solution.py:206
  49.5 1.5 %collective-permute-start.15 = (bf16[64,4096]{1,0:T(8,128)(2,1)S(1)}, bf16[64,4096]{1,0:T(8,128)(2,1)S(1)}, u32[]{:S(2)}, u32[]{:S(2)}) collective-permute-start(bf16[64,4096]{1,0:T(8,128)(2,1)S(1)} %get-tuple-element.61), channel_id=1, source_target_pairs={{0,24},{8,16},{16,8},{24,0},{1,25},{9,17},{17,9},{25,1},{2,26},{10... | collective-permute-start | bytes 1572872 | tf_op jit(solution)/shard_map/ppermute | solution.py:23
  51.0 1.1 collective-permute-start.24
  52.1 5.1 %near_parts.1 = (f32[128,4096]{1,0:T(8,128)S(1)}, f32[128,4096]{1,0:T(8,128)S(1)}, f32[128,4096]{1,0:T(8,128)S(1)}, f32[128,4096]{1,0:T(8,128)S(1)}, f32[128,4096]{1,0:T(8,128)S(1)}, /*index=5*/f32[128,4096]{1,0:T(8,128)S(1)}) custom-call(bf16[512,512]{1,0:T(8,128)(2,1)S(1)} %get-tuple-element.55.feat_x, bf16[512,512]{1,0:T(8,128)(2,1)S(1)} %get-tuple-element.56.feat_y, ...), custom_call_target="tpu_custom_call" | custom-call | flops 1 | bytes 1 | tf_op jit(solution)/shard_map/near_parts/pallas_call | solution.py:212
  57.3 4.1 %collective-permute-done.15 = bf16[64,4096]{1,0:T(8,128)(2,1)S(1)} collective-permute-done((bf16[64,4096]{1,0:T(8,128)(2,1)S(1)}, bf16[64,4096]{1,0:T(8,128)(2,1)S(1)}, u32[]{:S(2)}, u32[]{:S(2)}) %collective-permute-start.15) | collective-permute-done | bytes 524320 | tf_op jit(solution)/shard_map/ppermute | solution.py:23
  62.0 1.6 %collective-permute-start.18 = (bf16[128,4096]{1,0:T(8,128)(2,1)S(1)}, bf16[128,4096]{1,0:T(8,128)(2,1)S(1)}, u32[]{:S(2)}, u32[]{:S(2)}) collective-permute-start(bf16[128,4096]{1,0:T(8,128)(2,1)S(1)} %add_convert_fusion.2), channel_id=1, source_target_pairs={{0,24},{8,16},{16,8},{24,0},{1,25},{9,17},{17,9},{25,1},{2,26},{10... | collective-permute-start | bytes 3145736 | tf_op jit(solution)/shard_map/ppermute | solution.py:23
  63.8 1.0 collective-permute-start.23
  65.7 18.0 %collective-permute-done.16 = bf16[128,4096]{1,0:T(8,128)(2,1)S(1)} collective-permute-done((bf16[128,4096]{1,0:T(8,128)(2,1)S(1)}, bf16[128,4096]{1,0:T(8,128)(2,1)S(1)}, u32[]{:S(2)}, u32[]{:S(2)}) %collective-permute-start.16) | collective-permute-done | bytes 1048608 | tf_op jit(solution)/shard_map/ppermute | solution.py:23
  84.5 0.9 collective-permute-start.19
  85.8 2.6 %collective-permute-start.21 = (bf16[32,4096]{1,0:T(8,128)(2,1)S(1)}, bf16[32,4096]{1,0:T(8,128)(2,1)S(1)}, u32[]{:S(2)}, u32[]{:S(2)}) collective-permute-start(bf16[32,4096]{1,0:T(8,128)(2,1)S(1)} %get-tuple-element.80), channel_id=1, source_target_pairs={{0,6},{2,4},{4,2},{6,0},{1,7},{3,5},{5,3},{7,1},{8,14},{10,12},{12... | collective-permute-start | bytes 786440 | tf_op jit(solution)/shard_map/ppermute | solution.py:23
  89.1 3.2 %collective-permute-start.27 = (bf16[32,4096]{1,0:T(8,128)(2,1)S(1)}, bf16[32,4096]{1,0:T(8,128)(2,1)S(1)}, u32[]{:S(2)}, u32[]{:S(2)}) collective-permute-start(bf16[32,4096]{1,0:T(8,128)(2,1)S(1)} %get-tuple-element.78), channel_id=1, source_target_pairs={{0,16},{8,24},{16,0},{24,8},{1,17},{9,25},{17,1},{25,9},{2,18},{10... | collective-permute-start | bytes 786440 | tf_op jit(solution)/shard_map/ppermute | solution.py:23
  93.0 5.2 %collective-permute-done.20 = bf16[32,4096]{1,0:T(8,128)(2,1)S(1)} collective-permute-done((bf16[32,4096]{1,0:T(8,128)(2,1)S(1)}, bf16[32,4096]{1,0:T(8,128)(2,1)S(1)}, u32[]{:S(2)}, u32[]{:S(2)}) %collective-permute-start.20) | collective-permute-done | bytes 262176 | tf_op jit(solution)/shard_map/ppermute | solution.py:23
  99.2 2.6 %collective-permute-done.28 = bf16[32,4096]{1,0:T(8,128)(2,1)S(1)} collective-permute-done((bf16[32,4096]{1,0:T(8,128)(2,1)S(1)}, bf16[32,4096]{1,0:T(8,128)(2,1)S(1)}, u32[]{:S(2)}, u32[]{:S(2)}) %collective-permute-start.28) | collective-permute-done | bytes 262176 | tf_op jit(solution)/shard_map/ppermute | solution.py:23
  102.2 9.3 %collective-permute-start.30 = (f32[16,4096]{1,0:T(8,128)S(1)}, f32[16,4096]{1,0:T(8,128)S(1)}, u32[]{:S(2)}, u32[]{:S(2)}) collective-permute-start(f32[16,4096]{1,0:T(8,128)S(1)} %pad_maximum_fusion.2), channel_id=1, source_target_pairs={{0,32},{32,64},{64,96},{1,33},{33,65},{65,97},{2,34},{34,66},{66,9... | collective-permute-start | bytes 786440 | tf_op jit(solution)/shard_map/ppermute | solution.py:234
  111.5 4.0 %collective-permute-start.31 = (bf16[16,4096]{1,0:T(8,128)(2,1)S(1)}, bf16[16,4096]{1,0:T(8,128)(2,1)S(1)}, u32[]{:S(2)}, u32[]{:S(2)}) collective-permute-start(bf16[16,4096]{1,0:T(8,128)(2,1)S(1)} %fusion.5), channel_id=1, source_target_pairs={{0,33},{1,32},{32,65},{33,64},{64,97},{65,96},{2,35},{3,34},{34,67... | collective-permute-start | bytes 393224 | tf_op jit(solution)/shard_map/ppermute | solution.py:235
  115.5 4.4 %collective-permute-done.31 = bf16[16,4096]{1,0:T(8,128)(2,1)S(1)} collective-permute-done((bf16[16,4096]{1,0:T(8,128)(2,1)S(1)}, bf16[16,4096]{1,0:T(8,128)(2,1)S(1)}, u32[]{:S(2)}, u32[]{:S(2)}) %collective-permute-start.31) | collective-permute-done | bytes 131104 | tf_op jit(solution)/shard_map/ppermute | solution.py:235
  (83 shorter events, 11.9 us)
Async XLA Ops:
  0.6 10.3 %collective-permute-start.3 = (bf16[16,4096]{1,0:T(8,128)(2,1)}, bf16[16,4096]{1,0:T(8,128)(2,1)S(1)}, u32[]{:S(2)}, u32[]{:S(2)}) collective-permute-start(bf16[16,4096]{1,0:T(8,128)(2,1)} %bitcast.23), channel_id=1, source_target_pairs={{0,1},{1,0},{2,3},{3,2},{4,5},{5,4},{6,7},{7,6},{8,9},{9,8},{10,11... | collective-permute-start | bytes 393224 | tf_op jit(solution)/shard_map/ppermute | solution.py:23
  6.9 6.9 %collective-permute-start = (bf16[16,4096]{1,0:T(8,128)(2,1)S(1)}, bf16[16,4096]{1,0:T(8,128)(2,1)S(1)}, u32[]{:S(2)}, u32[]{:S(2)}) collective-permute-start(bf16[16,4096]{1,0:T(8,128)(2,1)S(1)} %norm.2), channel_id=1, source_target_pairs={{0,8},{8,0},{16,24},{24,16},{1,9},{9,1},{17,25},{25,17},{2,10},{10... | collective-permute-start | bytes 393224 | tf_op jit(solution)/shard_map/ppermute | solution.py:23
  8.2 7.5 %collective-permute-start.1 = (bf16[16,4096]{1,0:T(8,128)(2,1)S(1)}, bf16[16,4096]{1,0:T(8,128)(2,1)S(1)}, u32[]{:S(2)}, u32[]{:S(2)}) collective-permute-start(bf16[16,4096]{1,0:T(8,128)(2,1)S(1)} %norm.2), channel_id=1, source_target_pairs={{0,16},{8,24},{16,0},{24,8},{1,17},{9,25},{17,1},{25,9},{2,18},{10... | collective-permute-start | bytes 393224 | tf_op jit(solution)/shard_map/ppermute | solution.py:23
  10.7 7.9 %collective-permute-start.2 = (bf16[16,4096]{1,0:T(8,128)(2,1)S(1)}, bf16[16,4096]{1,0:T(8,128)(2,1)S(1)}, u32[]{:S(2)}, u32[]{:S(2)}) collective-permute-start(bf16[16,4096]{1,0:T(8,128)(2,1)S(1)} %norm.2), channel_id=1, source_target_pairs={{0,24},{8,16},{16,8},{24,0},{1,25},{9,17},{17,9},{25,1},{2,26},{10... | collective-permute-start | bytes 393224 | tf_op jit(solution)/shard_map/ppermute | solution.py:23
  11.0 10.9 %collective-permute-start.10 = (bf16[16,4096]{1,0:T(8,128)(2,1)S(1)}, bf16[16,4096]{1,0:T(8,128)(2,1)S(1)}, u32[]{:S(2)}, u32[]{:S(2)}) collective-permute-start(bf16[16,4096]{1,0:T(8,128)(2,1)S(1)} %norm.3), channel_id=1, source_target_pairs={{0,6},{2,4},{4,2},{6,0},{1,7},{3,5},{5,3},{7,1},{8,14},{10,12},{12... | collective-permute-start | bytes 393224 | tf_op jit(solution)/shard_map/ppermute | solution.py:23
  13.9 8.1 %collective-permute-start.8 = (bf16[16,4096]{1,0:T(8,128)(2,1)S(1)}, bf16[16,4096]{1,0:T(8,128)(2,1)S(1)}, u32[]{:S(2)}, u32[]{:S(2)}) collective-permute-start(bf16[16,4096]{1,0:T(8,128)(2,1)S(1)} %norm.3), channel_id=1, source_target_pairs={{0,2},{2,0},{4,6},{6,4},{1,3},{3,1},{5,7},{7,5},{8,10},{10,8},{12,... | collective-permute-start | bytes 393224 | tf_op jit(solution)/shard_map/ppermute | solution.py:23
  13.9 8.1 %collective-permute-start.9 = (bf16[16,4096]{1,0:T(8,128)(2,1)S(1)}, bf16[16,4096]{1,0:T(8,128)(2,1)S(1)}, u32[]{:S(2)}, u32[]{:S(2)}) collective-permute-start(bf16[16,4096]{1,0:T(8,128)(2,1)S(1)} %norm.3), channel_id=1, source_target_pairs={{0,4},{2,6},{4,0},{6,2},{1,5},{3,7},{5,1},{7,3},{8,12},{10,14},{12... | collective-permute-start | bytes 393224 | tf_op jit(solution)/shard_map/ppermute | solution.py:23
  18.6 13.8 %collective-permute-start.4 = (bf16[64,4096]{1,0:T(8,128)(2,1)S(1)}, bf16[64,4096]{1,0:T(8,128)(2,1)S(1)}, u32[]{:S(2)}, u32[]{:S(2)}) collective-permute-start(bf16[64,4096]{1,0:T(8,128)(2,1)S(1)} %pad_maximum_fusion._.refs_0_), channel_id=1, source_target_pairs={{0,2},{2,0},{4,6},{6,4},{1,3},{3,1},{5,7},{7,5},{8,10},{10,8},{12,... | collective-permute-start | bytes 1572872 | tf_op jit(solution)/shard_map/ppermute | solution.py:23
  20.0 13.0 %collective-permute-start.5 = (bf16[64,4096]{1,0:T(8,128)(2,1)S(1)}, bf16[64,4096]{1,0:T(8,128)(2,1)S(1)}, u32[]{:S(2)}, u32[]{:S(2)}) collective-permute-start(bf16[64,4096]{1,0:T(8,128)(2,1)S(1)} %pad_maximum_fusion._.refs_0_), channel_id=1, source_target_pairs={{0,6},{2,4},{4,2},{6,0},{1,7},{3,5},{5,3},{7,1},{8,14},{10,12},{12... | collective-permute-start | bytes 1572872 | tf_op jit(solution)/shard_map/ppermute | solution.py:23
  22.0 13.1 %collective-permute-start.11 = (bf16[64,4096]{1,0:T(8,128)(2,1)S(1)}, bf16[64,4096]{1,0:T(8,128)(2,1)S(1)}, u32[]{:S(2)}, u32[]{:S(2)}) collective-permute-start(bf16[64,4096]{1,0:T(8,128)(2,1)S(1)} %pad_maximum_fusion.1.refs_3_), channel_id=1, source_target_pairs={{0,8},{8,0},{16,24},{24,16},{1,9},{9,1},{17,25},{25,17},{2,10},{10... | collective-permute-start | bytes 1572872 | tf_op jit(solution)/shard_map/ppermute | solution.py:23
  22.1 13.1 %collective-permute-start.12 = (bf16[64,4096]{1,0:T(8,128)(2,1)S(1)}, bf16[64,4096]{1,0:T(8,128)(2,1)S(1)}, u32[]{:S(2)}, u32[]{:S(2)}) collective-permute-start(bf16[64,4096]{1,0:T(8,128)(2,1)S(1)} %pad_maximum_fusion.1.refs_3_), channel_id=1, source_target_pairs={{0,24},{8,16},{16,8},{24,0},{1,25},{9,17},{17,9},{25,1},{2,26},{10... | collective-permute-start | bytes 1572872 | tf_op jit(solution)/shard_map/ppermute | solution.py:23
  33.0 11.0 %collective-permute-start.6 = (bf16[32,4096]{1,0:T(8,128)(2,1)S(1)}, bf16[32,4096]{1,0:T(8,128)(2,1)S(1)}, u32[]{:S(2)}, u32[]{:S(2)}) collective-permute-start(bf16[32,4096]{1,0:T(8,128)(2,1)S(1)} %slice.74), channel_id=1, source_target_pairs={{0,6},{2,4},{4,2},{6,0},{1,7},{3,5},{5,3},{7,1},{8,14},{10,12},{12... | collective-permute-start | bytes 786440 | tf_op jit(solution)/shard_map/ppermute | solution.py:23
  35.0 9.0 %collective-permute-start.7 = (bf16[32,4096]{1,0:T(8,128)(2,1)S(1)}, bf16[32,4096]{1,0:T(8,128)(2,1)S(1)}, u32[]{:S(2)}, u32[]{:S(2)}) collective-permute-start(bf16[32,4096]{1,0:T(8,128)(2,1)S(1)} %slice.75), channel_id=1, source_target_pairs={{0,2},{2,0},{4,6},{6,4},{1,3},{3,1},{5,7},{7,5},{8,10},{10,8},{12,... | collective-permute-start | bytes 786440 | tf_op jit(solution)/shard_map/ppermute | solution.py:23
  35.2 8.9 %collective-permute-start.13 = (bf16[32,4096]{1,0:T(8,128)(2,1)S(1)}, bf16[32,4096]{1,0:T(8,128)(2,1)S(1)}, u32[]{:S(2)}, u32[]{:S(2)}) collective-permute-start(bf16[32,4096]{1,0:T(8,128)(2,1)S(1)} %slice.76), channel_id=1, source_target_pairs={{0,24},{8,16},{16,8},{24,0},{1,25},{9,17},{17,9},{25,1},{2,26},{10... | collective-permute-start | bytes 786440 | tf_op jit(solution)/shard_map/ppermute | solution.py:23
  38.8 6.0 %collective-permute-start.14 = (bf16[32,4096]{1,0:T(8,128)(2,1)S(1)}, bf16[32,4096]{1,0:T(8,128)(2,1)S(1)}, u32[]{:S(2)}, u32[]{:S(2)}) collective-permute-start(bf16[32,4096]{1,0:T(8,128)(2,1)S(1)} %slice.77), channel_id=1, source_target_pairs={{0,8},{8,0},{16,24},{24,16},{1,9},{9,1},{17,25},{25,17},{2,10},{10... | collective-permute-start | bytes 786440 | tf_op jit(solution)/shard_map/ppermute | solution.py:23
  49.5 11.9 %collective-permute-start.15 = (bf16[64,4096]{1,0:T(8,128)(2,1)S(1)}, bf16[64,4096]{1,0:T(8,128)(2,1)S(1)}, u32[]{:S(2)}, u32[]{:S(2)}) collective-permute-start(bf16[64,4096]{1,0:T(8,128)(2,1)S(1)} %get-tuple-element.61), channel_id=1, source_target_pairs={{0,24},{8,16},{16,8},{24,0},{1,25},{9,17},{17,9},{25,1},{2,26},{10... | collective-permute-start | bytes 1572872 | tf_op jit(solution)/shard_map/ppermute | solution.py:23
  51.0 10.8 %collective-permute-start.17 = (bf16[64,4096]{1,0:T(8,128)(2,1)S(1)}, bf16[64,4096]{1,0:T(8,128)(2,1)S(1)}, u32[]{:S(2)}, u32[]{:S(2)}) collective-permute-start(bf16[64,4096]{1,0:T(8,128)(2,1)S(1)} %get-tuple-element.63), channel_id=1, source_target_pairs={{0,8},{8,0},{16,24},{24,16},{1,9},{9,1},{17,25},{25,17},{2,10},{10... | collective-permute-start | bytes 1572872 | tf_op jit(solution)/shard_map/ppermute | solution.py:23
  51.0 12.7 %collective-permute-start.22 = (bf16[64,4096]{1,0:T(8,128)(2,1)S(1)}, bf16[64,4096]{1,0:T(8,128)(2,1)S(1)}, u32[]{:S(2)}, u32[]{:S(2)}) collective-permute-start(bf16[64,4096]{1,0:T(8,128)(2,1)S(1)} %get-tuple-element.66), channel_id=1, source_target_pairs={{0,6},{2,4},{4,2},{6,0},{1,7},{3,5},{5,3},{7,1},{8,14},{10,12},{12... | collective-permute-start | bytes 1572872 | tf_op jit(solution)/shard_map/ppermute | solution.py:23
  51.0 13.8 %collective-permute-start.24 = (bf16[64,4096]{1,0:T(8,128)(2,1)S(1)}, bf16[64,4096]{1,0:T(8,128)(2,1)S(1)}, u32[]{:S(2)}, u32[]{:S(2)}) collective-permute-start(bf16[64,4096]{1,0:T(8,128)(2,1)S(1)} %get-tuple-element.68), channel_id=1, source_target_pairs={{0,2},{2,0},{4,6},{6,4},{1,3},{3,1},{5,7},{7,5},{8,10},{10,8},{12,... | collective-permute-start | bytes 1572872 | tf_op jit(solution)/shard_map/ppermute | solution.py:23
  61.6 22.1 %collective-permute-start.16 = (bf16[128,4096]{1,0:T(8,128)(2,1)S(1)}, bf16[128,4096]{1,0:T(8,128)(2,1)S(1)}, u32[]{:S(2)}, u32[]{:S(2)}) collective-permute-start(bf16[128,4096]{1,0:T(8,128)(2,1)S(1)} %add_convert_fusion.3), channel_id=1, source_target_pairs={{0,8},{8,0},{16,24},{24,16},{1,9},{9,1},{17,25},{25,17},{2,10},{10... | collective-permute-start | bytes 3145736 | tf_op jit(solution)/shard_map/ppermute | solution.py:23
  62.0 22.0 %collective-permute-start.18 = (bf16[128,4096]{1,0:T(8,128)(2,1)S(1)}, bf16[128,4096]{1,0:T(8,128)(2,1)S(1)}, u32[]{:S(2)}, u32[]{:S(2)}) collective-permute-start(bf16[128,4096]{1,0:T(8,128)(2,1)S(1)} %add_convert_fusion.2), channel_id=1, source_target_pairs={{0,24},{8,16},{16,8},{24,0},{1,25},{9,17},{17,9},{25,1},{2,26},{10... | collective-permute-start | bytes 3145736 | tf_op jit(solution)/shard_map/ppermute | solution.py:23
  63.8 24.6 %collective-permute-start.23 = (bf16[128,4096]{1,0:T(8,128)(2,1)S(1)}, bf16[128,4096]{1,0:T(8,128)(2,1)S(1)}, u32[]{:S(2)}, u32[]{:S(2)}) collective-permute-start(bf16[128,4096]{1,0:T(8,128)(2,1)S(1)} %add_convert_fusion.1), channel_id=1, source_target_pairs={{0,2},{2,0},{4,6},{6,4},{1,3},{3,1},{5,7},{7,5},{8,10},{10,8},{12,... | collective-permute-start | bytes 3145736 | tf_op jit(solution)/shard_map/ppermute | solution.py:23
  65.0 23.4 %collective-permute-start.25 = (bf16[128,4096]{1,0:T(8,128)(2,1)S(1)}, bf16[128,4096]{1,0:T(8,128)(2,1)S(1)}, u32[]{:S(2)}, u32[]{:S(2)}) collective-permute-start(bf16[128,4096]{1,0:T(8,128)(2,1)S(1)} %add_convert_fusion), channel_id=1, source_target_pairs={{0,6},{2,4},{4,2},{6,0},{1,7},{3,5},{5,3},{7,1},{8,14},{10,12},{12... | collective-permute-start | bytes 3145736 | tf_op jit(solution)/shard_map/ppermute | solution.py:23
  84.5 7.8 %collective-permute-start.19 = (bf16[32,4096]{1,0:T(8,128)(2,1)S(1)}, bf16[32,4096]{1,0:T(8,128)(2,1)S(1)}, u32[]{:S(2)}, u32[]{:S(2)}) collective-permute-start(bf16[32,4096]{1,0:T(8,128)(2,1)S(1)} %get-tuple-element.79), channel_id=1, source_target_pairs={{0,2},{2,0},{4,6},{6,4},{1,3},{3,1},{5,7},{7,5},{8,10},{10,8},{12,... | collective-permute-start | bytes 786440 | tf_op jit(solution)/shard_map/ppermute | solution.py:23
  85.4 12.8 %collective-permute-start.20 = (bf16[32,4096]{1,0:T(8,128)(2,1)S(1)}, bf16[32,4096]{1,0:T(8,128)(2,1)S(1)}, u32[]{:S(2)}, u32[]{:S(2)}) collective-permute-start(bf16[32,4096]{1,0:T(8,128)(2,1)S(1)} %get-tuple-element.81), channel_id=1, source_target_pairs={{0,4},{2,6},{4,0},{6,2},{1,5},{3,7},{5,1},{7,3},{8,12},{10,14},{12... | collective-permute-start | bytes 786440 | tf_op jit(solution)/shard_map/ppermute | solution.py:23
  85.8 12.5 %collective-permute-start.21 = (bf16[32,4096]{1,0:T(8,128)(2,1)S(1)}, bf16[32,4096]{1,0:T(8,128)(2,1)S(1)}, u32[]{:S(2)}, u32[]{:S(2)}) collective-permute-start(bf16[32,4096]{1,0:T(8,128)(2,1)S(1)} %get-tuple-element.80), channel_id=1, source_target_pairs={{0,6},{2,4},{4,2},{6,0},{1,7},{3,5},{5,3},{7,1},{8,14},{10,12},{12... | collective-permute-start | bytes 786440 | tf_op jit(solution)/shard_map/ppermute | solution.py:23
  88.9 9.5 %collective-permute-start.26 = (bf16[32,4096]{1,0:T(8,128)(2,1)S(1)}, bf16[32,4096]{1,0:T(8,128)(2,1)S(1)}, u32[]{:S(2)}, u32[]{:S(2)}) collective-permute-start(bf16[32,4096]{1,0:T(8,128)(2,1)S(1)} %get-tuple-element.76), channel_id=1, source_target_pairs={{0,8},{8,0},{16,24},{24,16},{1,9},{9,1},{17,25},{25,17},{2,10},{10... | collective-permute-start | bytes 786440 | tf_op jit(solution)/shard_map/ppermute | solution.py:23
  89.1 10.1 %collective-permute-start.27 = (bf16[32,4096]{1,0:T(8,128)(2,1)S(1)}, bf16[32,4096]{1,0:T(8,128)(2,1)S(1)}, u32[]{:S(2)}, u32[]{:S(2)}) collective-permute-start(bf16[32,4096]{1,0:T(8,128)(2,1)S(1)} %get-tuple-element.78), channel_id=1, source_target_pairs={{0,16},{8,24},{16,0},{24,8},{1,17},{9,25},{17,1},{25,9},{2,18},{10... | collective-permute-start | bytes 786440 | tf_op jit(solution)/shard_map/ppermute | solution.py:23
  92.3 9.5 %collective-permute-start.28 = (bf16[32,4096]{1,0:T(8,128)(2,1)S(1)}, bf16[32,4096]{1,0:T(8,128)(2,1)S(1)}, u32[]{:S(2)}, u32[]{:S(2)}) collective-permute-start(bf16[32,4096]{1,0:T(8,128)(2,1)S(1)} %get-tuple-element.77), channel_id=1, source_target_pairs={{0,24},{8,16},{16,8},{24,0},{1,25},{9,17},{17,9},{25,1},{2,26},{10... | collective-permute-start | bytes 786440 | tf_op jit(solution)/shard_map/ppermute | solution.py:23
  102.1 17.8 %collective-permute-start.29 = (bf16[16,8192]{1,0:T(8,128)(2,1)S(1)}, bf16[16,8192]{1,0:T(8,128)(2,1)S(1)}, u32[]{:S(2)}, u32[]{:S(2)}) collective-permute-start(bf16[16,8192]{1,0:T(8,128)(2,1)S(1)} %pad_maximum_fusion.4), channel_id=1, source_target_pairs={{0,1},{1,0},{2,3},{3,2},{4,5},{5,4},{6,7},{7,6},{8,9},{9,8},{10,11... | collective-permute-start | bytes 786440 | tf_op jit(solution)/shard_map/ppermute | solution.py:23
  102.2 17.7 %collective-permute-start.30 = (f32[16,4096]{1,0:T(8,128)S(1)}, f32[16,4096]{1,0:T(8,128)S(1)}, u32[]{:S(2)}, u32[]{:S(2)}) collective-permute-start(f32[16,4096]{1,0:T(8,128)S(1)} %pad_maximum_fusion.2), channel_id=1, source_target_pairs={{0,32},{32,64},{64,96},{1,33},{33,65},{65,97},{2,34},{34,66},{66,9... | collective-permute-start | bytes 786440 | tf_op jit(solution)/shard_map/ppermute | solution.py:234
  111.5 8.4 %collective-permute-start.31 = (bf16[16,4096]{1,0:T(8,128)(2,1)S(1)}, bf16[16,4096]{1,0:T(8,128)(2,1)S(1)}, u32[]{:S(2)}, u32[]{:S(2)}) collective-permute-start(bf16[16,4096]{1,0:T(8,128)(2,1)S(1)} %fusion.5), channel_id=1, source_target_pairs={{0,33},{1,32},{32,65},{33,64},{64,97},{65,96},{2,35},{3,34},{34,67... | collective-permute-start | bytes 393224 | tf_op jit(solution)/shard_map/ppermute | solution.py:235
  (10 other events, 52.6 us)

commit v4 on v3

--- a/solution.py
+++ b/solution.py
@@ -54,13 +54,11 @@
     return x_first, y_first
 
 
-def place(first, rest, rows, out_x, out_y):
+def place(first, rest, out, order, rows):
     early = first.shape[0]
-    x_first, y_first = block_orders(rows)
-    for out, order in ((out_x, x_first), (out_y, y_first)):
-        for at, start in enumerate(order):
-            src, start = (first, start) if start < early else (rest, start - early)
-            out[at * rows:(at + 1) * rows, :] = src[start:start + rows, :]
+    for at, start in enumerate(order):
+        src, start = (first, start) if start < early else (rest, start - early)
+        out[at * rows:(at + 1) * rows, :] = src[start:start + rows, :]
 
 
 def feature_units(tokens, enc, bias):
@@ -95,71 +93,79 @@
     hid[...] = hidden_units(tokens, gate, up)
 
 
-def products(feat, hid, down, dec, at, side):
-    width = down.shape[1]
-    half = width // 2
-    f, h = feat[at, :], hid[at, :]
-    cols = slice(side * half, (side + 1) * half)
-    ahead = slice(width + side * half, width + (side + 1) * half)
-    yield slice(0, half), dot(f, dec[:, ahead])
-    yield slice(half, width), dot(f, dec[:, cols]) - dot(h, down[:, cols])
+def forward_part(feat, dec, at):
+    width = dec.shape[1] // 2
+    return dot(feat[at, :], dec[:, width:])
+
+
+def error_part(feat, hid, down, dec, at):
+    width = dec.shape[1] // 2
+    return dot(feat[at, :], dec[:, :width]) - dot(hid[at, :], down[...])
 
 
 def far_kernel(rows, *refs):
     pieces, (feat, hid, enc, bias, gate, up, down, dec), outs = refs[:4], refs[4:12], refs[12:16]
-    feat_x, feat_y, hid_x, hid_y, feat_late, hid_late = refs[16:]
+    feat_x, feat_y, hid_y, feat_late, hid_late = refs[16:]
     tokens = jnp.concatenate([p[...] for p in pieces], axis=0)
+    x_first, y_first = block_orders(rows)
     feat_late[...] = feature_units(tokens, enc, bias)
     hid_late[...] = hidden_units(tokens, gate, up)
-    place(feat, feat_late, rows, feat_x, feat_y)
-    place(hid, hid_late, rows, hid_x, hid_y)
+    place(feat, feat_late, feat_x, x_first, rows)
+    place(feat, feat_late, feat_y, y_first, rows)
+    place(hid, hid_late, hid_y, y_first, rows)
     mid = 4 * rows
-    for side, (f, h) in enumerate(((feat_x, hid_x), (feat_y, hid_y))):
-        for cols, value in products(f, h, down, dec, slice(0, 2 * mid), side):
-            outs[2 * side][:, cols] = value[:mid].astype(BF)
-            outs[2 * side + 1][:, cols] = value[mid:].astype(BF)
-
-
-def near_kernel(rows, feat_x, feat_y, hid_x, hid_y, down, dec, *outs):
+    far = slice(0, 2 * mid)
+    for side, value in enumerate((forward_part(feat_x, dec, far), error_part(feat_y, hid_y, down, dec, far))):
+        outs[2 * side][...] = value[:mid].astype(BF)
+        outs[2 * side + 1][...] = value[mid:].astype(BF)
+
+
+def near_kernel(rows, feat_x, feat_y, hid_y, down, dec, *outs):
     block = 8 * rows
-    for side, (f, h) in enumerate(((feat_x, hid_x), (feat_y, hid_y))):
-        for cols, value in products(f, h, down, dec, slice(block, 4 * block), side):
-            for at in range(3):
-                outs[3 * side + at][:, cols] = value[at * block:(at + 1) * block]
+    near = slice(block, 4 * block)
+    for side, value in enumerate((forward_part(feat_x, dec, near), error_part(feat_y, hid_y, down, dec, near))):
+        for at in range(3):
+            outs[3 * side + at][...] = value[at * block:(at + 1) * block]
 
 
 def hop_far(parts, axis):
     return swap(parts[0], axis, 1), swap(parts[1], axis, 3)
 
 
-def hop_near(parts, arrived, axis):
+def near_rows(parts, arrived):
     upper, lower = (v.astype(F32) for v in arrived)
     zeros = jnp.zeros_like(upper)
     one = parts[0] + jnp.concatenate([zeros, lower], axis=0)
     three = parts[1] + jnp.concatenate([upper, zeros], axis=0)
-    return swap(one.astype(BF), axis, 1), swap(three.astype(BF), axis, 3)
-
-
-def total_of(own, arrived):
-    for value in arrived:
-        own = own + value.astype(F32)
-    return own
-
-
-def split_rows(array, count):
-    rows = array.shape[0] // count
-    return [array[i * rows:(i + 1) * rows] for i in range(count)]
-
-
-def direct(total, axis):
-    parts = split_rows(total, 4)
-    return parts[0], [swap(parts[r].astype(BF), axis, r) for r in (1, 2, 3)]
+    return one.astype(BF), three.astype(BF)
+
+
+def after(values, others):
+    return tie(*values, *others)[:len(values)]
+
+
+def hop_near(rows, axis):
+    return swap(rows[0], axis, 1), swap(rows[1], axis, 3)
+
+
+def sum_kernel(own, near, behind, rest, *sends):
+    total = own[...] + near[...].astype(F32) + behind[...].astype(F32)
+    count = rest.shape[0]
+    rest[...] = total[:count]
+    for at, out in enumerate(sends, 1):
+        out[...] = total[at * count:(at + 1) * count].astype(BF)
+
+
+def last_kernel(rest, one, two, three, own, other):
+    total = rest[...] + one[...].astype(F32) + two[...].astype(F32) + three[...].astype(F32)
+    count = own.shape[0]
+    own[...] = total[:count]
+    other[...] = total[count:].astype(BF)
 
 
 def body(resid, norm_gain, w_gate, w_up, w_down, w_enc, b_enc, w_dec, carry_in):
     rows = resid.shape[1]
     width = resid.shape[2]
-    half = width // 2
     block = 8 * rows
     def shape(count, cols, dtype=BF):
         return jax.ShapeDtypeStruct((count, cols), dtype)
@@ -203,41 +209,48 @@
     feat, hid = call(
         first_kernel, "first_units", [VMEM] * 10, [shape(early, features), shape(early, hidden)], [], 12,
     )(*own_early, *oth_early, enc, b_enc, gate, up)
-    *far_parts, feat_x, feat_y, hid_x, hid_y = call(
+    *far_parts, feat_x, feat_y, hid_y = call(
         functools.partial(far_kernel, rows), "far_parts", [VMEM] * 12,
-        [shape(block // 2, width)] * 4 + [shape(4 * block, features)] * 2 + [shape(4 * block, hidden)] * 2,
+        [shape(block // 2, width)] * 4 + [shape(4 * block, features)] * 2 + [shape(4 * block, hidden)],
         [pltpu.VMEM((block, features), BF), pltpu.VMEM((block, hidden), BF)], 12,
     )(*own_late, *oth_late, feat, hid, enc, b_enc, gate, up, down, dec)
-    far_a, far_b = hop_far(far_parts[:2], FX), hop_far(far_parts[2:], FY)
+    far_f, far_e = hop_far(far_parts[:2], FX), hop_far(far_parts[2:], FY)
     near_parts = call(
-        functools.partial(near_kernel, rows), "near_parts", [VMEM] * 6,
+        functools.partial(near_kernel, rows), "near_parts", [VMEM] * 5,
         [shape(block, width, F32)] * 6, [], 12,
-    )(feat_x, feat_y, hid_x, hid_y, down, dec)
-    near_a = hop_near(near_parts[:2], far_a, FX)
-    near_b = hop_near(near_parts[3:5], far_b, FY)
-    da = direct(total_of(near_parts[2], near_a), FY)
-    db = direct(total_of(near_parts[5], near_b), FX)
-    low_a, low_b = total_of(*da), total_of(*db)
-
-    def halves(cols):
-        return split_rows(jnp.concatenate([low_a[:, cols], low_b[:, cols]], axis=1), 2)
-
-    fwd_own, fwd_oth = halves(slice(0, half))
-    err_own, err_oth = halves(slice(half, width))
-    fwd_oth = fwd_oth.astype(BF)
-    count = lax.axis_size("grp")
+    )(feat_x, feat_y, hid_y, down, dec)
+    rows_f = near_rows(near_parts[:2], far_f)
+    near_f = hop_near(rows_f, FX)
+    near_e = hop_near(near_rows(near_parts[3:5], after(far_e, rows_f)), FY)
+    quarter = 2 * rows
+
+    def second_stage(own, arrived, axis):
+        rest, *sends = call(
+            sum_kernel, "first_sums", [VMEM] * 3,
+            [shape(quarter, width, F32)] + [shape(quarter, width)] * 3, [], 8,
+        )(own, *arrived)
+        return rest, sends, [swap(part, axis, r) for r, part in enumerate(sends, 1)]
+
+    def last_sums(rest, arrived):
+        return call(
+            last_kernel, "second_sums", [VMEM] * 4, [shape(rows, width, F32), shape(rows, width)], [], 4,
+        )(rest, *arrived)
+
+    rest_f, sends_f, arrived_f = second_stage(near_parts[2], near_f, FY)
+    rest_e, sends_e, arrived_e = second_stage(near_parts[5], after(near_e, sends_f), FX)
+    arrived_f = after(arrived_f, sends_e)
+    fwd_own, fwd_oth = last_sums(rest_f, arrived_f)
+    count, planes = lax.axis_size("grp"), lax.axis_size(FZ)
     onward = [(i, i + 1) for i in range(count - 1)]
-    planes = lax.axis_size(FZ)
     crossed = [(i * planes + z, (i + 1) * planes + (z ^ 1)) for i in range(count - 1) for z in range(planes)]
-    arrived, passed, passed_oth = tie(
-        swap(jnp.concatenate([fwd_oth, err_oth.astype(BF)], axis=1), FZ, 1),
-        lax.ppermute(fwd_own, "grp", onward),
-        lax.ppermute(fwd_oth, ("grp", FZ), crossed),
-    )
-    arrived = arrived.astype(F32)
+    passed_oth = lax.ppermute(fwd_oth, ("grp", FZ), crossed)
+    arrived = swap(fwd_oth, FZ, 1)
+    passed = lax.ppermute(fwd_own, "grp", onward)
+    err_own, err_oth = last_sums(rest_e, arrived_e)
+    err_arrived = swap(err_oth, FZ, 1)
     incoming = jnp.where(lax.axis_index("grp") == 0, carry_in, passed + passed_oth.astype(F32))
-    to_next = fwd_own + arrived[:, :width]
-    errors = err_own + arrived[:, width:] + incoming
+    to_next = fwd_own + arrived.astype(F32)
+    errors = err_own + err_arrived.astype(F32) + incoming
     return (errors[None], to_next[None])
 
 

time: 121 us -> 116 us (0.959)
  waiting for transfers between devices: 42.5 us -> 39.8 us
  starting transfers between devices: 50.2 us -> 47.9 us
    ppermute x2, waiting for transfers between devices: 4.39 us -> 0.1 us  [the longest x1 0.1 us: body(): passed = lax.ppermute(fwd_own, 'grp', onward)]
    ppermute x30 -> x31, starting transfers between devices: 36.9 us -> 35.2 us  [swap(): return lax.ppermute(value, axis, [(i, i ^ distance) for i in range(count)])]
    ppermute x30 -> x31, waiting for transfers between devices: 38.2 us -> 39.7 us  [swap(): return lax.ppermute(value, axis, [(i, i ^ distance) for i in range(count)])]
    pallas_call x1 -> x5, Pallas kernels: 5.14 us -> 6 us  [the longest x1 5.15 us: body(): call(functools.partial(near_kernel, rows), 'near_parts', [VMEM] * 5, [sha...]
  transfers between devices with their start and end apart: 32 -> 33, of which waited for: 12 -> 13; matrix products, arithmetic and copies ran while one was open for 2% -> 1% of each run, Pallas kernels for 9% -> 10%
where the time goes in v4:
time: 116 us
  starting transfers between devices  47.9 us (41%)
  waiting for transfers between devices  39.8 us (34%)
  Pallas kernels  16.8 us (14%)
  local copies, waits for them, and re-layouts  8.02 us (7%)
  other arithmetic  2.32 us (2%)
    ppermute x31, waiting for transfers between devices, swap(): return lax.ppermute(value, axis, [(i, i ^ distance) for i in range(count)])  39.7 us
    ppermute x31, starting transfers between devices, swap(): return lax.ppermute(value, axis, [(i, i ^ distance) for i in range(count)])  35.2 us
    ppermute x1, starting transfers between devices, body(): passed_oth = lax.ppermute(fwd_oth, ('grp', FZ), crossed)  10 us
    unnamed x20, local copies, waits for them, and re-layouts  7.95 us
    pallas_call x1, Pallas kernels, body(): call(functools.partial(near_kernel, rows), 'near_parts', [VMEM] * 5, [sha...  5.15 us
    pallas_call x1, Pallas kernels, body(): call(first_kernel, 'first_units', [VMEM] * 10, [shape(early, features), s...  5.07 us
    pallas_call x1, Pallas kernels, body(): call(functools.partial(far_kernel, rows), 'far_parts', [VMEM] * 12, [shap...  4.62 us
    ppermute x1, starting transfers between devices, body(): passed = lax.ppermute(fwd_own, 'grp', onward)  2.75 us
  transfers between devices with their start and end apart: 33, of which 13 were waited for; matrix products, arithmetic and copies ran while one was open for 1% of the time, Pallas kernels for 10%

profile of v4, /device:TPU:1, one launch (start us, length us, event | category | flops | bytes accessed | tf_op | source)
XLA Modules:
  0.0 115.8 jit_solution(1338659022678568587)
XLA Ops:
  0.6 4.5 %collective-permute-start.3 = (bf16[16,4096]{1,0:T(8,128)(2,1)}, bf16[16,4096]{1,0:T(8,128)(2,1)S(1)}, u32[]{:S(2)}, u32[]{:S(2)}) collective-permute-start(bf16[16,4096]{1,0:T(8,128)(2,1)} %bitcast.23), channel_id=1, source_target_pairs={{0,1},{1,0},{2,3},{3,2},{4,5},{5,4},{6,7},{7,6},{8,9},{9,8},{10,11... | collective-permute-start | bytes 393224 | tf_op jit(solution)/shard_map/ppermute | solution.py:23
  6.9 1.3 %collective-permute-start = (bf16[16,4096]{1,0:T(8,128)(2,1)S(1)}, bf16[16,4096]{1,0:T(8,128)(2,1)S(1)}, u32[]{:S(2)}, u32[]{:S(2)}) collective-permute-start(bf16[16,4096]{1,0:T(8,128)(2,1)S(1)} %norm.2), channel_id=1, source_target_pairs={{0,8},{8,0},{16,24},{24,16},{1,9},{9,1},{17,25},{25,17},{2,10},{10... | collective-permute-start | bytes 393224 | tf_op jit(solution)/shard_map/ppermute | solution.py:23
  8.2 2.5 %collective-permute-start.1 = (bf16[16,4096]{1,0:T(8,128)(2,1)S(1)}, bf16[16,4096]{1,0:T(8,128)(2,1)S(1)}, u32[]{:S(2)}, u32[]{:S(2)}) collective-permute-start(bf16[16,4096]{1,0:T(8,128)(2,1)S(1)} %norm.2), channel_id=1, source_target_pairs={{0,16},{8,24},{16,0},{24,8},{1,17},{9,25},{17,1},{25,9},{2,18},{10... | collective-permute-start | bytes 393224 | tf_op jit(solution)/shard_map/ppermute | solution.py:23
  11.0 2.8 %collective-permute-start.10 = (bf16[16,4096]{1,0:T(8,128)(2,1)S(1)}, bf16[16,4096]{1,0:T(8,128)(2,1)S(1)}, u32[]{:S(2)}, u32[]{:S(2)}) collective-permute-start(bf16[16,4096]{1,0:T(8,128)(2,1)S(1)} %norm.3), channel_id=1, source_target_pairs={{0,6},{2,4},{4,2},{6,0},{1,7},{3,5},{5,3},{7,1},{8,14},{10,12},{12... | collective-permute-start | bytes 393224 | tf_op jit(solution)/shard_map/ppermute | solution.py:23
  13.9 1.3 %collective-permute-start.9 = (bf16[16,4096]{1,0:T(8,128)(2,1)S(1)}, bf16[16,4096]{1,0:T(8,128)(2,1)S(1)}, u32[]{:S(2)}, u32[]{:S(2)}) collective-permute-start(bf16[16,4096]{1,0:T(8,128)(2,1)S(1)} %norm.3), channel_id=1, source_target_pairs={{0,4},{2,6},{4,0},{6,2},{1,5},{3,7},{5,1},{7,3},{8,12},{10,14},{12... | collective-permute-start | bytes 393224 | tf_op jit(solution)/shard_map/ppermute | solution.py:23
  15.8 2.8 %collective-permute-done.2 = bf16[16,4096]{1,0:T(8,128)(2,1)S(1)} collective-permute-done((bf16[16,4096]{1,0:T(8,128)(2,1)S(1)}, bf16[16,4096]{1,0:T(8,128)(2,1)S(1)}, u32[]{:S(2)}, u32[]{:S(2)}) %collective-permute-start.2) | collective-permute-done | bytes 131104 | tf_op jit(solution)/shard_map/ppermute | solution.py:23
  18.6 1.4 %collective-permute-start.4 = (bf16[64,4096]{1,0:T(8,128)(2,1)S(1)}, bf16[64,4096]{1,0:T(8,128)(2,1)S(1)}, u32[]{:S(2)}, u32[]{:S(2)}) collective-permute-start(bf16[64,4096]{1,0:T(8,128)(2,1)S(1)} %pad_maximum_fusion._.refs_0_), channel_id=1, source_target_pairs={{0,2},{2,0},{4,6},{6,4},{1,3},{3,1},{5,7},{7,5},{8,10},{10,8},{12,... | collective-permute-start | bytes 1572872 | tf_op jit(solution)/shard_map/ppermute | solution.py:23
  20.0 1.9 %collective-permute-start.5 = (bf16[64,4096]{1,0:T(8,128)(2,1)S(1)}, bf16[64,4096]{1,0:T(8,128)(2,1)S(1)}, u32[]{:S(2)}, u32[]{:S(2)}) collective-permute-start(bf16[64,4096]{1,0:T(8,128)(2,1)S(1)} %pad_maximum_fusion._.refs_0_), channel_id=1, source_target_pairs={{0,6},{2,4},{4,2},{6,0},{1,7},{3,5},{5,3},{7,1},{8,14},{10,12},{12... | collective-permute-start | bytes 1572872 | tf_op jit(solution)/shard_map/ppermute | solution.py:23
  22.1 1.0 collective-permute-start.12
  23.1 2.2 %copy-done.1 = bf16[1,4096,512]{2,1,0:T(8,128)(2,1)S(1)} copy-done((bf16[1,4096,512]{2,1,0:T(8,128)(2,1)S(1)}, bf16[1,4096,512]{2,1,0:T(8,128)(2,1)}, u32[]{:S(2)}) %copy-start.1) | copy-done | bytes 4194328
  25.3 2.0 %copy-done.2 = bf16[1,4096,448]{1,2,0:T(8,128)(2,1)S(1)} copy-done((bf16[1,4096,448]{1,2,0:T(8,128)(2,1)S(1)}, bf16[1,4096,448]{1,2,0:T(8,128)(2,1)}, u32[]{:S(2)}) %copy-start.2) | copy-done | bytes 3670040
  27.3 2.0 %copy-done.3 = bf16[1,4096,448]{1,2,0:T(8,128)(2,1)S(1)} copy-done((bf16[1,4096,448]{1,2,0:T(8,128)(2,1)S(1)}, bf16[1,4096,448]{1,2,0:T(8,128)(2,1)}, u32[]{:S(2)}) %copy-start.3) | copy-done | bytes 3670040
  30.2 2.2 %collective-permute-done.4.refs_1_ = bf16[64,4096]{1,0:T(8,128)(2,1)S(1)} collective-permute-done((bf16[64,4096]{1,0:T(8,128)(2,1)S(1)}, bf16[64,4096]{1,0:T(8,128)(2,1)S(1)}, u32[]{:S(2)}, u32[]{:S(2)}) %collective-permute-start.4) | collective-permute-done | bytes 524320 | tf_op jit(solution)/shard_map/ppermute | solution.py:23
  33.0 2.0 %collective-permute-start.6 = (bf16[32,4096]{1,0:T(8,128)(2,1)S(1)}, bf16[32,4096]{1,0:T(8,128)(2,1)S(1)}, u32[]{:S(2)}, u32[]{:S(2)}) collective-permute-start(bf16[32,4096]{1,0:T(8,128)(2,1)S(1)} %slice.12), channel_id=1, source_target_pairs={{0,6},{2,4},{4,2},{6,0},{1,7},{3,5},{5,3},{7,1},{8,14},{10,12},{12... | collective-permute-start | bytes 786440 | tf_op jit(solution)/shard_map/ppermute | solution.py:23
  35.2 3.6 %collective-permute-start.13 = (bf16[32,4096]{1,0:T(8,128)(2,1)S(1)}, bf16[32,4096]{1,0:T(8,128)(2,1)S(1)}, u32[]{:S(2)}, u32[]{:S(2)}) collective-permute-start(bf16[32,4096]{1,0:T(8,128)(2,1)S(1)} %slice.14), channel_id=1, source_target_pairs={{0,24},{8,16},{16,8},{24,0},{1,25},{9,17},{17,9},{25,1},{2,26},{10... | collective-permute-start | bytes 786440 | tf_op jit(solution)/shard_map/ppermute | solution.py:23
  38.9 5.1 %first_units.1 = (bf16[384,512]{1,0:T(8,128)(2,1)S(1)}, bf16[384,448]{1,0:T(8,128)(2,1)S(1)}) custom-call(bf16[64,4096]{1,0:T(8,128)(2,1)S(1)} %pad_maximum_fusion._.refs_0_, bf16[64,4096]{1,0:T(8,128)(2,1)S(1)} %collective-permute-done.4.refs_1_, bf16[64,4096]{1,0:T(8,128)(2,1)S(1)} %collective-permute-done.5.refs_2_, ...), custom_call_target="tpu_custom_call" | custom-call | flops 1 | bytes 1 | tf_op jit(solution)/shard_map/first_units/pallas_call | solution.py:209
  44.8 4.6 %far_parts.1 = (bf16[64,4096]{1,0:T(8,128)(2,1)S(1)}, bf16[64,4096]{1,0:T(8,128)(2,1)S(1)}, bf16[64,4096]{1,0:T(8,128)(2,1)S(1)}, bf16[64,4096]{1,0:T(8,128)(2,1...) custom-call(bf16[32,4096]{1,0:T(8,128)(2,1)S(1)} %collective-permute-done.6.refs_0_,, ...), custom_call_target="tpu_custom_call" | custom-call | flops 1 | bytes 1 | tf_op jit(solution)/shard_map/far_parts/pallas_call | solution.py:212
  50.2 1.0 collective-permute-start.17
  51.2 1.2 %collective-permute-start.15 = (bf16[64,4096]{1,0:T(8,128)(2,1)S(1)}, bf16[64,4096]{1,0:T(8,128)(2,1)S(1)}, u32[]{:S(2)}, u32[]{:S(2)}) collective-permute-start(bf16[64,4096]{1,0:T(8,128)(2,1)S(1)} %get-tuple-element.75), channel_id=1, source_target_pairs={{0,2},{2,0},{4,6},{6,4},{1,3},{3,1},{5,7},{7,5},{8,10},{10,8},{12,... | collective-permute-start | bytes 1572872 | tf_op jit(solution)/shard_map/ppermute | solution.py:23
  52.6 5.1 %near_parts.1 = (f32[128,4096]{1,0:T(8,128)S(1)}, f32[128,4096]{1,0:T(8,128)S(1)}, f32[128,4096]{1,0:T(8,128)S(1)}, f32[128,4096]{1,0:T(8,128)S(1)}, f32[128,4096]{1,0:T(8,128)S(1)}, /*index=5*/f32[128,4096]{1,0:T(8,128)S(1)}) custom-call(bf16[512,512]{1,0:T(8,128)(2,1)S(1)} %get-tuple-element.70.feat_x, bf16[512,512]{1,0:T(8,128)(2,1)S(1)} %get-tuple-element.71.feat_y, ...), custom_call_target="tpu_custom_call" | custom-call | flops 1 | bytes 1 | tf_op jit(solution)/shard_map/near_parts/pallas_call | solution.py:218
  57.8 2.3 %collective-permute-done.18 = bf16[64,4096]{1,0:T(8,128)(2,1)S(1)} collective-permute-done((bf16[64,4096]{1,0:T(8,128)(2,1)S(1)}, bf16[64,4096]{1,0:T(8,128)(2,1)S(1)}, u32[]{:S(2)}, u32[]{:S(2)}) %collective-permute-start.18) | collective-permute-done | bytes 524320 | tf_op jit(solution)/shard_map/ppermute | solution.py:23
  60.3 1.7 %collective-permute-start.22 = (bf16[128,4096]{1,0:T(8,128)(2,1)S(1)}, bf16[128,4096]{1,0:T(8,128)(2,1)S(1)}, u32[]{:S(2)}, u32[]{:S(2)}) collective-permute-start(bf16[128,4096]{1,0:T(8,128)(2,1)S(1)} %add_convert_fusion.2), channel_id=1, source_target_pairs={{0,24},{8,16},{16,8},{24,0},{1,25},{9,17},{17,9},{25,1},{2,26},{10... | collective-permute-start | bytes 3145736 | tf_op jit(solution)/shard_map/ppermute | solution.py:23
  64.4 20.2 %collective-permute-done.22.behind = bf16[128,4096]{1,0:T(8,128)(2,1)S(1)} collective-permute-done((bf16[128,4096]{1,0:T(8,128)(2,1)S(1)}, bf16[128,4096]{1,0:T(8,128)(2,1)S(1)}, u32[]{:S(2)}, u32[]{:S(2)}) %collective-permute-start.22) | collective-permute-done | bytes 1048608 | tf_op jit(solution)/shard_map/ppermute | solution.py:23
  84.9 1.8 %collective-permute-start.27 = (bf16[32,4096]{1,0:T(8,128)(2,1)S(1)}, bf16[32,4096]{1,0:T(8,128)(2,1)S(1)}, u32[]{:S(2)}, u32[]{:S(2)}) collective-permute-start(bf16[32,4096]{1,0:T(8,128)(2,1)S(1)} %get-tuple-element.85), channel_id=1, source_target_pairs={{0,2},{2,0},{4,6},{6,4},{1,3},{3,1},{5,7},{7,5},{8,10},{10,8},{12,... | collective-permute-start | bytes 786440 | tf_op jit(solution)/shard_map/ppermute | solution.py:23
  86.7 2.5 %collective-permute-start.29 = (bf16[32,4096]{1,0:T(8,128)(2,1)S(1)}, bf16[32,4096]{1,0:T(8,128)(2,1)S(1)}, u32[]{:S(2)}, u32[]{:S(2)}) collective-permute-start(bf16[32,4096]{1,0:T(8,128)(2,1)S(1)} %get-tuple-element.87), channel_id=1, source_target_pairs={{0,6},{2,4},{4,2},{6,0},{1,7},{3,5},{5,3},{7,1},{8,14},{10,12},{12... | collective-permute-start | bytes 786440 | tf_op jit(solution)/shard_map/ppermute | solution.py:23
  89.7 1.4 %collective-permute-start.24 = (bf16[32,4096]{1,0:T(8,128)(2,1)S(1)}, bf16[32,4096]{1,0:T(8,128)(2,1)S(1)}, u32[]{:S(2)}, u32[]{:S(2)}) collective-permute-start(bf16[32,4096]{1,0:T(8,128)(2,1)S(1)} %get-tuple-element.92), channel_id=1, source_target_pairs={{0,16},{8,24},{16,0},{24,8},{1,17},{9,25},{17,1},{25,9},{2,18},{10... | collective-permute-start | bytes 786440 | tf_op jit(solution)/shard_map/ppermute | solution.py:23
  91.0 1.8 %collective-permute-done.27.one = bf16[32,4096]{1,0:T(8,128)(2,1)S(1)} collective-permute-done((bf16[32,4096]{1,0:T(8,128)(2,1)S(1)}, bf16[32,4096]{1,0:T(8,128)(2,1)S(1)}, u32[]{:S(2)}, u32[]{:S(2)}) %collective-permute-start.27) | collective-permute-done | bytes 262176 | tf_op jit(solution)/shard_map/ppermute | solution.py:23
  92.8 1.1 collective-permute-start.25
  93.9 4.6 %collective-permute-done.28.two = bf16[32,4096]{1,0:T(8,128)(2,1)S(1)} collective-permute-done((bf16[32,4096]{1,0:T(8,128)(2,1)S(1)}, bf16[32,4096]{1,0:T(8,128)(2,1)S(1)}, u32[]{:S(2)}, u32[]{:S(2)}) %collective-permute-start.28) | collective-permute-done | bytes 262176 | tf_op jit(solution)/shard_map/ppermute | solution.py:23
  98.7 10.0 %collective-permute-start.31 = (bf16[16,4096]{1,0:T(8,128)(2,1)S(1)}, bf16[16,4096]{1,0:T(8,128)(2,1)S(1)}, u32[]{:S(2)}, u32[]{:S(2)}) collective-permute-start(bf16[16,4096]{1,0:T(8,128)(2,1)S(1)} %get-tuple-element.101), channel_id=1, source_target_pairs={{0,33},{1,32},{32,65},{33,64},{64,97},{65,96},{2,35},{3,34},{34,67... | collective-permute-start | bytes 393224 | tf_op jit(solution)/shard_map/ppermute | solution.py:246
  109.0 2.8 %collective-permute-start.30 = (f32[16,4096]{1,0:T(8,128)S(1)}, f32[16,4096]{1,0:T(8,128)S(1)}, u32[]{:S(2)}, u32[]{:S(2)}) collective-permute-start(f32[16,4096]{1,0:T(8,128)S(1)} %get-tuple-element.100), channel_id=1, source_target_pairs={{0,32},{32,64},{64,96},{1,33},{33,65},{65,97},{2,34},{34,66},{66,9... | collective-permute-start | bytes 786440 | tf_op jit(solution)/shard_map/ppermute | solution.py:248
  112.5 2.5 %collective-permute-done.26 = bf16[16,4096]{1,0:T(8,128)(2,1)S(1)} collective-permute-done((bf16[16,4096]{1,0:T(8,128)(2,1)S(1)}, bf16[16,4096]{1,0:T(8,128)(2,1)S(1)}, u32[]{:S(2)}, u32[]{:S(2)}) %collective-permute-start.26) | collective-permute-done | bytes 131104 | tf_op jit(solution)/shard_map/ppermute | solution.py:23
  (77 shorter events, 11.8 us)
Async XLA Ops:
  0.6 10.3 %collective-permute-start.3 = (bf16[16,4096]{1,0:T(8,128)(2,1)}, bf16[16,4096]{1,0:T(8,128)(2,1)S(1)}, u32[]{:S(2)}, u32[]{:S(2)}) collective-permute-start(bf16[16,4096]{1,0:T(8,128)(2,1)} %bitcast.23), channel_id=1, source_target_pairs={{0,1},{1,0},{2,3},{3,2},{4,5},{5,4},{6,7},{7,6},{8,9},{9,8},{10,11... | collective-permute-start | bytes 393224 | tf_op jit(solution)/shard_map/ppermute | solution.py:23
  6.9 6.9 %collective-permute-start = (bf16[16,4096]{1,0:T(8,128)(2,1)S(1)}, bf16[16,4096]{1,0:T(8,128)(2,1)S(1)}, u32[]{:S(2)}, u32[]{:S(2)}) collective-permute-start(bf16[16,4096]{1,0:T(8,128)(2,1)S(1)} %norm.2), channel_id=1, source_target_pairs={{0,8},{8,0},{16,24},{24,16},{1,9},{9,1},{17,25},{25,17},{2,10},{10... | collective-permute-start | bytes 393224 | tf_op jit(solution)/shard_map/ppermute | solution.py:23
  8.2 7.5 %collective-permute-start.1 = (bf16[16,4096]{1,0:T(8,128)(2,1)S(1)}, bf16[16,4096]{1,0:T(8,128)(2,1)S(1)}, u32[]{:S(2)}, u32[]{:S(2)}) collective-permute-start(bf16[16,4096]{1,0:T(8,128)(2,1)S(1)} %norm.2), channel_id=1, source_target_pairs={{0,16},{8,24},{16,0},{24,8},{1,17},{9,25},{17,1},{25,9},{2,18},{10... | collective-permute-start | bytes 393224 | tf_op jit(solution)/shard_map/ppermute | solution.py:23
  10.7 7.9 %collective-permute-start.2 = (bf16[16,4096]{1,0:T(8,128)(2,1)S(1)}, bf16[16,4096]{1,0:T(8,128)(2,1)S(1)}, u32[]{:S(2)}, u32[]{:S(2)}) collective-permute-start(bf16[16,4096]{1,0:T(8,128)(2,1)S(1)} %norm.2), channel_id=1, source_target_pairs={{0,24},{8,16},{16,8},{24,0},{1,25},{9,17},{17,9},{25,1},{2,26},{10... | collective-permute-start | bytes 393224 | tf_op jit(solution)/shard_map/ppermute | solution.py:23
  11.0 10.9 %collective-permute-start.10 = (bf16[16,4096]{1,0:T(8,128)(2,1)S(1)}, bf16[16,4096]{1,0:T(8,128)(2,1)S(1)}, u32[]{:S(2)}, u32[]{:S(2)}) collective-permute-start(bf16[16,4096]{1,0:T(8,128)(2,1)S(1)} %norm.3), channel_id=1, source_target_pairs={{0,6},{2,4},{4,2},{6,0},{1,7},{3,5},{5,3},{7,1},{8,14},{10,12},{12... | collective-permute-start | bytes 393224 | tf_op jit(solution)/shard_map/ppermute | solution.py:23
  13.9 8.1 %collective-permute-start.8 = (bf16[16,4096]{1,0:T(8,128)(2,1)S(1)}, bf16[16,4096]{1,0:T(8,128)(2,1)S(1)}, u32[]{:S(2)}, u32[]{:S(2)}) collective-permute-start(bf16[16,4096]{1,0:T(8,128)(2,1)S(1)} %norm.3), channel_id=1, source_target_pairs={{0,2},{2,0},{4,6},{6,4},{1,3},{3,1},{5,7},{7,5},{8,10},{10,8},{12,... | collective-permute-start | bytes 393224 | tf_op jit(solution)/shard_map/ppermute | solution.py:23
  13.9 8.1 %collective-permute-start.9 = (bf16[16,4096]{1,0:T(8,128)(2,1)S(1)}, bf16[16,4096]{1,0:T(8,128)(2,1)S(1)}, u32[]{:S(2)}, u32[]{:S(2)}) collective-permute-start(bf16[16,4096]{1,0:T(8,128)(2,1)S(1)} %norm.3), channel_id=1, source_target_pairs={{0,4},{2,6},{4,0},{6,2},{1,5},{3,7},{5,1},{7,3},{8,12},{10,14},{12... | collective-permute-start | bytes 393224 | tf_op jit(solution)/shard_map/ppermute | solution.py:23
  18.6 13.8 %collective-permute-start.4 = (bf16[64,4096]{1,0:T(8,128)(2,1)S(1)}, bf16[64,4096]{1,0:T(8,128)(2,1)S(1)}, u32[]{:S(2)}, u32[]{:S(2)}) collective-permute-start(bf16[64,4096]{1,0:T(8,128)(2,1)S(1)} %pad_maximum_fusion._.refs_0_), channel_id=1, source_target_pairs={{0,2},{2,0},{4,6},{6,4},{1,3},{3,1},{5,7},{7,5},{8,10},{10,8},{12,... | collective-permute-start | bytes 1572872 | tf_op jit(solution)/shard_map/ppermute | solution.py:23
  20.0 13.0 %collective-permute-start.5 = (bf16[64,4096]{1,0:T(8,128)(2,1)S(1)}, bf16[64,4096]{1,0:T(8,128)(2,1)S(1)}, u32[]{:S(2)}, u32[]{:S(2)}) collective-permute-start(bf16[64,4096]{1,0:T(8,128)(2,1)S(1)} %pad_maximum_fusion._.refs_0_), channel_id=1, source_target_pairs={{0,6},{2,4},{4,2},{6,0},{1,7},{3,5},{5,3},{7,1},{8,14},{10,12},{12... | collective-permute-start | bytes 1572872 | tf_op jit(solution)/shard_map/ppermute | solution.py:23
  22.0 13.1 %collective-permute-start.11 = (bf16[64,4096]{1,0:T(8,128)(2,1)S(1)}, bf16[64,4096]{1,0:T(8,128)(2,1)S(1)}, u32[]{:S(2)}, u32[]{:S(2)}) collective-permute-start(bf16[64,4096]{1,0:T(8,128)(2,1)S(1)} %pad_maximum_fusion.1.refs_3_), channel_id=1, source_target_pairs={{0,8},{8,0},{16,24},{24,16},{1,9},{9,1},{17,25},{25,17},{2,10},{10... | collective-permute-start | bytes 1572872 | tf_op jit(solution)/shard_map/ppermute | solution.py:23
  22.1 13.1 %collective-permute-start.12 = (bf16[64,4096]{1,0:T(8,128)(2,1)S(1)}, bf16[64,4096]{1,0:T(8,128)(2,1)S(1)}, u32[]{:S(2)}, u32[]{:S(2)}) collective-permute-start(bf16[64,4096]{1,0:T(8,128)(2,1)S(1)} %pad_maximum_fusion.1.refs_3_), channel_id=1, source_target_pairs={{0,24},{8,16},{16,8},{24,0},{1,25},{9,17},{17,9},{25,1},{2,26},{10... | collective-permute-start | bytes 1572872 | tf_op jit(solution)/shard_map/ppermute | solution.py:23
  33.0 11.0 %collective-permute-start.6 = (bf16[32,4096]{1,0:T(8,128)(2,1)S(1)}, bf16[32,4096]{1,0:T(8,128)(2,1)S(1)}, u32[]{:S(2)}, u32[]{:S(2)}) collective-permute-start(bf16[32,4096]{1,0:T(8,128)(2,1)S(1)} %slice.12), channel_id=1, source_target_pairs={{0,6},{2,4},{4,2},{6,0},{1,7},{3,5},{5,3},{7,1},{8,14},{10,12},{12... | collective-permute-start | bytes 786440 | tf_op jit(solution)/shard_map/ppermute | solution.py:23
  35.0 9.0 %collective-permute-start.7 = (bf16[32,4096]{1,0:T(8,128)(2,1)S(1)}, bf16[32,4096]{1,0:T(8,128)(2,1)S(1)}, u32[]{:S(2)}, u32[]{:S(2)}) collective-permute-start(bf16[32,4096]{1,0:T(8,128)(2,1)S(1)} %slice.13), channel_id=1, source_target_pairs={{0,2},{2,0},{4,6},{6,4},{1,3},{3,1},{5,7},{7,5},{8,10},{10,8},{12,... | collective-permute-start | bytes 786440 | tf_op jit(solution)/shard_map/ppermute | solution.py:23
  35.2 8.9 %collective-permute-start.13 = (bf16[32,4096]{1,0:T(8,128)(2,1)S(1)}, bf16[32,4096]{1,0:T(8,128)(2,1)S(1)}, u32[]{:S(2)}, u32[]{:S(2)}) collective-permute-start(bf16[32,4096]{1,0:T(8,128)(2,1)S(1)} %slice.14), channel_id=1, source_target_pairs={{0,24},{8,16},{16,8},{24,0},{1,25},{9,17},{17,9},{25,1},{2,26},{10... | collective-permute-start | bytes 786440 | tf_op jit(solution)/shard_map/ppermute | solution.py:23
  49.4 10.7 %collective-permute-start.18 = (bf16[64,4096]{1,0:T(8,128)(2,1)S(1)}, bf16[64,4096]{1,0:T(8,128)(2,1)S(1)}, u32[]{:S(2)}, u32[]{:S(2)}) collective-permute-start(bf16[64,4096]{1,0:T(8,128)(2,1)S(1)} %get-tuple-element.80), channel_id=1, source_target_pairs={{0,8},{8,0},{16,24},{24,16},{1,9},{9,1},{17,25},{25,17},{2,10},{10... | collective-permute-start | bytes 1572872 | tf_op jit(solution)/shard_map/ppermute | solution.py:23
  50.2 12.2 %collective-permute-start.17 = (bf16[64,4096]{1,0:T(8,128)(2,1)S(1)}, bf16[64,4096]{1,0:T(8,128)(2,1)S(1)}, u32[]{:S(2)}, u32[]{:S(2)}) collective-permute-start(bf16[64,4096]{1,0:T(8,128)(2,1)S(1)} %get-tuple-element.78), channel_id=1, source_target_pairs={{0,24},{8,16},{16,8},{24,0},{1,25},{9,17},{17,9},{25,1},{2,26},{10... | collective-permute-start | bytes 1572872 | tf_op jit(solution)/shard_map/ppermute | solution.py:23
  51.2 11.5 %collective-permute-start.15 = (bf16[64,4096]{1,0:T(8,128)(2,1)S(1)}, bf16[64,4096]{1,0:T(8,128)(2,1)S(1)}, u32[]{:S(2)}, u32[]{:S(2)}) collective-permute-start(bf16[64,4096]{1,0:T(8,128)(2,1)S(1)} %get-tuple-element.75), channel_id=1, source_target_pairs={{0,2},{2,0},{4,6},{6,4},{1,3},{3,1},{5,7},{7,5},{8,10},{10,8},{12,... | collective-permute-start | bytes 1572872 | tf_op jit(solution)/shard_map/ppermute | solution.py:23
  52.3 11.3 %collective-permute-start.16 = (bf16[64,4096]{1,0:T(8,128)(2,1)S(1)}, bf16[64,4096]{1,0:T(8,128)(2,1)S(1)}, u32[]{:S(2)}, u32[]{:S(2)}) collective-permute-start(bf16[64,4096]{1,0:T(8,128)(2,1)S(1)} %get-tuple-element.76), channel_id=1, source_target_pairs={{0,6},{2,4},{4,2},{6,0},{1,7},{3,5},{5,3},{7,1},{8,14},{10,12},{12... | collective-permute-start | bytes 1572872 | tf_op jit(solution)/shard_map/ppermute | solution.py:23
  60.3 24.3 %collective-permute-start.22 = (bf16[128,4096]{1,0:T(8,128)(2,1)S(1)}, bf16[128,4096]{1,0:T(8,128)(2,1)S(1)}, u32[]{:S(2)}, u32[]{:S(2)}) collective-permute-start(bf16[128,4096]{1,0:T(8,128)(2,1)S(1)} %add_convert_fusion.2), channel_id=1, source_target_pairs={{0,24},{8,16},{16,8},{24,0},{1,25},{9,17},{17,9},{25,1},{2,26},{10... | collective-permute-start | bytes 3145736 | tf_op jit(solution)/shard_map/ppermute | solution.py:23
  62.6 22.0 %collective-permute-start.21 = (bf16[128,4096]{1,0:T(8,128)(2,1)S(1)}, bf16[128,4096]{1,0:T(8,128)(2,1)S(1)}, u32[]{:S(2)}, u32[]{:S(2)}) collective-permute-start(bf16[128,4096]{1,0:T(8,128)(2,1)S(1)} %add_convert_fusion.3), channel_id=1, source_target_pairs={{0,8},{8,0},{16,24},{24,16},{1,9},{9,1},{17,25},{25,17},{2,10},{10... | collective-permute-start | bytes 3145736 | tf_op jit(solution)/shard_map/ppermute | solution.py:23
  63.8 25.4 %collective-permute-start.20 = (bf16[128,4096]{1,0:T(8,128)(2,1)S(1)}, bf16[128,4096]{1,0:T(8,128)(2,1)S(1)}, u32[]{:S(2)}, u32[]{:S(2)}) collective-permute-start(bf16[128,4096]{1,0:T(8,128)(2,1)S(1)} %add_convert_fusion), channel_id=1, source_target_pairs={{0,6},{2,4},{4,2},{6,0},{1,7},{3,5},{5,3},{7,1},{8,14},{10,12},{12... | collective-permute-start | bytes 3145736 | tf_op jit(solution)/shard_map/ppermute | solution.py:23
  64.3 25.0 %collective-permute-start.19 = (bf16[128,4096]{1,0:T(8,128)(2,1)S(1)}, bf16[128,4096]{1,0:T(8,128)(2,1)S(1)}, u32[]{:S(2)}, u32[]{:S(2)}) collective-permute-start(bf16[128,4096]{1,0:T(8,128)(2,1)S(1)} %add_convert_fusion.1), channel_id=1, source_target_pairs={{0,2},{2,0},{4,6},{6,4},{1,3},{3,1},{5,7},{7,5},{8,10},{10,8},{12,... | collective-permute-start | bytes 3145736 | tf_op jit(solution)/shard_map/ppermute | solution.py:23
  84.9 7.9 %collective-permute-start.27 = (bf16[32,4096]{1,0:T(8,128)(2,1)S(1)}, bf16[32,4096]{1,0:T(8,128)(2,1)S(1)}, u32[]{:S(2)}, u32[]{:S(2)}) collective-permute-start(bf16[32,4096]{1,0:T(8,128)(2,1)S(1)} %get-tuple-element.85), channel_id=1, source_target_pairs={{0,2},{2,0},{4,6},{6,4},{1,3},{3,1},{5,7},{7,5},{8,10},{10,8},{12,... | collective-permute-start | bytes 786440 | tf_op jit(solution)/shard_map/ppermute | solution.py:23
  86.7 11.8 %collective-permute-start.28 = (bf16[32,4096]{1,0:T(8,128)(2,1)S(1)}, bf16[32,4096]{1,0:T(8,128)(2,1)S(1)}, u32[]{:S(2)}, u32[]{:S(2)}) collective-permute-start(bf16[32,4096]{1,0:T(8,128)(2,1)S(1)} %get-tuple-element.86), channel_id=1, source_target_pairs={{0,4},{2,6},{4,0},{6,2},{1,5},{3,7},{5,1},{7,3},{8,12},{10,14},{12... | collective-permute-start | bytes 786440 | tf_op jit(solution)/shard_map/ppermute | solution.py:23
  86.7 11.8 %collective-permute-start.29 = (bf16[32,4096]{1,0:T(8,128)(2,1)S(1)}, bf16[32,4096]{1,0:T(8,128)(2,1)S(1)}, u32[]{:S(2)}, u32[]{:S(2)}) collective-permute-start(bf16[32,4096]{1,0:T(8,128)(2,1)S(1)} %get-tuple-element.87), channel_id=1, source_target_pairs={{0,6},{2,4},{4,2},{6,0},{1,7},{3,5},{5,3},{7,1},{8,14},{10,12},{12... | collective-permute-start | bytes 786440 | tf_op jit(solution)/shard_map/ppermute | solution.py:23
  89.6 19.2 %collective-permute-start.23 = (bf16[32,4096]{1,0:T(8,128)(2,1)S(1)}, bf16[32,4096]{1,0:T(8,128)(2,1)S(1)}, u32[]{:S(2)}, u32[]{:S(2)}) collective-permute-start(bf16[32,4096]{1,0:T(8,128)(2,1)S(1)} %get-tuple-element.91), channel_id=1, source_target_pairs={{0,8},{8,0},{16,24},{24,16},{1,9},{9,1},{17,25},{25,17},{2,10},{10... | collective-permute-start | bytes 786440 | tf_op jit(solution)/shard_map/ppermute | solution.py:23
  89.7 19.1 %collective-permute-start.24 = (bf16[32,4096]{1,0:T(8,128)(2,1)S(1)}, bf16[32,4096]{1,0:T(8,128)(2,1)S(1)}, u32[]{:S(2)}, u32[]{:S(2)}) collective-permute-start(bf16[32,4096]{1,0:T(8,128)(2,1)S(1)} %get-tuple-element.92), channel_id=1, source_target_pairs={{0,16},{8,24},{16,0},{24,8},{1,17},{9,25},{17,1},{25,9},{2,18},{10... | collective-permute-start | bytes 786440 | tf_op jit(solution)/shard_map/ppermute | solution.py:23
  92.8 16.0 %collective-permute-start.25 = (bf16[32,4096]{1,0:T(8,128)(2,1)S(1)}, bf16[32,4096]{1,0:T(8,128)(2,1)S(1)}, u32[]{:S(2)}, u32[]{:S(2)}) collective-permute-start(bf16[32,4096]{1,0:T(8,128)(2,1)S(1)} %get-tuple-element.93), channel_id=1, source_target_pairs={{0,24},{8,16},{16,8},{24,0},{1,25},{9,17},{17,9},{25,1},{2,26},{10... | collective-permute-start | bytes 786440 | tf_op jit(solution)/shard_map/ppermute | solution.py:23
  98.6 13.1 %collective-permute-start.32 = (bf16[16,4096]{1,0:T(8,128)(2,1)S(1)}, bf16[16,4096]{1,0:T(8,128)(2,1)S(1)}, u32[]{:S(2)}, u32[]{:S(2)}) collective-permute-start(bf16[16,4096]{1,0:T(8,128)(2,1)S(1)} %get-tuple-element.101), channel_id=1, source_target_pairs={{0,1},{1,0},{2,3},{3,2},{4,5},{5,4},{6,7},{7,6},{8,9},{9,8},{10,11... | collective-permute-start | bytes 393224 | tf_op jit(solution)/shard_map/ppermute | solution.py:23
  98.7 16.2 %collective-permute-start.31 = (bf16[16,4096]{1,0:T(8,128)(2,1)S(1)}, bf16[16,4096]{1,0:T(8,128)(2,1)S(1)}, u32[]{:S(2)}, u32[]{:S(2)}) collective-permute-start(bf16[16,4096]{1,0:T(8,128)(2,1)S(1)} %get-tuple-element.101), channel_id=1, source_target_pairs={{0,33},{1,32},{32,65},{33,64},{64,97},{65,96},{2,35},{3,34},{34,67... | collective-permute-start | bytes 393224 | tf_op jit(solution)/shard_map/ppermute | solution.py:246
  108.9 6.0 %collective-permute-start.26 = (bf16[16,4096]{1,0:T(8,128)(2,1)S(1)}, bf16[16,4096]{1,0:T(8,128)(2,1)S(1)}, u32[]{:S(2)}, u32[]{:S(2)}) collective-permute-start(bf16[16,4096]{1,0:T(8,128)(2,1)S(1)} %get-tuple-element.95), channel_id=1, source_target_pairs={{0,1},{1,0},{2,3},{3,2},{4,5},{5,4},{6,7},{7,6},{8,9},{9,8},{10,11... | collective-permute-start | bytes 393224 | tf_op jit(solution)/shard_map/ppermute | solution.py:23
  109.0 6.1 %collective-permute-start.30 = (f32[16,4096]{1,0:T(8,128)S(1)}, f32[16,4096]{1,0:T(8,128)S(1)}, u32[]{:S(2)}, u32[]{:S(2)}) collective-permute-start(f32[16,4096]{1,0:T(8,128)S(1)} %get-tuple-element.100), channel_id=1, source_target_pairs={{0,32},{32,64},{64,96},{1,33},{33,65},{65,97},{2,34},{34,66},{66,9... | collective-permute-start | bytes 786440 | tf_op jit(solution)/shard_map/ppermute | solution.py:248
  (11 other events, 66.1 us)

commit v5 on v4

--- a/solution.py
+++ b/solution.py
@@ -33,6 +33,11 @@
 
 def dot_t(a, b):
     return lax.dot_general(a, b, (((1,), (1,)), ((), ())), preferred_element_type=F32)
+
+
+def row_of(block, axis):
+    two, one, three = (swap(block, axis, r) for r in (2, 1, 3))
+    return jnp.concatenate([block, one, two, three], axis=0)
 
 
 def ring_gather(block, axis):
@@ -188,8 +193,8 @@
     other = swap(resid[0], FZ, 1)
     normed = norm(resid[0])
     other = norm(other)
-    plane = jnp.concatenate([normed] + [swap(normed, FX, r) for r in (1, 2, 3)], axis=0)
-    other_plane = jnp.concatenate([other] + [swap(other, FY, r) for r in (1, 2, 3)], axis=0)
+    plane = row_of(normed, FX)
+    other_plane = row_of(other, FY)
     plane = tie(plane, other)[0]
     own_early = ring_gather(plane, FY)
     oth_early = ring_gather(other_plane, FX)
@@ -229,7 +234,7 @@
             sum_kernel, "first_sums", [VMEM] * 3,
             [shape(quarter, width, F32)] + [shape(quarter, width)] * 3, [], 8,
         )(own, *arrived)
-        return rest, sends, [swap(part, axis, r) for r, part in enumerate(sends, 1)]
+        return rest, sends, [swap(sends[r - 1], axis, r) for r in (2, 1, 3)]
 
     def last_sums(rest, arrived):
         return call(

time: 116 us -> 116 us (level)
  waiting for transfers between devices: 39.8 us -> 43.1 us
  starting transfers between devices: 47.9 us -> 44.8 us
    ppermute x31, waiting for transfers between devices: 39.7 us -> 43.1 us  [swap(): return lax.ppermute(value, axis, [(i, i ^ distance) for i in range(count)])]
    ppermute x1, starting transfers between devices: 10 us -> 8.13 us  [body(): passed_oth = lax.ppermute(fwd_oth, ('grp', FZ), crossed)]
    ppermute x31, starting transfers between devices: 35.2 us -> 33.9 us  [swap(): return lax.ppermute(value, axis, [(i, i ^ distance) for i in range(count)])]
where the time goes in v5:
time: 116 us
  starting transfers between devices  44.8 us (39%)
  waiting for transfers between devices  43.1 us (37%)
  Pallas kernels  16.8 us (14%)
  local copies, waits for them, and re-layouts  8.02 us (7%)
  other arithmetic  2.32 us (2%)
    ppermute x31, waiting for transfers between devices, swap(): return lax.ppermute(value, axis, [(i, i ^ distance) for i in range(count)])  43.1 us
    ppermute x31, starting transfers between devices, swap(): return lax.ppermute(value, axis, [(i, i ^ distance) for i in range(count)])  33.9 us
    ppermute x1, starting transfers between devices, body(): passed_oth = lax.ppermute(fwd_oth, ('grp', FZ), crossed)  8.13 us
    unnamed x20, local copies, waits for them, and re-layouts  7.95 us
    pallas_call x1, Pallas kernels, body(): call(functools.partial(near_kernel, rows), 'near_parts', [VMEM] * 5, [sha...  5.15 us
    pallas_call x1, Pallas kernels, body(): call(first_kernel, 'first_units', [VMEM] * 10, [shape(early, features), s...  5.07 us
    pallas_call x1, Pallas kernels, body(): call(functools.partial(far_kernel, rows), 'far_parts', [VMEM] * 12, [shap...  4.62 us
    ppermute x1, starting transfers between devices, body(): passed = lax.ppermute(fwd_own, 'grp', onward)  2.75 us
  transfers between devices with their start and end apart: 33, of which 13 were waited for; matrix products, arithmetic and copies ran while one was open for 1% of the time, Pallas kernels for 10%

profile of v5, /device:TPU:1, one launch (start us, length us, event | category | flops | bytes accessed | tf_op | source)
XLA Modules:
  0.0 116.0 jit_solution(11498442668276599395)
XLA Ops:
  0.6 4.5 %collective-permute-start.3 = (bf16[16,4096]{1,0:T(8,128)(2,1)}, bf16[16,4096]{1,0:T(8,128)(2,1)S(1)}, u32[]{:S(2)}, u32[]{:S(2)}) collective-permute-start(bf16[16,4096]{1,0:T(8,128)(2,1)} %bitcast.23), channel_id=1, source_target_pairs={{0,1},{1,0},{2,3},{3,2},{4,5},{5,4},{6,7},{7,6},{8,9},{9,8},{10,11... | collective-permute-start | bytes 393224 | tf_op jit(solution)/shard_map/ppermute | solution.py:23
  6.9 1.3 %collective-permute-start = (bf16[16,4096]{1,0:T(8,128)(2,1)S(1)}, bf16[16,4096]{1,0:T(8,128)(2,1)S(1)}, u32[]{:S(2)}, u32[]{:S(2)}) collective-permute-start(bf16[16,4096]{1,0:T(8,128)(2,1)S(1)} %norm.2), channel_id=1, source_target_pairs={{0,8},{8,0},{16,24},{24,16},{1,9},{9,1},{17,25},{25,17},{2,10},{10... | collective-permute-start | bytes 393224 | tf_op jit(solution)/shard_map/ppermute | solution.py:23
  8.2 2.5 %collective-permute-start.1 = (bf16[16,4096]{1,0:T(8,128)(2,1)S(1)}, bf16[16,4096]{1,0:T(8,128)(2,1)S(1)}, u32[]{:S(2)}, u32[]{:S(2)}) collective-permute-start(bf16[16,4096]{1,0:T(8,128)(2,1)S(1)} %norm.2), channel_id=1, source_target_pairs={{0,16},{8,24},{16,0},{24,8},{1,17},{9,25},{17,1},{25,9},{2,18},{10... | collective-permute-start | bytes 393224 | tf_op jit(solution)/shard_map/ppermute | solution.py:23
  11.0 2.8 %collective-permute-start.10 = (bf16[16,4096]{1,0:T(8,128)(2,1)S(1)}, bf16[16,4096]{1,0:T(8,128)(2,1)S(1)}, u32[]{:S(2)}, u32[]{:S(2)}) collective-permute-start(bf16[16,4096]{1,0:T(8,128)(2,1)S(1)} %norm.3), channel_id=1, source_target_pairs={{0,6},{2,4},{4,2},{6,0},{1,7},{3,5},{5,3},{7,1},{8,14},{10,12},{12... | collective-permute-start | bytes 393224 | tf_op jit(solution)/shard_map/ppermute | solution.py:23
  13.9 1.3 %collective-permute-start.9 = (bf16[16,4096]{1,0:T(8,128)(2,1)S(1)}, bf16[16,4096]{1,0:T(8,128)(2,1)S(1)}, u32[]{:S(2)}, u32[]{:S(2)}) collective-permute-start(bf16[16,4096]{1,0:T(8,128)(2,1)S(1)} %norm.3), channel_id=1, source_target_pairs={{0,4},{2,6},{4,0},{6,2},{1,5},{3,7},{5,1},{7,3},{8,12},{10,14},{12... | collective-permute-start | bytes 393224 | tf_op jit(solution)/shard_map/ppermute | solution.py:23
  15.8 2.8 %collective-permute-done.2 = bf16[16,4096]{1,0:T(8,128)(2,1)S(1)} collective-permute-done((bf16[16,4096]{1,0:T(8,128)(2,1)S(1)}, bf16[16,4096]{1,0:T(8,128)(2,1)S(1)}, u32[]{:S(2)}, u32[]{:S(2)}) %collective-permute-start.2) | collective-permute-done | bytes 131104 | tf_op jit(solution)/shard_map/ppermute | solution.py:23
  18.6 1.4 %collective-permute-start.4 = (bf16[64,4096]{1,0:T(8,128)(2,1)S(1)}, bf16[64,4096]{1,0:T(8,128)(2,1)S(1)}, u32[]{:S(2)}, u32[]{:S(2)}) collective-permute-start(bf16[64,4096]{1,0:T(8,128)(2,1)S(1)} %pad_maximum_fusion._.refs_0_), channel_id=1, source_target_pairs={{0,2},{2,0},{4,6},{6,4},{1,3},{3,1},{5,7},{7,5},{8,10},{10,8},{12,... | collective-permute-start | bytes 1572872 | tf_op jit(solution)/shard_map/ppermute | solution.py:23
  20.0 1.9 %collective-permute-start.5 = (bf16[64,4096]{1,0:T(8,128)(2,1)S(1)}, bf16[64,4096]{1,0:T(8,128)(2,1)S(1)}, u32[]{:S(2)}, u32[]{:S(2)}) collective-permute-start(bf16[64,4096]{1,0:T(8,128)(2,1)S(1)} %pad_maximum_fusion._.refs_0_), channel_id=1, source_target_pairs={{0,6},{2,4},{4,2},{6,0},{1,7},{3,5},{5,3},{7,1},{8,14},{10,12},{12... | collective-permute-start | bytes 1572872 | tf_op jit(solution)/shard_map/ppermute | solution.py:23
  22.1 1.0 collective-permute-start.12
  23.1 2.2 %copy-done.1 = bf16[1,4096,512]{2,1,0:T(8,128)(2,1)S(1)} copy-done((bf16[1,4096,512]{2,1,0:T(8,128)(2,1)S(1)}, bf16[1,4096,512]{2,1,0:T(8,128)(2,1)}, u32[]{:S(2)}) %copy-start.1) | copy-done | bytes 4194328
  25.3 2.0 %copy-done.2 = bf16[1,4096,448]{1,2,0:T(8,128)(2,1)S(1)} copy-done((bf16[1,4096,448]{1,2,0:T(8,128)(2,1)S(1)}, bf16[1,4096,448]{1,2,0:T(8,128)(2,1)}, u32[]{:S(2)}) %copy-start.2) | copy-done | bytes 3670040
  27.3 2.0 %copy-done.3 = bf16[1,4096,448]{1,2,0:T(8,128)(2,1)S(1)} copy-done((bf16[1,4096,448]{1,2,0:T(8,128)(2,1)S(1)}, bf16[1,4096,448]{1,2,0:T(8,128)(2,1)}, u32[]{:S(2)}) %copy-start.3) | copy-done | bytes 3670040
  30.2 2.2 %collective-permute-done.4.refs_1_ = bf16[64,4096]{1,0:T(8,128)(2,1)S(1)} collective-permute-done((bf16[64,4096]{1,0:T(8,128)(2,1)S(1)}, bf16[64,4096]{1,0:T(8,128)(2,1)S(1)}, u32[]{:S(2)}, u32[]{:S(2)}) %collective-permute-start.4) | collective-permute-done | bytes 524320 | tf_op jit(solution)/shard_map/ppermute | solution.py:23
  33.0 2.0 %collective-permute-start.6 = (bf16[32,4096]{1,0:T(8,128)(2,1)S(1)}, bf16[32,4096]{1,0:T(8,128)(2,1)S(1)}, u32[]{:S(2)}, u32[]{:S(2)}) collective-permute-start(bf16[32,4096]{1,0:T(8,128)(2,1)S(1)} %slice.12), channel_id=1, source_target_pairs={{0,6},{2,4},{4,2},{6,0},{1,7},{3,5},{5,3},{7,1},{8,14},{10,12},{12... | collective-permute-start | bytes 786440 | tf_op jit(solution)/shard_map/ppermute | solution.py:23
  35.2 3.6 %collective-permute-start.13 = (bf16[32,4096]{1,0:T(8,128)(2,1)S(1)}, bf16[32,4096]{1,0:T(8,128)(2,1)S(1)}, u32[]{:S(2)}, u32[]{:S(2)}) collective-permute-start(bf16[32,4096]{1,0:T(8,128)(2,1)S(1)} %slice.14), channel_id=1, source_target_pairs={{0,24},{8,16},{16,8},{24,0},{1,25},{9,17},{17,9},{25,1},{2,26},{10... | collective-permute-start | bytes 786440 | tf_op jit(solution)/shard_map/ppermute | solution.py:23
  38.9 5.1 %first_units.1 = (bf16[384,512]{1,0:T(8,128)(2,1)S(1)}, bf16[384,448]{1,0:T(8,128)(2,1)S(1)}) custom-call(bf16[64,4096]{1,0:T(8,128)(2,1)S(1)} %pad_maximum_fusion._.refs_0_, bf16[64,4096]{1,0:T(8,128)(2,1)S(1)} %collective-permute-done.4.refs_1_, bf16[64,4096]{1,0:T(8,128)(2,1)S(1)} %collective-permute-done.5.refs_2_, ...), custom_call_target="tpu_custom_call" | custom-call | flops 1 | bytes 1 | tf_op jit(solution)/shard_map/first_units/pallas_call | solution.py:214
  44.8 4.6 %far_parts.1 = (bf16[64,4096]{1,0:T(8,128)(2,1)S(1)}, bf16[64,4096]{1,0:T(8,128)(2,1)S(1)}, bf16[64,4096]{1,0:T(8,128)(2,1)S(1)}, bf16[64,4096]{1,0:T(8,128)(2,1...) custom-call(bf16[32,4096]{1,0:T(8,128)(2,1)S(1)} %collective-permute-done.6.refs_0_,, ...), custom_call_target="tpu_custom_call" | custom-call | flops 1 | bytes 1 | tf_op jit(solution)/shard_map/far_parts/pallas_call | solution.py:217
  50.2 1.0 collective-permute-start.17
  51.2 1.2 %collective-permute-start.15 = (bf16[64,4096]{1,0:T(8,128)(2,1)S(1)}, bf16[64,4096]{1,0:T(8,128)(2,1)S(1)}, u32[]{:S(2)}, u32[]{:S(2)}) collective-permute-start(bf16[64,4096]{1,0:T(8,128)(2,1)S(1)} %get-tuple-element.75), channel_id=1, source_target_pairs={{0,2},{2,0},{4,6},{6,4},{1,3},{3,1},{5,7},{7,5},{8,10},{10,8},{12,... | collective-permute-start | bytes 1572872 | tf_op jit(solution)/shard_map/ppermute | solution.py:23
  52.6 5.1 %near_parts.1 = (f32[128,4096]{1,0:T(8,128)S(1)}, f32[128,4096]{1,0:T(8,128)S(1)}, f32[128,4096]{1,0:T(8,128)S(1)}, f32[128,4096]{1,0:T(8,128)S(1)}, f32[128,4096]{1,0:T(8,128)S(1)}, /*index=5*/f32[128,4096]{1,0:T(8,128)S(1)}) custom-call(bf16[512,512]{1,0:T(8,128)(2,1)S(1)} %get-tuple-element.70.feat_x, bf16[512,512]{1,0:T(8,128)(2,1)S(1)} %get-tuple-element.71.feat_y, ...), custom_call_target="tpu_custom_call" | custom-call | flops 1 | bytes 1 | tf_op jit(solution)/shard_map/near_parts/pallas_call | solution.py:223
  57.8 2.3 %collective-permute-done.18 = bf16[64,4096]{1,0:T(8,128)(2,1)S(1)} collective-permute-done((bf16[64,4096]{1,0:T(8,128)(2,1)S(1)}, bf16[64,4096]{1,0:T(8,128)(2,1)S(1)}, u32[]{:S(2)}, u32[]{:S(2)}) %collective-permute-start.18) | collective-permute-done | bytes 524320 | tf_op jit(solution)/shard_map/ppermute | solution.py:23
  60.3 1.7 %collective-permute-start.22 = (bf16[128,4096]{1,0:T(8,128)(2,1)S(1)}, bf16[128,4096]{1,0:T(8,128)(2,1)S(1)}, u32[]{:S(2)}, u32[]{:S(2)}) collective-permute-start(bf16[128,4096]{1,0:T(8,128)(2,1)S(1)} %add_convert_fusion.2), channel_id=1, source_target_pairs={{0,24},{8,16},{16,8},{24,0},{1,25},{9,17},{17,9},{25,1},{2,26},{10... | collective-permute-start | bytes 3145736 | tf_op jit(solution)/shard_map/ppermute | solution.py:23
  64.4 20.2 %collective-permute-done.22.behind = bf16[128,4096]{1,0:T(8,128)(2,1)S(1)} collective-permute-done((bf16[128,4096]{1,0:T(8,128)(2,1)S(1)}, bf16[128,4096]{1,0:T(8,128)(2,1)S(1)}, u32[]{:S(2)}, u32[]{:S(2)}) %collective-permute-start.22) | collective-permute-done | bytes 1048608 | tf_op jit(solution)/shard_map/ppermute | solution.py:23
  84.9 1.2 %collective-permute-start.27 = (bf16[32,4096]{1,0:T(8,128)(2,1)S(1)}, bf16[32,4096]{1,0:T(8,128)(2,1)S(1)}, u32[]{:S(2)}, u32[]{:S(2)}) collective-permute-start(bf16[32,4096]{1,0:T(8,128)(2,1)S(1)} %get-tuple-element.86), channel_id=1, source_target_pairs={{0,4},{2,6},{4,0},{6,2},{1,5},{3,7},{5,1},{7,3},{8,12},{10,14},{12... | collective-permute-start | bytes 786440 | tf_op jit(solution)/shard_map/ppermute | solution.py:23
  86.8 2.3 %collective-permute-start.29 = (bf16[32,4096]{1,0:T(8,128)(2,1)S(1)}, bf16[32,4096]{1,0:T(8,128)(2,1)S(1)}, u32[]{:S(2)}, u32[]{:S(2)}) collective-permute-start(bf16[32,4096]{1,0:T(8,128)(2,1)S(1)} %get-tuple-element.87), channel_id=1, source_target_pairs={{0,6},{2,4},{4,2},{6,0},{1,7},{3,5},{5,3},{7,1},{8,14},{10,12},{12... | collective-permute-start | bytes 786440 | tf_op jit(solution)/shard_map/ppermute | solution.py:23
  89.5 1.0 collective-permute-start.23
  90.4 4.5 %collective-permute-done.27.one = bf16[32,4096]{1,0:T(8,128)(2,1)S(1)} collective-permute-done((bf16[32,4096]{1,0:T(8,128)(2,1)S(1)}, bf16[32,4096]{1,0:T(8,128)(2,1)S(1)}, u32[]{:S(2)}, u32[]{:S(2)}) %collective-permute-start.27) | collective-permute-done | bytes 262176 | tf_op jit(solution)/shard_map/ppermute | solution.py:23
  95.2 3.6 %collective-permute-done.28.two = bf16[32,4096]{1,0:T(8,128)(2,1)S(1)} collective-permute-done((bf16[32,4096]{1,0:T(8,128)(2,1)S(1)}, bf16[32,4096]{1,0:T(8,128)(2,1)S(1)}, u32[]{:S(2)}, u32[]{:S(2)}) %collective-permute-start.28) | collective-permute-done | bytes 262176 | tf_op jit(solution)/shard_map/ppermute | solution.py:23
  98.8 1.1 collective-permute-done.29.three
  100.3 8.1 %collective-permute-start.31 = (bf16[16,4096]{1,0:T(8,128)(2,1)S(1)}, bf16[16,4096]{1,0:T(8,128)(2,1)S(1)}, u32[]{:S(2)}, u32[]{:S(2)}) collective-permute-start(bf16[16,4096]{1,0:T(8,128)(2,1)S(1)} %get-tuple-element.101), channel_id=1, source_target_pairs={{0,33},{1,32},{32,65},{33,64},{64,97},{65,96},{2,35},{3,34},{34,67... | collective-permute-start | bytes 393224 | tf_op jit(solution)/shard_map/ppermute | solution.py:251
  108.6 2.8 %collective-permute-start.30 = (f32[16,4096]{1,0:T(8,128)S(1)}, f32[16,4096]{1,0:T(8,128)S(1)}, u32[]{:S(2)}, u32[]{:S(2)}) collective-permute-start(f32[16,4096]{1,0:T(8,128)S(1)} %get-tuple-element.100), channel_id=1, source_target_pairs={{0,32},{32,64},{64,96},{1,33},{33,65},{65,97},{2,34},{34,66},{66,9... | collective-permute-start | bytes 786440 | tf_op jit(solution)/shard_map/ppermute | solution.py:253
  112.1 3.1 %collective-permute-done.26 = bf16[16,4096]{1,0:T(8,128)(2,1)S(1)} collective-permute-done((bf16[16,4096]{1,0:T(8,128)(2,1)S(1)}, bf16[16,4096]{1,0:T(8,128)(2,1)S(1)}, u32[]{:S(2)}, u32[]{:S(2)}) %collective-permute-start.26) | collective-permute-done | bytes 131104 | tf_op jit(solution)/shard_map/ppermute | solution.py:23
  (77 shorter events, 12.6 us)
Async XLA Ops:
  0.6 10.3 %collective-permute-start.3 = (bf16[16,4096]{1,0:T(8,128)(2,1)}, bf16[16,4096]{1,0:T(8,128)(2,1)S(1)}, u32[]{:S(2)}, u32[]{:S(2)}) collective-permute-start(bf16[16,4096]{1,0:T(8,128)(2,1)} %bitcast.23), channel_id=1, source_target_pairs={{0,1},{1,0},{2,3},{3,2},{4,5},{5,4},{6,7},{7,6},{8,9},{9,8},{10,11... | collective-permute-start | bytes 393224 | tf_op jit(solution)/shard_map/ppermute | solution.py:23
  6.9 6.9 %collective-permute-start = (bf16[16,4096]{1,0:T(8,128)(2,1)S(1)}, bf16[16,4096]{1,0:T(8,128)(2,1)S(1)}, u32[]{:S(2)}, u32[]{:S(2)}) collective-permute-start(bf16[16,4096]{1,0:T(8,128)(2,1)S(1)} %norm.2), channel_id=1, source_target_pairs={{0,8},{8,0},{16,24},{24,16},{1,9},{9,1},{17,25},{25,17},{2,10},{10... | collective-permute-start | bytes 393224 | tf_op jit(solution)/shard_map/ppermute | solution.py:23
  8.2 7.5 %collective-permute-start.1 = (bf16[16,4096]{1,0:T(8,128)(2,1)S(1)}, bf16[16,4096]{1,0:T(8,128)(2,1)S(1)}, u32[]{:S(2)}, u32[]{:S(2)}) collective-permute-start(bf16[16,4096]{1,0:T(8,128)(2,1)S(1)} %norm.2), channel_id=1, source_target_pairs={{0,16},{8,24},{16,0},{24,8},{1,17},{9,25},{17,1},{25,9},{2,18},{10... | collective-permute-start | bytes 393224 | tf_op jit(solution)/shard_map/ppermute | solution.py:23
  10.7 7.9 %collective-permute-start.2 = (bf16[16,4096]{1,0:T(8,128)(2,1)S(1)}, bf16[16,4096]{1,0:T(8,128)(2,1)S(1)}, u32[]{:S(2)}, u32[]{:S(2)}) collective-permute-start(bf16[16,4096]{1,0:T(8,128)(2,1)S(1)} %norm.2), channel_id=1, source_target_pairs={{0,24},{8,16},{16,8},{24,0},{1,25},{9,17},{17,9},{25,1},{2,26},{10... | collective-permute-start | bytes 393224 | tf_op jit(solution)/shard_map/ppermute | solution.py:23
  11.0 10.9 %collective-permute-start.10 = (bf16[16,4096]{1,0:T(8,128)(2,1)S(1)}, bf16[16,4096]{1,0:T(8,128)(2,1)S(1)}, u32[]{:S(2)}, u32[]{:S(2)}) collective-permute-start(bf16[16,4096]{1,0:T(8,128)(2,1)S(1)} %norm.3), channel_id=1, source_target_pairs={{0,6},{2,4},{4,2},{6,0},{1,7},{3,5},{5,3},{7,1},{8,14},{10,12},{12... | collective-permute-start | bytes 393224 | tf_op jit(solution)/shard_map/ppermute | solution.py:23
  13.9 8.1 %collective-permute-start.8 = (bf16[16,4096]{1,0:T(8,128)(2,1)S(1)}, bf16[16,4096]{1,0:T(8,128)(2,1)S(1)}, u32[]{:S(2)}, u32[]{:S(2)}) collective-permute-start(bf16[16,4096]{1,0:T(8,128)(2,1)S(1)} %norm.3), channel_id=1, source_target_pairs={{0,2},{2,0},{4,6},{6,4},{1,3},{3,1},{5,7},{7,5},{8,10},{10,8},{12,... | collective-permute-start | bytes 393224 | tf_op jit(solution)/shard_map/ppermute | solution.py:23
  13.9 8.1 %collective-permute-start.9 = (bf16[16,4096]{1,0:T(8,128)(2,1)S(1)}, bf16[16,4096]{1,0:T(8,128)(2,1)S(1)}, u32[]{:S(2)}, u32[]{:S(2)}) collective-permute-start(bf16[16,4096]{1,0:T(8,128)(2,1)S(1)} %norm.3), channel_id=1, source_target_pairs={{0,4},{2,6},{4,0},{6,2},{1,5},{3,7},{5,1},{7,3},{8,12},{10,14},{12... | collective-permute-start | bytes 393224 | tf_op jit(solution)/shard_map/ppermute | solution.py:23
  18.6 13.8 %collective-permute-start.4 = (bf16[64,4096]{1,0:T(8,128)(2,1)S(1)}, bf16[64,4096]{1,0:T(8,128)(2,1)S(1)}, u32[]{:S(2)}, u32[]{:S(2)}) collective-permute-start(bf16[64,4096]{1,0:T(8,128)(2,1)S(1)} %pad_maximum_fusion._.refs_0_), channel_id=1, source_target_pairs={{0,2},{2,0},{4,6},{6,4},{1,3},{3,1},{5,7},{7,5},{8,10},{10,8},{12,... | collective-permute-start | bytes 1572872 | tf_op jit(solution)/shard_map/ppermute | solution.py:23
  20.0 13.0 %collective-permute-start.5 = (bf16[64,4096]{1,0:T(8,128)(2,1)S(1)}, bf16[64,4096]{1,0:T(8,128)(2,1)S(1)}, u32[]{:S(2)}, u32[]{:S(2)}) collective-permute-start(bf16[64,4096]{1,0:T(8,128)(2,1)S(1)} %pad_maximum_fusion._.refs_0_), channel_id=1, source_target_pairs={{0,6},{2,4},{4,2},{6,0},{1,7},{3,5},{5,3},{7,1},{8,14},{10,12},{12... | collective-permute-start | bytes 1572872 | tf_op jit(solution)/shard_map/ppermute | solution.py:23
  22.0 13.1 %collective-permute-start.11 = (bf16[64,4096]{1,0:T(8,128)(2,1)S(1)}, bf16[64,4096]{1,0:T(8,128)(2,1)S(1)}, u32[]{:S(2)}, u32[]{:S(2)}) collective-permute-start(bf16[64,4096]{1,0:T(8,128)(2,1)S(1)} %pad_maximum_fusion.1.refs_3_), channel_id=1, source_target_pairs={{0,8},{8,0},{16,24},{24,16},{1,9},{9,1},{17,25},{25,17},{2,10},{10... | collective-permute-start | bytes 1572872 | tf_op jit(solution)/shard_map/ppermute | solution.py:23
  22.1 13.1 %collective-permute-start.12 = (bf16[64,4096]{1,0:T(8,128)(2,1)S(1)}, bf16[64,4096]{1,0:T(8,128)(2,1)S(1)}, u32[]{:S(2)}, u32[]{:S(2)}) collective-permute-start(bf16[64,4096]{1,0:T(8,128)(2,1)S(1)} %pad_maximum_fusion.1.refs_3_), channel_id=1, source_target_pairs={{0,24},{8,16},{16,8},{24,0},{1,25},{9,17},{17,9},{25,1},{2,26},{10... | collective-permute-start | bytes 1572872 | tf_op jit(solution)/shard_map/ppermute | solution.py:23
  33.0 11.0 %collective-permute-start.6 = (bf16[32,4096]{1,0:T(8,128)(2,1)S(1)}, bf16[32,4096]{1,0:T(8,128)(2,1)S(1)}, u32[]{:S(2)}, u32[]{:S(2)}) collective-permute-start(bf16[32,4096]{1,0:T(8,128)(2,1)S(1)} %slice.12), channel_id=1, source_target_pairs={{0,6},{2,4},{4,2},{6,0},{1,7},{3,5},{5,3},{7,1},{8,14},{10,12},{12... | collective-permute-start | bytes 786440 | tf_op jit(solution)/shard_map/ppermute | solution.py:23
  35.0 9.0 %collective-permute-start.7 = (bf16[32,4096]{1,0:T(8,128)(2,1)S(1)}, bf16[32,4096]{1,0:T(8,128)(2,1)S(1)}, u32[]{:S(2)}, u32[]{:S(2)}) collective-permute-start(bf16[32,4096]{1,0:T(8,128)(2,1)S(1)} %slice.13), channel_id=1, source_target_pairs={{0,2},{2,0},{4,6},{6,4},{1,3},{3,1},{5,7},{7,5},{8,10},{10,8},{12,... | collective-permute-start | bytes 786440 | tf_op jit(solution)/shard_map/ppermute | solution.py:23
  35.2 8.9 %collective-permute-start.13 = (bf16[32,4096]{1,0:T(8,128)(2,1)S(1)}, bf16[32,4096]{1,0:T(8,128)(2,1)S(1)}, u32[]{:S(2)}, u32[]{:S(2)}) collective-permute-start(bf16[32,4096]{1,0:T(8,128)(2,1)S(1)} %slice.14), channel_id=1, source_target_pairs={{0,24},{8,16},{16,8},{24,0},{1,25},{9,17},{17,9},{25,1},{2,26},{10... | collective-permute-start | bytes 786440 | tf_op jit(solution)/shard_map/ppermute | solution.py:23
  49.4 10.7 %collective-permute-start.18 = (bf16[64,4096]{1,0:T(8,128)(2,1)S(1)}, bf16[64,4096]{1,0:T(8,128)(2,1)S(1)}, u32[]{:S(2)}, u32[]{:S(2)}) collective-permute-start(bf16[64,4096]{1,0:T(8,128)(2,1)S(1)} %get-tuple-element.80), channel_id=1, source_target_pairs={{0,8},{8,0},{16,24},{24,16},{1,9},{9,1},{17,25},{25,17},{2,10},{10... | collective-permute-start | bytes 1572872 | tf_op jit(solution)/shard_map/ppermute | solution.py:23
  50.2 12.2 %collective-permute-start.17 = (bf16[64,4096]{1,0:T(8,128)(2,1)S(1)}, bf16[64,4096]{1,0:T(8,128)(2,1)S(1)}, u32[]{:S(2)}, u32[]{:S(2)}) collective-permute-start(bf16[64,4096]{1,0:T(8,128)(2,1)S(1)} %get-tuple-element.78), channel_id=1, source_target_pairs={{0,24},{8,16},{16,8},{24,0},{1,25},{9,17},{17,9},{25,1},{2,26},{10... | collective-permute-start | bytes 1572872 | tf_op jit(solution)/shard_map/ppermute | solution.py:23
  51.2 11.5 %collective-permute-start.15 = (bf16[64,4096]{1,0:T(8,128)(2,1)S(1)}, bf16[64,4096]{1,0:T(8,128)(2,1)S(1)}, u32[]{:S(2)}, u32[]{:S(2)}) collective-permute-start(bf16[64,4096]{1,0:T(8,128)(2,1)S(1)} %get-tuple-element.75), channel_id=1, source_target_pairs={{0,2},{2,0},{4,6},{6,4},{1,3},{3,1},{5,7},{7,5},{8,10},{10,8},{12,... | collective-permute-start | bytes 1572872 | tf_op jit(solution)/shard_map/ppermute | solution.py:23
  52.3 11.3 %collective-permute-start.16 = (bf16[64,4096]{1,0:T(8,128)(2,1)S(1)}, bf16[64,4096]{1,0:T(8,128)(2,1)S(1)}, u32[]{:S(2)}, u32[]{:S(2)}) collective-permute-start(bf16[64,4096]{1,0:T(8,128)(2,1)S(1)} %get-tuple-element.76), channel_id=1, source_target_pairs={{0,6},{2,4},{4,2},{6,0},{1,7},{3,5},{5,3},{7,1},{8,14},{10,12},{12... | collective-permute-start | bytes 1572872 | tf_op jit(solution)/shard_map/ppermute | solution.py:23
  60.3 24.3 %collective-permute-start.22 = (bf16[128,4096]{1,0:T(8,128)(2,1)S(1)}, bf16[128,4096]{1,0:T(8,128)(2,1)S(1)}, u32[]{:S(2)}, u32[]{:S(2)}) collective-permute-start(bf16[128,4096]{1,0:T(8,128)(2,1)S(1)} %add_convert_fusion.2), channel_id=1, source_target_pairs={{0,24},{8,16},{16,8},{24,0},{1,25},{9,17},{17,9},{25,1},{2,26},{10... | collective-permute-start | bytes 3145736 | tf_op jit(solution)/shard_map/ppermute | solution.py:23
  62.6 22.0 %collective-permute-start.21 = (bf16[128,4096]{1,0:T(8,128)(2,1)S(1)}, bf16[128,4096]{1,0:T(8,128)(2,1)S(1)}, u32[]{:S(2)}, u32[]{:S(2)}) collective-permute-start(bf16[128,4096]{1,0:T(8,128)(2,1)S(1)} %add_convert_fusion.3), channel_id=1, source_target_pairs={{0,8},{8,0},{16,24},{24,16},{1,9},{9,1},{17,25},{25,17},{2,10},{10... | collective-permute-start | bytes 3145736 | tf_op jit(solution)/shard_map/ppermute | solution.py:23
  63.8 25.3 %collective-permute-start.20 = (bf16[128,4096]{1,0:T(8,128)(2,1)S(1)}, bf16[128,4096]{1,0:T(8,128)(2,1)S(1)}, u32[]{:S(2)}, u32[]{:S(2)}) collective-permute-start(bf16[128,4096]{1,0:T(8,128)(2,1)S(1)} %add_convert_fusion), channel_id=1, source_target_pairs={{0,6},{2,4},{4,2},{6,0},{1,7},{3,5},{5,3},{7,1},{8,14},{10,12},{12... | collective-permute-start | bytes 3145736 | tf_op jit(solution)/shard_map/ppermute | solution.py:23
  64.3 24.9 %collective-permute-start.19 = (bf16[128,4096]{1,0:T(8,128)(2,1)S(1)}, bf16[128,4096]{1,0:T(8,128)(2,1)S(1)}, u32[]{:S(2)}, u32[]{:S(2)}) collective-permute-start(bf16[128,4096]{1,0:T(8,128)(2,1)S(1)} %add_convert_fusion.1), channel_id=1, source_target_pairs={{0,2},{2,0},{4,6},{6,4},{1,3},{3,1},{5,7},{7,5},{8,10},{10,8},{12,... | collective-permute-start | bytes 3145736 | tf_op jit(solution)/shard_map/ppermute | solution.py:23
  84.9 10.0 %collective-permute-start.27 = (bf16[32,4096]{1,0:T(8,128)(2,1)S(1)}, bf16[32,4096]{1,0:T(8,128)(2,1)S(1)}, u32[]{:S(2)}, u32[]{:S(2)}) collective-permute-start(bf16[32,4096]{1,0:T(8,128)(2,1)S(1)} %get-tuple-element.86), channel_id=1, source_target_pairs={{0,4},{2,6},{4,0},{6,2},{1,5},{3,7},{5,1},{7,3},{8,12},{10,14},{12... | collective-permute-start | bytes 786440 | tf_op jit(solution)/shard_map/ppermute | solution.py:23
  86.2 12.6 %collective-permute-start.28 = (bf16[32,4096]{1,0:T(8,128)(2,1)S(1)}, bf16[32,4096]{1,0:T(8,128)(2,1)S(1)}, u32[]{:S(2)}, u32[]{:S(2)}) collective-permute-start(bf16[32,4096]{1,0:T(8,128)(2,1)S(1)} %get-tuple-element.85), channel_id=1, source_target_pairs={{0,2},{2,0},{4,6},{6,4},{1,3},{3,1},{5,7},{7,5},{8,10},{10,8},{12,... | collective-permute-start | bytes 786440 | tf_op jit(solution)/shard_map/ppermute | solution.py:23
  86.8 13.1 %collective-permute-start.29 = (bf16[32,4096]{1,0:T(8,128)(2,1)S(1)}, bf16[32,4096]{1,0:T(8,128)(2,1)S(1)}, u32[]{:S(2)}, u32[]{:S(2)}) collective-permute-start(bf16[32,4096]{1,0:T(8,128)(2,1)S(1)} %get-tuple-element.87), channel_id=1, source_target_pairs={{0,6},{2,4},{4,2},{6,0},{1,7},{3,5},{5,3},{7,1},{8,14},{10,12},{12... | collective-permute-start | bytes 786440 | tf_op jit(solution)/shard_map/ppermute | solution.py:23
  89.5 18.9 %collective-permute-start.23 = (bf16[32,4096]{1,0:T(8,128)(2,1)S(1)}, bf16[32,4096]{1,0:T(8,128)(2,1)S(1)}, u32[]{:S(2)}, u32[]{:S(2)}) collective-permute-start(bf16[32,4096]{1,0:T(8,128)(2,1)S(1)} %get-tuple-element.91), channel_id=1, source_target_pairs={{0,16},{8,24},{16,0},{24,8},{1,17},{9,25},{17,1},{25,9},{2,18},{10... | collective-permute-start | bytes 786440 | tf_op jit(solution)/shard_map/ppermute | solution.py:23
  90.4 18.0 %collective-permute-start.24 = (bf16[32,4096]{1,0:T(8,128)(2,1)S(1)}, bf16[32,4096]{1,0:T(8,128)(2,1)S(1)}, u32[]{:S(2)}, u32[]{:S(2)}) collective-permute-start(bf16[32,4096]{1,0:T(8,128)(2,1)S(1)} %get-tuple-element.92), channel_id=1, source_target_pairs={{0,8},{8,0},{16,24},{24,16},{1,9},{9,1},{17,25},{25,17},{2,10},{10... | collective-permute-start | bytes 786440 | tf_op jit(solution)/shard_map/ppermute | solution.py:23
  94.9 13.5 %collective-permute-start.25 = (bf16[32,4096]{1,0:T(8,128)(2,1)S(1)}, bf16[32,4096]{1,0:T(8,128)(2,1)S(1)}, u32[]{:S(2)}, u32[]{:S(2)}) collective-permute-start(bf16[32,4096]{1,0:T(8,128)(2,1)S(1)} %get-tuple-element.93), channel_id=1, source_target_pairs={{0,24},{8,16},{16,8},{24,0},{1,25},{9,17},{17,9},{25,1},{2,26},{10... | collective-permute-start | bytes 786440 | tf_op jit(solution)/shard_map/ppermute | solution.py:23
  100.0 11.4 %collective-permute-start.32 = (bf16[16,4096]{1,0:T(8,128)(2,1)S(1)}, bf16[16,4096]{1,0:T(8,128)(2,1)S(1)}, u32[]{:S(2)}, u32[]{:S(2)}) collective-permute-start(bf16[16,4096]{1,0:T(8,128)(2,1)S(1)} %get-tuple-element.101), channel_id=1, source_target_pairs={{0,1},{1,0},{2,3},{3,2},{4,5},{5,4},{6,7},{7,6},{8,9},{9,8},{10,11... | collective-permute-start | bytes 393224 | tf_op jit(solution)/shard_map/ppermute | solution.py:23
  100.3 14.9 %collective-permute-start.31 = (bf16[16,4096]{1,0:T(8,128)(2,1)S(1)}, bf16[16,4096]{1,0:T(8,128)(2,1)S(1)}, u32[]{:S(2)}, u32[]{:S(2)}) collective-permute-start(bf16[16,4096]{1,0:T(8,128)(2,1)S(1)} %get-tuple-element.101), channel_id=1, source_target_pairs={{0,33},{1,32},{32,65},{33,64},{64,97},{65,96},{2,35},{3,34},{34,67... | collective-permute-start | bytes 393224 | tf_op jit(solution)/shard_map/ppermute | solution.py:251
  108.5 6.6 %collective-permute-start.26 = (bf16[16,4096]{1,0:T(8,128)(2,1)S(1)}, bf16[16,4096]{1,0:T(8,128)(2,1)S(1)}, u32[]{:S(2)}, u32[]{:S(2)}) collective-permute-start(bf16[16,4096]{1,0:T(8,128)(2,1)S(1)} %get-tuple-element.95), channel_id=1, source_target_pairs={{0,1},{1,0},{2,3},{3,2},{4,5},{5,4},{6,7},{7,6},{8,9},{9,8},{10,11... | collective-permute-start | bytes 393224 | tf_op jit(solution)/shard_map/ppermute | solution.py:23
  108.6 6.6 %collective-permute-start.30 = (f32[16,4096]{1,0:T(8,128)S(1)}, f32[16,4096]{1,0:T(8,128)S(1)}, u32[]{:S(2)}, u32[]{:S(2)}) collective-permute-start(f32[16,4096]{1,0:T(8,128)S(1)} %get-tuple-element.100), channel_id=1, source_target_pairs={{0,32},{32,64},{64,96},{1,33},{33,65},{65,97},{2,34},{34,66},{66,9... | collective-permute-start | bytes 786440 | tf_op jit(solution)/shard_map/ppermute | solution.py:253
  (11 other events, 66.3 us)
